TPU v7x, 32 devices: a whole 2x2x4 slice. The times are simulated.
32 devices in a mesh: segment: 2 (over x), skyx: 4 (over z), skyy: 4 (over y, core).
Axes of the slice: x: 2, y: 2, z: 4, core: 2. Of those that a mesh axis runs over, the one named last changes fastest.
Arguments:
- frames: float32 [2, 2048, 2048], P('segment', 'skyx', 'skyy'), may hold values from -6 to 6
- row_shift: int32 [16], P('skyx'), may hold values from -126 to 125, as said below
- row_frac: float32 [2048], P('skyx'), may hold values from 0 to 1
- col_shift: int32 [16], P('skyy'), may hold values from -126 to 125, as said below
- col_frac: float32 [2048], P('skyy'), may hold values from 0 to 1
- profile_cols: bfloat16 [4, 31], replicated, may hold values from -1 to 1
- profile_rows: bfloat16 [8, 31], replicated, may hold values from -1 to 1
- coef_table: float32 [16, 32], replicated, may hold values from -1 to 1
- weight_ids: int32 [16, 16], P('skyx', 'skyy'), may hold values from 0 to 15
Outputs:
- images: float32 [2, 2048, 2048], P('segment', 'skyx', 'skyy')
Inputs may be any that keep to these rules, and one draw needn't show every extreme that they name: `row_shift`: in the first block of every sky tile the shift is at most -64, in the last block of every sky tile at least 64. Both ends of the range occur in every draw. `col_shift`: in the first block of every sky tile the shift is at most -64, in the last block of every sky tile at least 64. Both ends of the range occur in every draw.
All inputs are finite; a program needn't handle non-finite values.
Results may differ from a plain program's by a relative error of at most 0.0033.
Values may be sent and summed in bfloat16 or wider, within the bound.
No kernel may reach another device: no remote copies, remote signals or barrier semaphores. Data moves between devices by JAX's collectives and lax.ppermute only.
A program may use at most 192 MiB of HBM per device.

v0:
```python
import jax
import jax.numpy as jnp
from jax import lax
from jax.sharding import PartitionSpec as P

BLK = 128
MARGIN = 128
KW = 31
NU = 4
NV = 8
HALF = 15


HIGHEST = lax.Precision.HIGHEST


def with_halo(block, sides, width):
    for axis, dim in sides:
        count = lax.axis_size(axis)
        forward = [(i, i + 1) for i in range(count - 1)]
        backward = [(target, source) for source, target in forward]
        low = lax.ppermute(
            lax.slice_in_dim(block, block.shape[dim] - width, None, axis=dim), axis, forward
        )
        high = lax.ppermute(lax.slice_in_dim(block, 0, width, axis=dim), axis, backward)
        block = jnp.concatenate([low, block, high], axis=dim)
    return block


def shifted(block, axis, distance):
    devices = range(lax.axis_size(axis))
    route = [(i - distance, i) for i in devices if i - distance in devices]
    return lax.ppermute(block, axis, route)


def lanczos(values):
    return jnp.where(jnp.abs(values) < 3.0, jnp.sinc(values) * jnp.sinc(values / 3.0), 0.0)


def dense_warp(shifts, fractions, wide_side):
    tile_side = fractions.shape[0]
    outputs = jnp.arange(tile_side, dtype=jnp.int32)
    sources = jnp.arange(wide_side, dtype=jnp.int32)
    block_shift = jnp.repeat(shifts, BLK)
    lag_int = sources[None, :] - MARGIN - outputs[:, None] - block_shift[:, None]
    inside = (lag_int >= -2) & (lag_int <= 3)
    values = lanczos(lag_int.astype(jnp.float32) - fractions[:, None])
    return jnp.where(inside, values, 0.0)


def banded_profiles(profiles, long_side, short_side, long_first):
    if long_first:
        lag_grid = (
            jnp.arange(long_side, dtype=jnp.int32)[:, None]
            - jnp.arange(short_side, dtype=jnp.int32)[None, :]
        )
    else:
        lag_grid = (
            jnp.arange(long_side, dtype=jnp.int32)[None, :]
            - jnp.arange(short_side, dtype=jnp.int32)[:, None]
        )
    profile_f = profiles.astype(jnp.float32)
    banded = jnp.zeros((profiles.shape[0],) + lag_grid.shape, jnp.float32)
    for tap in range(KW):
        banded = banded + jnp.where(lag_grid[None] == tap, profile_f[:, tap][:, None, None], 0.0)
    return banded.astype(profiles.dtype)


def subtract(padded, science, profile_cols, profile_rows, coef_table, weight_ids):
    tile_side = science.shape[0]
    long_side = tile_side + 2 * HALF
    blocks = tile_side // BLK
    col_band = banded_profiles(profile_cols, long_side, tile_side, True)
    row_band = banded_profiles(profile_rows, long_side, tile_side, False).reshape(
        NV * tile_side, long_side
    )
    onehot_ids = (weight_ids[:, :, None] == jnp.arange(coef_table.shape[0])[None, None, :]).astype(
        jnp.float32
    )
    factors = jnp.einsum("ics,sk->ick", onehot_ids, coef_table, precision=HIGHEST)
    total_sum = jnp.zeros((blocks, BLK, blocks, BLK), jnp.float32)
    for prof_col in range(NU):
        passed = jnp.dot(padded, col_band[prof_col], preferred_element_type=jnp.float32).astype(
            jnp.bfloat16
        )
        basis_all = jnp.dot(row_band, passed, preferred_element_type=jnp.float32)
        basis_all = basis_all.reshape(NV, blocks, BLK, blocks, BLK)
        for prof_row in range(NV):
            factor = factors[:, None, :, None, prof_col * NV + prof_row]
            total_sum = total_sum + basis_all[prof_row] * factor
    return science - total_sum.reshape(tile_side, tile_side)


def local(
    frames,
    row_shift,
    row_frac,
    col_shift,
    col_frac,
    profile_cols,
    profile_rows,
    coef_table,
    weight_ids,
):
    frame_tile = frames[0]
    tile_side = frame_tile.shape[0]
    wide_side = tile_side + 2 * MARGIN
    is_warper = lax.axis_index("segment") == 0
    row_weights = dense_warp(row_shift, row_frac, wide_side)
    col_weights = dense_warp(col_shift, col_frac, wide_side)
    extended = with_halo(frame_tile, (("skyx", 0), ("skyy", 1)), MARGIN)
    rows_warped = lax.cond(
        is_warper,
        lambda: jnp.dot(row_weights, extended, precision=HIGHEST),
        lambda: jnp.zeros((tile_side, wide_side), jnp.float32),
    )
    warped = lax.cond(
        is_warper,
        lambda: jnp.dot(rows_warped, col_weights.T, precision=HIGHEST).astype(jnp.bfloat16),
        lambda: jnp.zeros((tile_side, tile_side), jnp.bfloat16),
    )
    arrived = shifted(warped, "segment", 1)
    padded = with_halo(arrived, (("skyx", 0), ("skyy", 1)), HALF)
    result = lax.cond(
        is_warper,
        lambda: warped.astype(jnp.float32),
        lambda: subtract(padded, frame_tile, profile_cols, profile_rows, coef_table, weight_ids),
    )
    return result[None]


def solution(mesh):
    placed = (
        P("segment", "skyx", "skyy"),
        P("skyx"),
        P("skyx"),
        P("skyy"),
        P("skyy"),
        P(),
        P(),
        P(),
        P("skyx", "skyy"),
    )
    return jax.shard_map(
        local, mesh=mesh, in_specs=placed, out_specs=P("segment", "skyx", "skyy"), check_vma=False
    )
```

profile of v0, /device:TPU:14, one launch (start us, length us, event | category | flops | bytes accessed | tf_op | source)
XLA Modules:
  0.0 458.3 jit_solution(3159991474148897095)
XLA Ops:
  1.1 3.5 collective-permute-start
  7.7 10.1 %fusion.154 = (f32[512,768]{1,0:T(8,128)S(1)}, f32[512,768]{1,0:T(8,128)S(1)}, f32[512,768]{1,0:T(8,128)}, f32[512,768]{1,0:T(8,128)}, f32[512,768]{1,0:T(8,128)...) fusion(f32[512]{0:T(512)} %param.20, ...), kind=kLoop, calls=%fused_computation.376 | loop fusion | flops 47579136 | bytes 22031360 | tf_op jit(solution)/shard_map/jit(sinc)/div | solution.py:37
  20.8 3.6 collective-permute-start.3
  42.9 37.4 %collective-permute-done.4 = bf16[512,512]{1,0:T(8,128)(2,1)S(1)} collective-permute-done((bf16[512,512]{1,0:T(8,128)(2,1)}, bf16[512,512]{1,0:T(8,128)(2,1)S(1)}, u32[]{:S(2)}, u32[]{:S(2)}) %collective-permute-start.4) | collective-permute-done | bytes 524320 | tf_op jit(solution)/shard_map/ppermute | solution.py:33
  80.2 3.5 collective-permute-start.5
  86.1 3.2 collective-permute-done.6
  91.4 3.6 collective-permute-start.8
  99.0 358.0 %conditional.5 = (f32[1,512,512]{2,1,0:T(8,128)}) conditional(s32[]{:T(128)} %convert_element_type.48, (bf16[8,31]{1,0:T(8,128)(2,1)S(1)}, bf16[4,31]{1,0:T(4,128)(2,1)S(1)}, bf16[542,542]{1,0:T(8,128)(2,1)}, s32[4,4]{1,0:T(4,128)S(1)}, f32[16,32]{1,0:T(8,128)S(1)}, /*index=5*/f32[512,512]{1,0:T(8,128)}) %tuple.227, ...), branch_computations={%region_4.6_spmd, %region_5.7_spmd} | conditional | flops 10551205888 | bytes 700141696 | solution.py:124
  106.4 3.2 copy.39
  111.4 3.2 copy.41
  116.9 3.2 copy.43
  121.9 3.2 copy.45
  127.0 3.1 copy.47
  132.2 3.2 copy.49
  137.2 3.1 copy.51
  142.3 3.1 copy.53
  147.5 3.2 copy.55
  157.5 3.1 copy.59
  162.6 3.5 copy.61
  168.0 3.2 copy.63
  173.0 3.1 copy.65
  178.0 3.3 copy.67
  183.2 3.1 copy.69
  188.2 3.2 copy.71
  193.3 3.2 copy.73
  198.6 3.2 copy.75
  203.7 3.2 copy.77
  208.7 3.1 copy.79
  214.1 3.1 copy.81
  219.2 3.1 copy.83
  224.2 3.2 copy.85
  229.4 3.1 copy.87
  234.4 3.2 copy.89
  239.5 3.1 copy.91
  244.5 3.4 copy.31
  249.7 3.2 copy.33
  254.8 3.1 copy.35
  257.9 43.2 %add_convert_fusion = bf16[4096,542]{0,1:T(8,128)(2,1)} fusion(pred[4096,542]{0,1:T(8,128)(4,1)} %bitcast.733, pred[4096,542]{0,1:T(8,128)(4,1)} %bitcast.732, pred[4096,542]{0,1:T(8,128)(4,1)} %bitcast.731, pred[4096,542]{0,1:T(8,128)(4,1)} %bitcast.730, pred[4096,542]{0,1:T(8,128)(4,1)} %bitcast.729, pred[4096,542]{0,1:T(8,128)(4,1)} %bitcast.728, ...), kind=kLoop, calls=%fused_computation.37 | loop fusion | flops 137641984 | bytes 73768960 | tf_op jit(solution)/shard_map/cond/branch_0_fun/convert_element_type | solution.py:66
  315.6 16.7 %add_convert_fusion.1 = bf16[4,542,512]{2,1,0:T(8,128)(2,1)S(1)} fusion(f32[4]{0:T(128)S(1)} %get-tuple-element.348, f32[4]{0:T(128)S(1)} %get-tuple-element.349, f32[4]{0:T(128)S(1)} %get-tuple-element.350, f32[4]{0:T(128)S(1)} %get-tuple-element.351, f32[4]{0:T(128)S(1)} %get-tuple-element.352, f32[4]{0:T(128)S(1)} %get-tuple-element.353, ...), kind=kLoop, calls=%fused_computation.38 | loop fusion | flops 68820992 | bytes 10823152 | tf_op jit(solution)/shard_map/cond/branch_0_fun/convert_element_type | solution.py:66
  332.3 10.5 %fusion.132 = f32[4096,512]{1,0:T(8,128)} fusion(bf16[4096,542]{0,1:T(8,128)(2,1)} %add_convert_fusion, bf16[542,542]{1,0:T(8,128)(2,1)} %get-tuple-element.94, bf16[4,542,512]{2,1,0:T(8,128)(2,1)S(1)} %add_convert_fusion.1), kind=kOutput, calls=%fused_computation.203 | convolution fusion | flops 2574404608 | bytes 13973256 | tf_op jit(solution)/shard_map/cond/branch_0_fun/dot_general | solution.py:86
  344.4 6.6 %fusion.173 = (f32[512,512]{1,0:T(8,128)S(1)}, f32[512,512]{1,0:T(8,128)S(1)}, f32[512,512]{1,0:T(8,128)}, f32[512,512]{1,0:T(8,128)}) fusion(f32[4096,512]{1,0:T(8,128)} %fusion.132, f32[64,8,4,128]{3,2,1,0:T(4,128)S(1)} %bitcast.794, f32[64,8,4,128]{3,2,1,0:T(4,128)S(1)} %bitcast.793, f32[64,8,4,128]{3,2,1,0:T(4,128)S(1)} %bitcast.792, ...), kind=kLoop, calls=%fused_computation.434 | loop fusion | flops 2359296 | bytes 17825792 | tf_op jit(solution)/shard_map/cond/branch_0_fun/slice | solution.py:90
  351.0 9.8 %fusion.133 = f32[4096,512]{1,0:T(8,128)} fusion(bf16[4096,542]{0,1:T(8,128)(2,1)} %add_convert_fusion, bf16[542,542]{1,0:T(8,128)(2,1)S(1)} %copy-done.8, bf16[4,542,512]{2,1,0:T(8,128)(2,1)} %copy-done.3), kind=kOutput, calls=%fused_computation.204 | convolution fusion | flops 2574404608 | bytes 13989640 | tf_op jit(solution)/shard_map/cond/branch_0_fun/dot_general | solution.py:86
  360.8 6.9 %fusion.174 = (f32[512,512]{1,0:T(8,128)}, f32[512,512]{1,0:T(8,128)}, f32[512,512]{1,0:T(8,128)}, f32[512,512]{1,0:T(8,128)}, f32[512,512]{1,0:T(8,128)}, /*ind...) fusion(f32[4096,512]{1,0:T(8,128)} %fusion.133), kind=kLoop, calls=%fused_computation.435 | loop fusion | bytes 16777216 | tf_op jit(solution)/shard_map/cond/branch_0_fun/slice | solution.py:90
  367.7 9.6 %fusion.134 = f32[4096,512]{1,0:T(8,128)} fusion(bf16[4096,542]{0,1:T(8,128)(2,1)} %add_convert_fusion, bf16[542,542]{1,0:T(8,128)(2,1)S(1)} %copy-done.8, bf16[4,542,512]{2,1,0:T(8,128)(2,1)} %copy-done.3), kind=kOutput, calls=%fused_computation.205 | convolution fusion | flops 2574404608 | bytes 13989640 | tf_op jit(solution)/shard_map/cond/branch_0_fun/dot_general | solution.py:86
  377.3 6.9 %fusion.175 = (f32[512,512]{1,0:T(8,128)}, f32[512,512]{1,0:T(8,128)}, f32[512,512]{1,0:T(8,128)}, f32[512,512]{1,0:T(8,128)}, f32[512,512]{1,0:T(8,128)}, /*ind...) fusion(f32[4096,512]{1,0:T(8,128)} %fusion.134), kind=kLoop, calls=%fused_computation.436 | loop fusion | bytes 16777216 | tf_op jit(solution)/shard_map/cond/branch_0_fun/slice | solution.py:90
  384.1 9.6 %fusion.135 = f32[4096,512]{1,0:T(8,128)} fusion(bf16[4096,542]{0,1:T(8,128)(2,1)} %add_convert_fusion, bf16[542,542]{1,0:T(8,128)(2,1)S(1)} %copy-done.8, bf16[4,542,512]{2,1,0:T(8,128)(2,1)} %copy-done.3), kind=kOutput, calls=%fused_computation.206 | convolution fusion | flops 2574404608 | bytes 13989640 | tf_op jit(solution)/shard_map/cond/branch_0_fun/dot_general | solution.py:86
  393.8 7.1 %fusion.176 = (f32[512,512]{1,0:T(8,128)}, f32[512,512]{1,0:T(8,128)}, f32[512,512]{1,0:T(8,128)}, f32[512,512]{1,0:T(8,128)}, f32[512,512]{1,0:T(8,128)}, /*ind...) fusion(f32[4096,512]{1,0:T(8,128)} %fusion.135), kind=kLoop, calls=%fused_computation.437 | loop fusion | bytes 16777216 | tf_op jit(solution)/shard_map/cond/branch_0_fun/slice | solution.py:90
  433.8 22.9 %fusion.101 = f32[1,512,512]{2,1,0:T(8,128)} fusion(f32[512,512]{1,0:T(8,128)S(1)} %copy-done.2, f32[512,512]{1,0:T(8,128)} %get-tuple-element.340, f32[64,8,4,128]{3,2,1,0:T(4,128)} %bitcast.785, f32[512,512]{1,0:T(8,128)} %get-tuple-element.341, f32[64,8,4,128]{3,2,1,0:T(4,128)} %bitcast.784, f32[512,512]{1,0:T(8,128)} %get-tuple-element.342, ...), kind=kLoop, calls=%fused_computation.141 | loop fusion | flops 14417920 | bytes 59768832 | tf_op jit(solution)/shard_map/broadcast_in_dim | solution.py:129
  (267 shorter events, 150.5 us)
Async XLA Ops:
  1.1 16.7 %collective-permute-start = (f32[128,512]{1,0:T(8,128)S(1)}, f32[128,512]{1,0:T(8,128)S(1)}, u32[]{:S(2)}, u32[]{:S(2)}) collective-permute-start(f32[128,512]{1,0:T(8,128)S(1)} %get-tuple-element.471), channel_id=1, source_target_pairs={{0,4},{4,8},{8,12},{1,5},{5,9},{9,13},{2,6},{6,10},{10,14},{3,7},{... | collective-permute-start | bytes 786440 | tf_op jit(solution)/shard_map/ppermute | solution.py:22
  4.6 13.3 %collective-permute-start.1 = (f32[128,512]{1,0:T(8,128)S(1)}, f32[128,512]{1,0:T(8,128)S(1)}, u32[]{:S(2)}, u32[]{:S(2)}) collective-permute-start(f32[128,512]{1,0:T(8,128)S(1)} %get-tuple-element.472), channel_id=1, source_target_pairs={{4,0},{8,4},{12,8},{5,1},{9,5},{13,9},{6,2},{10,6},{14,10},{7,3},{... | collective-permute-start | bytes 786440 | tf_op jit(solution)/shard_map/ppermute | solution.py:25
  7.7 10.1 %copy-start = (f32[1,512,512]{2,1,0:T(8,128)S(1)}, f32[1,512,512]{2,1,0:T(8,128)}, u32[]{:S(2)}) copy-start(f32[1,512,512]{2,1,0:T(8,128)} %param.16) | copy-start | bytes 3145732
  17.8 6.7 %copy-start.9 = (f32[512]{0:T(512)S(1)}, f32[512]{0:T(512)}, u32[]{:S(2)}) copy-start(f32[512]{0:T(512)} %param.20) | copy-start | bytes 6148
  17.8 6.7 %copy-start.10 = (f32[512]{0:T(512)S(1)}, f32[512]{0:T(512)}, u32[]{:S(2)}) copy-start(f32[512]{0:T(512)} %param.18) | copy-start | bytes 6148
  17.8 9.1 %copy-start.4 = (f32[128,512]{1,0:T(8,128)}, f32[128,512]{1,0:T(8,128)S(1)}, u32[]{:S(2)}) copy-start(f32[128,512]{1,0:T(8,128)S(1)} %collective-permute-done) | copy-start | bytes 786436
  17.8 9.1 %copy-start.6 = (f32[128,512]{1,0:T(8,128)}, f32[128,512]{1,0:T(8,128)S(1)}, u32[]{:S(2)}) copy-start(f32[128,512]{1,0:T(8,128)S(1)} %collective-permute-done.1) | copy-start | bytes 786436
  18.9 10.1 %collective-permute-start.2 = (f32[768,128]{1,0:T(8,128)}, f32[768,128]{1,0:T(8,128)}, u32[]{:S(2)}, u32[]{:S(2)}) collective-permute-start(f32[768,128]{1,0:T(8,128)} %get-tuple-element.469), channel_id=1, source_target_pairs={{0,1},{1,2},{2,3},{4,5},{5,6},{6,7},{8,9},{9,10},{10,11},{12,13},{... | collective-permute-start | bytes 1179656 | tf_op jit(solution)/shard_map/ppermute | solution.py:22
  20.8 9.2 %collective-permute-start.3 = (f32[768,128]{1,0:T(8,128)}, f32[768,128]{1,0:T(8,128)}, u32[]{:S(2)}, u32[]{:S(2)}) collective-permute-start(f32[768,128]{1,0:T(8,128)} %get-tuple-element.470), channel_id=1, source_target_pairs={{1,0},{2,1},{3,2},{5,4},{6,5},{7,6},{9,8},{10,9},{11,10},{13,12},{... | collective-permute-start | bytes 1179656 | tf_op jit(solution)/shard_map/ppermute | solution.py:25
  26.9 3.1 copy-start.1
  26.9 3.1 copy-start.5
  27.0 3.1 copy-start.7
  41.4 57.6 %copy-start.11 = (bf16[8,31]{1,0:T(8,128)(2,1)S(1)}, bf16[8,31]{1,0:T(8,128)(2,1)}, u32[]{:S(2)}) copy-start(bf16[8,31]{1,0:T(8,128)(2,1)} %param.22) | copy-start | bytes 1492
  41.4 57.6 %copy-start.12 = (bf16[4,31]{1,0:T(4,128)(2,1)S(1)}, bf16[4,31]{1,0:T(4,128)(2,1)}, u32[]{:S(2)}) copy-start(bf16[4,31]{1,0:T(4,128)(2,1)} %param.21) | copy-start | bytes 748
  41.4 57.6 %copy-start.13 = (f32[16,32]{1,0:T(8,128)S(1)}, f32[16,32]{1,0:T(8,128)}, u32[]{:S(2)}) copy-start(f32[16,32]{1,0:T(8,128)} %param.23) | copy-start | bytes 6148
  41.4 57.6 %copy-start.14 = (s32[4,4]{1,0:T(4,128)S(1)}, s32[4,4]{1,0:T(4,128)}, u32[]{:S(2)}) copy-start(s32[4,4]{1,0:T(4,128)} %param.24) | copy-start | bytes 196
  41.4 38.8 %collective-permute-start.4 = (bf16[512,512]{1,0:T(8,128)(2,1)}, bf16[512,512]{1,0:T(8,128)(2,1)S(1)}, u32[]{:S(2)}, u32[]{:S(2)}) collective-permute-start(bf16[512,512]{1,0:T(8,128)(2,1)} %get-tuple-element.184), channel_id=1, source_target_pairs={{0,16},{1,17},{2,18},{3,19},{4,20},{5,21},{6,22},{7,23},{8,24},{9,... | collective-permute-start | bytes 1572872 | tf_op jit(solution)/shard_map/ppermute | solution.py:33
  80.2 5.9 %collective-permute-start.5 = (bf16[15,512]{1,0:T(8,128)(2,1)S(1)}, bf16[15,512]{1,0:T(8,128)(2,1)S(1)}, u32[]{:S(2)}, u32[]{:S(2)}) collective-permute-start(bf16[15,512]{1,0:T(8,128)(2,1)S(1)} %get-tuple-element.475), channel_id=1, source_target_pairs={{0,4},{4,8},{8,12},{1,5},{5,9},{9,13},{2,6},{6,10},{10,14},{3,7},{... | collective-permute-start | bytes 46088 | tf_op jit(solution)/shard_map/ppermute | solution.py:22
  83.7 5.6 %collective-permute-start.6 = (bf16[15,512]{1,0:T(8,128)(2,1)S(1)}, bf16[15,512]{1,0:T(8,128)(2,1)S(1)}, u32[]{:S(2)}, u32[]{:S(2)}) collective-permute-start(bf16[15,512]{1,0:T(8,128)(2,1)S(1)} %get-tuple-element.476), channel_id=1, source_target_pairs={{4,0},{8,4},{12,8},{5,1},{9,5},{13,9},{6,2},{10,6},{14,10},{7,3},{... | collective-permute-start | bytes 46088 | tf_op jit(solution)/shard_map/ppermute | solution.py:25
  89.5 6.4 %collective-permute-start.7 = (bf16[542,15]{1,0:T(8,128)(2,1)S(1)}, bf16[542,15]{1,0:T(8,128)(2,1)S(1)}, u32[]{:S(2)}, u32[]{:S(2)}) collective-permute-start(bf16[542,15]{1,0:T(8,128)(2,1)S(1)} %get-tuple-element.473), channel_id=1, source_target_pairs={{0,1},{1,2},{2,3},{4,5},{5,6},{6,7},{8,9},{9,10},{10,11},{12,13},{... | collective-permute-start | bytes 48788 | tf_op jit(solution)/shard_map/ppermute | solution.py:22
  91.4 6.2 %collective-permute-start.8 = (bf16[542,15]{1,0:T(8,128)(2,1)S(1)}, bf16[542,15]{1,0:T(8,128)(2,1)S(1)}, u32[]{:S(2)}, u32[]{:S(2)}) collective-permute-start(bf16[542,15]{1,0:T(8,128)(2,1)S(1)} %get-tuple-element.474), channel_id=1, source_target_pairs={{1,0},{2,1},{3,2},{5,4},{6,5},{7,6},{9,8},{10,9},{11,10},{13,12},{... | collective-permute-start | bytes 48788 | tf_op jit(solution)/shard_map/ppermute | solution.py:25
  332.3 10.5 %copy-start.3 = (bf16[4,542,512]{2,1,0:T(8,128)(2,1)}, bf16[4,542,512]{2,1,0:T(8,128)(2,1)S(1)}, u32[]{:S(2)}) copy-start(bf16[4,542,512]{2,1,0:T(8,128)(2,1)S(1)} %add_convert_fusion.1) | copy-start | bytes 6660100 | tf_op jit(solution)/shard_map/cond
  344.3 6.6 %copy-start.8 = (bf16[542,542]{1,0:T(8,128)(2,1)S(1)}, bf16[542,542]{1,0:T(8,128)(2,1)}, u32[]{:S(2)}) copy-start(bf16[542,542]{1,0:T(8,128)(2,1)} %get-tuple-element.94) | copy-start | bytes 1762588 | tf_op jit(solution)/shard_map/cond
  430.2 3.6 copy-start.2
where the time goes:
time: 467 us; the launch traced here: 458 us
  local copies, waits for them, and re-layouts  220 us (47%)
  other arithmetic  127 us (27%)
  waiting for transfers between devices  44.3 us (9%)
  matrix products  39.8 us (9%)
  starting transfers between devices  24.2 us (5%)
    cond x151, local copies, waits for them, and re-layouts  160 us
    convert_element_type x2, other arithmetic, banded_profiles(): return banded.astype(profiles.dtype)  60 us
    dot_general x4, matrix products, subtract(): basis_all = jnp.dot(row_band, passed, preferred_element_type=jnp.float32)  39.5 us
    ppermute x1, waiting for transfers between devices, shifted(): return lax.ppermute(block, axis, route)  37.4 us
    mul x32, local copies, waits for them, and re-layouts, subtract(): total_sum = total_sum + basis_all[prof_row] * factor  28.3 us
    broadcast_in_dim x1, other arithmetic, local(): return result[None]  22.9 us
    slice x3, local copies, waits for them, and re-layouts, subtract(): total_sum = total_sum + basis_all[prof_row] * factor  20.8 us
    eq x47, other arithmetic, banded_profiles(): lag_grid[None] == tap  17.5 us
  transfers between devices with their start and end apart: 9, of which 5 were waited for; matrix products, arithmetic and copies ran while one was open for 3% of the time, Pallas kernels for 0%

commit v1 on v0

v1 whole, which is shorter than its diff:
```python
import functools
import math

import jax
import jax.numpy as jnp
from jax import lax
from jax.experimental import pallas as pl
from jax.experimental.pallas import tpu as pltpu
from jax.sharding import PartitionSpec as P

BLK = 128
KW = 31
HALF = 15
ROW0 = 48
F32 = jnp.float32
BF16 = jnp.bfloat16
HIGHEST = lax.Precision.HIGHEST
VM = pl.BlockSpec(memory_space=pltpu.VMEM)
HBM = pl.BlockSpec(memory_space=pl.ANY)
SM = pl.BlockSpec(memory_space=pltpu.SMEM)


def moved(block, step, sources):
    axes = ("segment", "skyx", "skyy")
    counts = [lax.axis_size(axis) for axis in axes]
    route = []
    for s in range(counts[0]):
        for i in range(counts[1]):
            for j in range(counts[2]):
                to = (s + step[0], i + step[1], j + step[2])
                if s in sources and all(0 <= to[k] < counts[k] for k in range(3)):
                    flat = [(a * counts[1] + b) * counts[2] + c for a, b, c in ((s, i, j), to)]
                    route.append(tuple(flat))
    return lax.ppermute(block, axes, route)


def sinc(values):
    angle = math.pi * values
    zero = values == 0.0
    return jnp.where(zero, 1.0, jnp.sin(angle) / jnp.where(zero, 1.0, angle))


def taps(frac):
    lag = lax.broadcasted_iota(jnp.int32, (8, BLK), 0) - 2
    values = lag.astype(F32) - frac
    weight = jnp.where(jnp.abs(values) < 3.0, sinc(values) * sinc(values / 3.0), 0.0)
    return jnp.where(lag <= 3, weight, 0.0)


def split(values):
    high = values.astype(BF16)
    return high, (values - high.astype(F32)).astype(BF16)


def banded(weight, shift, depth, offset):
    lag = (
        lax.broadcasted_iota(jnp.int32, (depth, BLK), 0)
        - lax.broadcasted_iota(jnp.int32, (depth, BLK), 1)
        + offset
        - shift.astype(jnp.int32)
    )
    total = jnp.zeros((depth, BLK), F32)
    for tap in range(6):
        total = jnp.where(lag == tap - 2, weight[tap : tap + 1], total)
    return total


def dot3(left, right, dims):
    lh, ll = left
    rh, rl = right
    dot = functools.partial(
        lax.dot_general, dimension_numbers=(dims, ((), ())), preferred_element_type=F32
    )
    return dot(lh, rh) + dot(lh, rl) + dot(ll, rh)


def prepare_kernel(
    nb, nu, nv, nx, ny,
    frame, left, right, meta, meta_up, meta_down, prof_cols, prof_rows, table, ids,
    own, across, to_up, to_down, side_up, side_down, kernels_out, band_out,
    src_hi, src_lo, row_hi, row_lo, kernels, band, coefs, sem,
):
    side = nb * BLK
    warper = lax.axis_index("segment") == 0
    i = lax.axis_index("skyx")
    j = lax.axis_index("skyy")

    @pl.when(warper)
    def _():
        for part, lane in ((left, 0), (frame, BLK), (right, BLK + side)):
            width = part.shape[1]
            hi, lo = split(part[0:side, :])
            src_hi[:, lane : lane + width] = hi
            src_lo[:, lane : lane + width] = lo
        lanes = lax.broadcasted_iota(jnp.int32, (1, BLK), 1)
        for b in range(nb):
            first = 0 if b == 0 else b
            count = 2 if b in (0, nb - 1) else 3
            if b == nb - 1:
                first = nb
            depth = count * BLK
            weight = taps(meta[2 * nb + b : 2 * nb + b + 1, :])
            shift = meta[3 * nb + b : 3 * nb + b + 1, :]
            mat = split(banded(weight, shift, depth, (first - 1 - b) * BLK))
            cols = slice(first * BLK, first * BLK + depth)
            hi, lo = split(dot3((src_hi[:, cols], src_lo[:, cols]), mat, ((1,), (0,))))
            row_hi[:, b * BLK : (b + 1) * BLK] = hi
            row_lo[:, b * BLK : (b + 1) * BLK] = lo
        low_ok = jnp.logical_and(lanes >= BLK - HALF, j > 0)
        high_ok = jnp.logical_and(lanes < HALF, j < ny - 1)
        low = split(jnp.where(low_ok, banded(taps(left[side : side + 1, :]), left[side + 1 : side + 2, :], BLK, BLK), 0.0))
        high = split(jnp.where(high_ok, banded(taps(right[side : side + 1, :]), right[side + 1 : side + 2, :], BLK, -BLK), 0.0))
        hi, lo = split(
            dot3((src_hi[:, BLK : 2 * BLK], src_lo[:, BLK : 2 * BLK]), low, ((1,), (0,)))
            + dot3((src_hi[:, side : side + BLK], src_lo[:, side : side + BLK]), high, ((1,), (0,)))
        )
        row_hi[:, side : side + BLK] = hi
        row_lo[:, side : side + BLK] = lo
        for b in range(-1, nb + 1):
            if b == -1:
                first, count = 0, 1
                weight = jnp.where(i > 0, taps(meta_up[0:1, :]), 0.0)
                shift = meta_up[1:2, :]
            elif b == nb:
                first, count = nb - 1, 1
                weight = jnp.where(i < nx - 1, taps(meta_down[0:1, :]), 0.0)
                shift = meta_down[1:2, :]
            else:
                first, count = (b, 1) if b in (0, nb - 1) else (b - 1, 3)
                weight = taps(meta[b : b + 1, :])
                shift = meta[nb + b : nb + b + 1, :]
            depth = count * BLK
            mat = split(banded(weight, shift, depth, (first - b) * BLK))
            rows = slice(first * BLK, first * BLK + depth)
            got = dot3(mat, (row_hi[rows, :], row_lo[rows, :]), ((0,), (0,))).astype(BF16)
            kept = side - 2 * ROW0
            if b == -1:
                to_up[...] = got[:, :side]
                side_up[...] = got
                across[kept + 16 : kept + 32, :] = got[BLK - 16 :, :]
            elif b == nb:
                to_down[...] = got[:, :side]
                side_down[...] = got
                across[kept : kept + 16, :] = got[:16, :]
            else:
                own[b * BLK : (b + 1) * BLK, :] = got[:, :side]
                low_row = max(b * BLK, ROW0)
                high_row = min((b + 1) * BLK, side - ROW0)
                across[low_row - ROW0 : high_row - ROW0, :] = got[low_row - b * BLK : high_row - b * BLK, :]

    @pl.when(jnp.logical_not(warper))
    def _():
        for bi in range(nb):
            for bj in range(nb):
                cell = bi * nb + bj
                coefs[cell : cell + 1, :] = table[pl.ds(ids[bi, bj], 1), :]
        width = nu * 160
        padded = prof_rows[...]
        spread = jnp.concatenate(
            [pltpu.roll(padded, p * 160 + 1, 1) for p in range(nu)], axis=0
        )
        base = jnp.dot(coefs[...], spread, precision=HIGHEST, preferred_element_type=F32)
        for cell in range(nb * nb):
            row = jnp.broadcast_to(base[cell : cell + 1, :], (BLK, width))
            kernels[cell] = pltpu.roll(row, 0, 1, stride=1, stride_axis=0).astype(BF16)
        for p in range(nu):
            row = jnp.broadcast_to(prof_cols[p : p + 1, :], (BLK, 3 * BLK))
            band[p * BLK : (p + 1) * BLK, :] = pltpu.roll(
                row, BLK - HALF, 1, stride=1, stride_axis=0
            ).astype(BF16)
        first = pltpu.make_async_copy(kernels, kernels_out, sem.at[0])
        second = pltpu.make_async_copy(band, band_out, sem.at[1])
        first.start()
        second.start()
        first.wait()
        second.wait()


def finish_kernel(
    nb, nu,
    frame, own, got_up, got_down, across, side_up, side_down, kernels_in, band_in,
    out, full, passed, kernels, band, sem,
):
    side = nb * BLK
    warper = lax.axis_index("segment") == 0
    last = side - BLK

    @pl.when(warper)
    def _():
        out[...] = own[...].astype(F32)
        for start, got in ((0, got_up), (last, got_down)):
            total = own[start : start + BLK, :].astype(F32) + got[...].astype(F32)
            out[start : start + BLK, :] = total.astype(BF16).astype(F32)

    @pl.when(jnp.logical_not(warper))
    def _():
        first = pltpu.make_async_copy(band_in, band, sem.at[0])
        second = pltpu.make_async_copy(kernels_in, kernels, sem.at[1])
        first.start()
        second.start()
        kept = side - 2 * ROW0

        def put(start, rows):
            stop = start + rows.shape[0]
            full[start:stop, BLK : BLK + side] = rows[:, :side]
            full[start:stop, :BLK] = rows[:, side:]
            full[start:stop, BLK + side :] = rows[:, side:]

        def added(one, two):
            return (one.astype(F32) + two.astype(F32)).astype(BF16)

        put(0, across[kept + 16 : kept + 32, :])
        put(16 + side, across[kept : kept + 16, :])
        put(16, side_up[:ROW0, :])
        both = BLK - ROW0
        put(16 + ROW0, added(across[:both, :], side_up[ROW0:, :]))
        put(16 + BLK, across[both : kept - both, :])
        put(16 + last, added(across[kept - both : kept, :], side_down[:both, :]))
        put(16 + side - ROW0, side_down[both:, :])
        first.wait()
        for bj in range(nb):
            got = lax.dot_general(
                full[:, bj * BLK : (bj + 3) * BLK], band[...], (((1,), (1,)), ((), ())),
                preferred_element_type=F32,
            ).astype(BF16)
            for p in range(nu):
                passed[p, :, bj * BLK : (bj + 1) * BLK] = got[:, p * BLK : (p + 1) * BLK]
        second.wait()
        for bi in range(nb):
            for bj in range(nb):
                cols = slice(bj * BLK, (bj + 1) * BLK)
                window = jnp.concatenate(
                    [passed[p, bi * BLK : bi * BLK + 160, cols] for p in range(nu)], axis=0
                )
                total = jnp.dot(kernels[bi * nb + bj], window, preferred_element_type=F32)
                rows = slice(bi * BLK, (bi + 1) * BLK)
                out[rows, cols] = frame[rows, cols] - total


def local(
    frames, row_shift, row_frac, col_shift, col_frac,
    profile_cols, profile_rows, coef_table, weight_ids,
):
    frame = frames[0]
    side = frame.shape[0]
    nb = side // BLK
    nu, nv = profile_cols.shape[0], profile_rows.shape[0]
    nx, ny = lax.axis_size("skyx"), lax.axis_size("skyy")
    spread_shift = lambda shift: jnp.broadcast_to(shift[:, None].astype(F32), (nb, BLK))
    row_meta = jnp.concatenate([row_frac.reshape(nb, BLK), spread_shift(row_shift)])
    col_meta = jnp.concatenate([col_frac.reshape(nb, BLK), spread_shift(col_shift)])
    meta = jnp.concatenate([row_meta, col_meta])
    fill = jnp.zeros((6, BLK), F32)

    def edge(array, b):
        return jnp.concatenate([array, col_meta[b : b + 1], col_meta[nb + b : nb + b + 1], fill])

    def row_edge(b):
        return jnp.concatenate([row_meta[b : b + 1], row_meta[nb + b : nb + b + 1], fill])

    left = moved(edge(frame[:, side - BLK :], nb - 1), (0, 0, 1), (0,))
    right = moved(edge(frame[:, :BLK], 0), (0, 0, -1), (0,))
    meta_up = moved(row_edge(nb - 1), (0, 1, 0), (0,))
    meta_down = moved(row_edge(0), (0, -1, 0), (0,))
    width = nu * 160
    prof_rows = jnp.pad(profile_rows.astype(F32), ((0, 0), (0, width - KW)))
    prof_cols = jnp.pad(profile_cols.astype(F32), ((0, 0), (0, 3 * BLK - KW)))
    wide = side + BLK
    kept = side - 2 * ROW0 + 32
    cells = nb * nb
    shape = jax.ShapeDtypeStruct
    own, across, to_up, to_down, side_up, side_down, kernels, band = pl.pallas_call(
        functools.partial(prepare_kernel, nb, nu, nv, nx, ny),
        out_shape=(
            shape((side, side), BF16), shape((kept, wide), BF16),
            shape((BLK, side), BF16), shape((BLK, side), BF16),
            shape((BLK, wide), BF16), shape((BLK, wide), BF16),
            shape((cells, BLK, width), BF16), shape((nu * BLK, 3 * BLK), BF16),
        ),
        in_specs=[VM] * 9 + [SM],
        out_specs=(VM,) * 6 + (HBM,) * 2,
        scratch_shapes=[
            pltpu.VMEM((side, side + 2 * BLK), BF16), pltpu.VMEM((side, side + 2 * BLK), BF16),
            pltpu.VMEM((side, wide), BF16), pltpu.VMEM((side, wide), BF16),
            pltpu.VMEM((cells, BLK, width), BF16), pltpu.VMEM((nu * BLK, 3 * BLK), BF16),
            pltpu.VMEM((cells, nu * nv), F32), pltpu.SemaphoreType.DMA((2,)),
        ],
        compiler_params=pltpu.CompilerParams(vmem_limit_bytes=48 << 20),
        name="prepare",
    )(frame, left, right, meta, meta_up, meta_down, prof_cols, prof_rows, coef_table, weight_ids)
    across = moved(across, (1, 0, 0), (0,))
    side_down_got = moved(side_up, (1, -1, 0), (0,))
    side_up_got = moved(side_down, (1, 1, 0), (0,))
    got_down = moved(to_up, (0, -1, 0), (0,))
    got_up = moved(to_down, (0, 1, 0), (0,))
    result = pl.pallas_call(
        functools.partial(finish_kernel, nb, nu),
        out_shape=shape((side, side), F32),
        in_specs=[VM] * 7 + [HBM] * 2,
        out_specs=VM,
        scratch_shapes=[
            pltpu.VMEM((side + 32, side + 2 * BLK), BF16), pltpu.VMEM((nu, side + 32, side), BF16),
            pltpu.VMEM((cells, BLK, width), BF16), pltpu.VMEM((nu * BLK, 3 * BLK), BF16),
            pltpu.SemaphoreType.DMA((2,)),
        ],
        compiler_params=pltpu.CompilerParams(vmem_limit_bytes=48 << 20),
        name="finish",
    )(frame, own, got_up, got_down, across, side_up_got, side_down_got, kernels, band)
    return result[None]


def solution(mesh):
    placed = (
        P("segment", "skyx", "skyy"), P("skyx"), P("skyx"), P("skyy"), P("skyy"),
        P(), P(), P(), P("skyx", "skyy"),
    )
    return jax.shard_map(
        local, mesh=mesh, in_specs=placed, out_specs=P("segment", "skyx", "skyy"), check_vma=False
    )
```

time: 467 us -> 54.4 us (0.12)
  the two profiles are of different devices: /device:TPU:14 before, /device:TPU:11 now
where the time goes in v1:
time: 54.4 us; the launch traced here: 53.9 us
  waiting for transfers between devices  25.5 us (47%)
  local copies, waits for them, and re-layouts  9.72 us (18%)
  starting transfers between devices  7.88 us (14%)
  Pallas kernels  6.73 us (12%)
  other arithmetic  3.83 us (7%)
    ppermute x9, waiting for transfers between devices, moved(): return lax.ppermute(block, axes, route)  25.5 us
    ppermute x9, starting transfers between devices, moved(): return lax.ppermute(block, axes, route)  7.88 us
    pallas_call x1, Pallas kernels, local(): pl.pallas_call(functools.partial(finish_kernel, nb, nu), out_shape=shape(...  3.61 us
    pallas_call x1, Pallas kernels, local(): pl.pallas_call(functools.partial(prepare_kernel, nb, nu, nv, nx, ny), out...  3.12 us
    unnamed x8, local copies, waits for them, and re-layouts  3.12 us
    convert_element_type x2, other arithmetic, local(): shift[:, None].astype(F32)  1.41 us
    concatenate x2, local copies, waits for them, and re-layouts, row_edge(): jnp.concatenate([row_meta[b:b + 1], row_meta[nb + b:nb + b + 1], fill])  1.35 us
    concatenate x2, local copies, waits for them, and re-layouts, edge(): jnp.concatenate([array, col_meta[b:b + 1], col_meta[nb + b:nb + b + 1], f...  1.35 us
  transfers between devices with their start and end apart: 9, of which 3 were waited for; matrix products, arithmetic and copies ran while one was open for 13% of the time, Pallas kernels for 0%

profile of v1, /device:TPU:11, one launch (start us, length us, event | category | flops | bytes accessed | tf_op | source)
XLA Modules:
  0.0 53.9 jit_solution(7026837486454521671)
XLA Ops:
  0.0 0.0 copy-start
  0.0 0.7 %convert_element_type.15 = f32[4]{0:T(128)S(1)} convert(s32[4]{0:T(128)} %param.10) | non-fusion elementwise | flops 4 | bytes 32 | tf_op jit(solution)/shard_map/convert_element_type | solution.py:249
  0.7 0.6 %fusion.1 = (f32[1]{0:T(128)}, f32[1]{0:T(128)}) fusion(f32[4]{0:T(128)S(1)} %convert_element_type.15), kind=kLoop, calls=%fused_computation.12 | loop fusion | bytes 16 | tf_op jit(solution)/shard_map/slice | solution.py:259
  1.3 0.7 %pad.17.clone = f32[8]{0:T(128)S(1)} pad(f32[1]{0:T(128)} %get-tuple-element.31, f32[]{:T(128)} %constant.11), padding=1_6 | pad | bytes 40 | tf_op jit(solution)/shard_map/concatenate | solution.py:259
  2.1 0.6 %pad.20.clone = f32[8]{0:T(128)S(1)} pad(f32[1]{0:T(128)} %get-tuple-element.32, f32[]{:T(128)} %constant.11), padding=1_6 | pad | bytes 40 | tf_op jit(solution)/shard_map/concatenate | solution.py:259
  2.7 0.8 %slice_bitcast_fusion = (f32[1,128]{1,0:T(1,128)S(1)}, f32[1,128]{1,0:T(1,128)S(1)}) fusion(f32[512]{0:T(512)} %param.11), kind=kLoop, calls=%fused_computation.7 | loop fusion | bytes 2048 | tf_op jit(solution)/shard_map/slice | solution.py:259
  3.4 0.1 pad_maximum_fusion.2
  3.5 0.6 %collective-permute-start.3 = (f32[8,128]{1,0:T(8,128)S(1)}, f32[8,128]{1,0:T(8,128)S(1)}, u32[]{:S(2)}, u32[]{:S(2)}) collective-permute-start(f32[8,128]{1,0:T(8,128)S(1)} %get-tuple-element.23), channel_id=1, source_target_pairs={{4,0},{5,1},{6,2},{7,3},{8,4},{9,5},{10,6},{11,7},{12,8},{13,9},{1... | collective-permute-start | bytes 12296 | tf_op jit(solution)/shard_map/ppermute | solution.py:34
  4.2 0.7 %collective-permute-start.2 = (f32[8,128]{1,0:T(8,128)S(1)}, f32[8,128]{1,0:T(8,128)S(1)}, u32[]{:S(2)}, u32[]{:S(2)}) collective-permute-start(f32[8,128]{1,0:T(8,128)S(1)} %get-tuple-element.24), channel_id=1, source_target_pairs={{0,4},{1,5},{2,6},{3,7},{4,8},{5,9},{6,10},{7,11},{8,12},{9,13},{1... | collective-permute-start | bytes 12296 | tf_op jit(solution)/shard_map/ppermute | solution.py:34
  4.8 0.7 %convert_element_type.14 = f32[4]{0:T(128)S(1)} convert(s32[4]{0:T(128)} %param.12) | non-fusion elementwise | flops 4 | bytes 32 | tf_op jit(solution)/shard_map/convert_element_type | solution.py:249
  5.5 0.6 %fusion.2 = (f32[1]{0:T(128)}, f32[1]{0:T(128)}) fusion(f32[4]{0:T(128)S(1)} %convert_element_type.14), kind=kLoop, calls=%fused_computation.13 | loop fusion | bytes 16 | tf_op jit(solution)/shard_map/slice | solution.py:256
  6.1 0.8 %slice_bitcast_fusion.2 = (f32[1,128]{1,0:T(1,128)S(1)}, f32[1,128]{1,0:T(1,128)S(1)}) fusion(f32[512]{0:T(512)} %param.13), kind=kLoop, calls=%fused_computation.9 | loop fusion | bytes 2048 | tf_op jit(solution)/shard_map/slice | solution.py:256
  6.9 0.7 %pad.28.clone = f32[520]{0:T(1024)S(1)} pad(f32[1]{0:T(128)} %get-tuple-element.33, f32[]{:T(128)} %constant.11), padding=513_6 | pad | bytes 2088 | tf_op jit(solution)/shard_map/concatenate | solution.py:256
  7.6 0.6 %pad.32.clone = f32[520]{0:T(1024)S(1)} pad(f32[1]{0:T(128)} %get-tuple-element.34, f32[]{:T(128)} %constant.11), padding=513_6 | pad | bytes 2088 | tf_op jit(solution)/shard_map/concatenate | solution.py:256
  8.2 1.1 %fusion = (f32[512,128]{1,0:T(8,128)S(1)}, f32[512,128]{1,0:T(8,128)S(1)}) fusion(f32[512,512]{1,0:T(8,128)} %bitcast.16), kind=kLoop, calls=%fused_computation.11 | loop fusion | bytes 1048576 | tf_op jit(solution)/shard_map/slice | solution.py:262
  9.3 0.2 pad_maximum_fusion
  9.5 0.7 %collective-permute-start.1 = (f32[520,128]{1,0:T(8,128)S(1)}, f32[520,128]{1,0:T(8,128)S(1)}, u32[]{:S(2)}, u32[]{:S(2)}) collective-permute-start(f32[520,128]{1,0:T(8,128)S(1)} %get-tuple-element.25), channel_id=1, source_target_pairs={{1,0},{2,1},{3,2},{5,4},{6,5},{7,6},{9,8},{10,9},{11,10},{13,12},{... | collective-permute-start | bytes 798728 | tf_op jit(solution)/shard_map/ppermute | solution.py:34
  10.2 0.7 %collective-permute-start = (f32[520,128]{1,0:T(8,128)S(1)}, f32[520,128]{1,0:T(8,128)S(1)}, u32[]{:S(2)}, u32[]{:S(2)}) collective-permute-start(f32[520,128]{1,0:T(8,128)S(1)} %get-tuple-element.26), channel_id=1, source_target_pairs={{0,1},{1,2},{2,3},{4,5},{5,6},{6,7},{8,9},{9,10},{10,11},{12,13},{... | collective-permute-start | bytes 798728 | tf_op jit(solution)/shard_map/ppermute | solution.py:34
  10.9 0.1 pad.25.clone
  10.9 0.1 pad.23.clone
  11.0 0.8 %maximum_maximum_fusion.meta = f32[16,128]{1,0:T(8,128)S(1)} fusion(f32[4,128]{1,0:T(4,128)} %bitcast.19, f32[4,128]{1,0:T(4,128)} %bitcast.20, f32[16]{0:T(128)S(1)} %pad.25.clone, f32[16]{0:T(128)S(1)} %pad.23.clone), kind=kLoop, calls=%fused_computation.3 | loop fusion | flops 6144 | bytes 12416 | tf_op jit(solution)/shard_map/concatenate | solution.py:252
  11.8 0.7 %pad_convert_fusion.prof_rows = f32[8,640]{1,0:T(8,128)S(1)} fusion(bf16[8,31]{1,0:T(8,128)(2,1)} %param.15), kind=kLoop, calls=%fused_computation.2 | loop fusion | flops 5120 | bytes 20976 | tf_op jit(solution)/shard_map/jit(_pad)/pad | solution.py:266
  12.5 0.7 %pad_convert_fusion.1.prof_cols = f32[4,384]{1,0:T(4,128)S(1)} fusion(bf16[4,31]{1,0:T(4,128)(2,1)} %param.14), kind=kLoop, calls=%fused_computation.6 | loop fusion | flops 1536 | bytes 6392 | tf_op jit(solution)/shard_map/jit(_pad)/pad | solution.py:267
  13.1 0.0 collective-permute-done.3.meta_down
  13.1 0.0 collective-permute-done.2.meta_up
  13.2 0.0 collective-permute-done.1.right
  13.2 0.0 collective-permute-done.left
  13.2 0.0 copy-done
  13.2 0.0 copy-start.2
  13.2 0.7 %copy-done.2 = f32[16,32]{1,0:T(8,128)S(1)} copy-done((f32[16,32]{1,0:T(8,128)S(1)}, f32[16,32]{1,0:T(8,128)}, u32[]{:S(2)}) %copy-start.2) | copy-done | bytes 2072
  13.9 0.0 copy-start.3
  13.9 0.7 %copy-done.3 = s32[4,4]{1,0:T(4,128)S(1)} copy-done((s32[4,4]{1,0:T(4,128)S(1)}, s32[4,4]{1,0:T(4,128)}, u32[]{:S(2)}) %copy-start.3) | copy-done | bytes 88
  14.6 3.1 %prepare.1 = (bf16[512,512]{1,0:T(8,128)(2,1)S(1)}, bf16[448,640]{1,0:T(8,128)(2,1)S(1)}, bf16[128,512]{1,0:T(8,128)(2,1)S(1)}, bf16[128,512]{1,0:T(8,128)(2,1)S...) custom-call(f32[512,512]{1,0:T(8,128)S(1)} %bitcast.17, ...), custom_call_target="tpu_custom_call" | custom-call | tf_op jit(solution)/shard_map/prepare/pallas_call | solution.py:272
  17.7 1.3 %collective-permute-start.6 = (bf16[448,640]{1,0:T(8,128)(2,1)S(1)}, bf16[448,640]{1,0:T(8,128)(2,1)S(1)}, u32[]{:S(2)}, u32[]{:S(2)}) collective-permute-start(bf16[448,640]{1,0:T(8,128)(2,1)S(1)} %get-tuple-element.16), channel_id=1, source_target_pairs={{0,16},{1,17},{2,18},{3,19},{4,20},{5,21},{6,22},{7,23},{8,24},{9,... | collective-permute-start | bytes 1720328 | tf_op jit(solution)/shard_map/ppermute | solution.py:34
  19.0 1.3 %collective-permute-start.7 = (bf16[128,640]{1,0:T(8,128)(2,1)S(1)}, bf16[128,640]{1,0:T(8,128)(2,1)S(1)}, u32[]{:S(2)}, u32[]{:S(2)}) collective-permute-start(bf16[128,640]{1,0:T(8,128)(2,1)S(1)} %get-tuple-element.17), channel_id=1, source_target_pairs={{0,20},{1,21},{2,22},{3,23},{4,24},{5,25},{6,26},{7,27},{8,28},{9,... | collective-permute-start | bytes 491528 | tf_op jit(solution)/shard_map/ppermute | solution.py:34
  20.3 1.3 %collective-permute-start.8 = (bf16[128,640]{1,0:T(8,128)(2,1)S(1)}, bf16[128,640]{1,0:T(8,128)(2,1)S(1)}, u32[]{:S(2)}, u32[]{:S(2)}) collective-permute-start(bf16[128,640]{1,0:T(8,128)(2,1)S(1)} %get-tuple-element.18), channel_id=1, source_target_pairs={{4,16},{5,17},{6,18},{7,19},{8,20},{9,21},{10,22},{11,23},{12,24},... | collective-permute-start | bytes 491528 | tf_op jit(solution)/shard_map/ppermute | solution.py:34
  21.6 0.7 %collective-permute-start.4 = (bf16[128,512]{1,0:T(8,128)(2,1)S(1)}, bf16[128,512]{1,0:T(8,128)(2,1)S(1)}, u32[]{:S(2)}, u32[]{:S(2)}) collective-permute-start(bf16[128,512]{1,0:T(8,128)(2,1)S(1)} %get-tuple-element.14), channel_id=1, source_target_pairs={{0,4},{1,5},{2,6},{3,7},{4,8},{5,9},{6,10},{7,11},{8,12},{9,13},{1... | collective-permute-start | bytes 393224 | tf_op jit(solution)/shard_map/ppermute | solution.py:34
  22.3 0.7 %collective-permute-start.5 = (bf16[128,512]{1,0:T(8,128)(2,1)S(1)}, bf16[128,512]{1,0:T(8,128)(2,1)S(1)}, u32[]{:S(2)}, u32[]{:S(2)}) collective-permute-start(bf16[128,512]{1,0:T(8,128)(2,1)S(1)} %get-tuple-element.15), channel_id=1, source_target_pairs={{4,0},{5,1},{6,2},{7,3},{8,4},{9,5},{10,6},{11,7},{12,8},{13,9},{1... | collective-permute-start | bytes 393224 | tf_op jit(solution)/shard_map/ppermute | solution.py:34
  23.0 0.0 collective-permute-done.4.got_up
  23.0 0.0 collective-permute-done.5.got_down
  23.0 11.5 %collective-permute-done.7.side_up = bf16[128,640]{1,0:T(8,128)(2,1)S(1)} collective-permute-done((bf16[128,640]{1,0:T(8,128)(2,1)S(1)}, bf16[128,640]{1,0:T(8,128)(2,1)S(1)}, u32[]{:S(2)}, u32[]{:S(2)}) %collective-permute-start.7) | collective-permute-done | bytes 163872 | tf_op jit(solution)/shard_map/ppermute | solution.py:34
  34.4 2.7 %collective-permute-done.8.side_down = bf16[128,640]{1,0:T(8,128)(2,1)S(1)} collective-permute-done((bf16[128,640]{1,0:T(8,128)(2,1)S(1)}, bf16[128,640]{1,0:T(8,128)(2,1)S(1)}, u32[]{:S(2)}, u32[]{:S(2)}) %collective-permute-start.8) | collective-permute-done | bytes 163872 | tf_op jit(solution)/shard_map/ppermute | solution.py:34
  37.2 11.3 %collective-permute-done.6.across = bf16[448,640]{1,0:T(8,128)(2,1)S(1)} collective-permute-done((bf16[448,640]{1,0:T(8,128)(2,1)S(1)}, bf16[448,640]{1,0:T(8,128)(2,1)S(1)}, u32[]{:S(2)}, u32[]{:S(2)}) %collective-permute-start.6) | collective-permute-done | bytes 573472 | tf_op jit(solution)/shard_map/ppermute | solution.py:34
  48.5 0.0 copy-start.1
  48.5 1.7 %copy-done.1 = bf16[16,128,640]{2,1,0:T(8,128)(2,1)S(1)} copy-done((bf16[16,128,640]{2,1,0:T(8,128)(2,1)S(1)}, bf16[16,128,640]{2,1,0:T(8,128)(2,1)}, u32[]{:S(2)}) %copy-start.1) | copy-done | bytes 2621464
  50.2 3.6 %finish.1 = f32[512,512]{1,0:T(8,128)} custom-call(f32[512,512]{1,0:T(8,128)S(1)} %bitcast.18, bf16[512,512]{1,0:T(8,128)(2,1)S(1)} %get-tuple-element.13.own, bf16[128,512]{1,0:T(8,128)(2,1)S(1)} %collective-permute-done.4.got_up, bf16[128,512]{1,0:T(8,128)(2,1)S(1)} %collective-permute-done.5.got_down, bf16[448,640]{1,0:T(8,128)(2,1)S(1)} %collective-permute-done.6.across, ...), custom_call_target="tpu_custom_call" | custom-call | tf_op jit(solution)/shard_map/finish/pallas_call | solution.py:296
  (1 shorter events, 0.0 us)
Async XLA Ops:
  0.0 13.2 %copy-start = (f32[1,512,512]{2,1,0:T(8,128)S(1)}, f32[1,512,512]{2,1,0:T(8,128)}, u32[]{:S(2)}) copy-start(f32[1,512,512]{2,1,0:T(8,128)} %param.9) | copy-start | bytes 3145732
  3.5 9.6 %collective-permute-start.3 = (f32[8,128]{1,0:T(8,128)S(1)}, f32[8,128]{1,0:T(8,128)S(1)}, u32[]{:S(2)}, u32[]{:S(2)}) collective-permute-start(f32[8,128]{1,0:T(8,128)S(1)} %get-tuple-element.23), channel_id=1, source_target_pairs={{4,0},{5,1},{6,2},{7,3},{8,4},{9,5},{10,6},{11,7},{12,8},{13,9},{1... | collective-permute-start | bytes 12296 | tf_op jit(solution)/shard_map/ppermute | solution.py:34
  4.2 9.0 %collective-permute-start.2 = (f32[8,128]{1,0:T(8,128)S(1)}, f32[8,128]{1,0:T(8,128)S(1)}, u32[]{:S(2)}, u32[]{:S(2)}) collective-permute-start(f32[8,128]{1,0:T(8,128)S(1)} %get-tuple-element.24), channel_id=1, source_target_pairs={{0,4},{1,5},{2,6},{3,7},{4,8},{5,9},{6,10},{7,11},{8,12},{9,13},{1... | collective-permute-start | bytes 12296 | tf_op jit(solution)/shard_map/ppermute | solution.py:34
  9.5 3.7 %collective-permute-start.1 = (f32[520,128]{1,0:T(8,128)S(1)}, f32[520,128]{1,0:T(8,128)S(1)}, u32[]{:S(2)}, u32[]{:S(2)}) collective-permute-start(f32[520,128]{1,0:T(8,128)S(1)} %get-tuple-element.25), channel_id=1, source_target_pairs={{1,0},{2,1},{3,2},{5,4},{6,5},{7,6},{9,8},{10,9},{11,10},{13,12},{... | collective-permute-start | bytes 798728 | tf_op jit(solution)/shard_map/ppermute | solution.py:34
  10.2 3.0 %collective-permute-start = (f32[520,128]{1,0:T(8,128)S(1)}, f32[520,128]{1,0:T(8,128)S(1)}, u32[]{:S(2)}, u32[]{:S(2)}) collective-permute-start(f32[520,128]{1,0:T(8,128)S(1)} %get-tuple-element.26), channel_id=1, source_target_pairs={{0,1},{1,2},{2,3},{4,5},{5,6},{6,7},{8,9},{9,10},{10,11},{12,13},{... | collective-permute-start | bytes 798728 | tf_op jit(solution)/shard_map/ppermute | solution.py:34
  13.2 0.7 %copy-start.2 = (f32[16,32]{1,0:T(8,128)S(1)}, f32[16,32]{1,0:T(8,128)}, u32[]{:S(2)}) copy-start(f32[16,32]{1,0:T(8,128)} %table.1) | copy-start | bytes 6148
  13.9 0.7 %copy-start.3 = (s32[4,4]{1,0:T(4,128)S(1)}, s32[4,4]{1,0:T(4,128)}, u32[]{:S(2)}) copy-start(s32[4,4]{1,0:T(4,128)} %ids.1) | copy-start | bytes 196
  17.7 30.8 %collective-permute-start.6 = (bf16[448,640]{1,0:T(8,128)(2,1)S(1)}, bf16[448,640]{1,0:T(8,128)(2,1)S(1)}, u32[]{:S(2)}, u32[]{:S(2)}) collective-permute-start(bf16[448,640]{1,0:T(8,128)(2,1)S(1)} %get-tuple-element.16), channel_id=1, source_target_pairs={{0,16},{1,17},{2,18},{3,19},{4,20},{5,21},{6,22},{7,23},{8,24},{9,... | collective-permute-start | bytes 1720328 | tf_op jit(solution)/shard_map/ppermute | solution.py:34
  19.0 15.4 %collective-permute-start.7 = (bf16[128,640]{1,0:T(8,128)(2,1)S(1)}, bf16[128,640]{1,0:T(8,128)(2,1)S(1)}, u32[]{:S(2)}, u32[]{:S(2)}) collective-permute-start(bf16[128,640]{1,0:T(8,128)(2,1)S(1)} %get-tuple-element.17), channel_id=1, source_target_pairs={{0,20},{1,21},{2,22},{3,23},{4,24},{5,25},{6,26},{7,27},{8,28},{9,... | collective-permute-start | bytes 491528 | tf_op jit(solution)/shard_map/ppermute | solution.py:34
  20.3 16.9 %collective-permute-start.8 = (bf16[128,640]{1,0:T(8,128)(2,1)S(1)}, bf16[128,640]{1,0:T(8,128)(2,1)S(1)}, u32[]{:S(2)}, u32[]{:S(2)}) collective-permute-start(bf16[128,640]{1,0:T(8,128)(2,1)S(1)} %get-tuple-element.18), channel_id=1, source_target_pairs={{4,16},{5,17},{6,18},{7,19},{8,20},{9,21},{10,22},{11,23},{12,24},... | collective-permute-start | bytes 491528 | tf_op jit(solution)/shard_map/ppermute | solution.py:34
  21.6 1.4 %collective-permute-start.4 = (bf16[128,512]{1,0:T(8,128)(2,1)S(1)}, bf16[128,512]{1,0:T(8,128)(2,1)S(1)}, u32[]{:S(2)}, u32[]{:S(2)}) collective-permute-start(bf16[128,512]{1,0:T(8,128)(2,1)S(1)} %get-tuple-element.14), channel_id=1, source_target_pairs={{0,4},{1,5},{2,6},{3,7},{4,8},{5,9},{6,10},{7,11},{8,12},{9,13},{1... | collective-permute-start | bytes 393224 | tf_op jit(solution)/shard_map/ppermute | solution.py:34
  22.3 0.7 %collective-permute-start.5 = (bf16[128,512]{1,0:T(8,128)(2,1)S(1)}, bf16[128,512]{1,0:T(8,128)(2,1)S(1)}, u32[]{:S(2)}, u32[]{:S(2)}) collective-permute-start(bf16[128,512]{1,0:T(8,128)(2,1)S(1)} %get-tuple-element.15), channel_id=1, source_target_pairs={{4,0},{5,1},{6,2},{7,3},{8,4},{9,5},{10,6},{11,7},{12,8},{13,9},{1... | collective-permute-start | bytes 393224 | tf_op jit(solution)/shard_map/ppermute | solution.py:34
  48.5 1.7 %copy-start.1 = (bf16[16,128,640]{2,1,0:T(8,128)(2,1)S(1)}, bf16[16,128,640]{2,1,0:T(8,128)(2,1)}, u32[]{:S(2)}) copy-start(bf16[16,128,640]{2,1,0:T(8,128)(2,1)} %get-tuple-element.19.kernels_in) | copy-start | bytes 7864324

commit v2 on v1

v2 whole, which is shorter than its diff:
```python
import functools
import math

import jax
import jax.numpy as jnp
from jax import lax
from jax.experimental import pallas as pl
from jax.experimental.pallas import tpu as pltpu
from jax.sharding import PartitionSpec as P

BLK = 128
KW = 31
HALF = 15
ROW0 = 48
F32 = jnp.float32
BF16 = jnp.bfloat16
HIGHEST = lax.Precision.HIGHEST
VM = pl.BlockSpec(memory_space=pltpu.VMEM)
SM = pl.BlockSpec(memory_space=pltpu.SMEM)


def moved(block, step, sources):
    axes = ("segment", "skyx", "skyy")
    counts = [lax.axis_size(axis) for axis in axes]
    route = []
    for s in range(counts[0]):
        for i in range(counts[1]):
            for j in range(counts[2]):
                to = (s + step[0], i + step[1], j + step[2])
                if s in sources and all(0 <= to[k] < counts[k] for k in range(3)):
                    flat = [(a * counts[1] + b) * counts[2] + c for a, b, c in ((s, i, j), to)]
                    route.append(tuple(flat))
    return lax.ppermute(block, axes, route)


def sinc(values):
    angle = math.pi * values
    zero = values == 0.0
    return jnp.where(zero, 1.0, jnp.sin(angle) / jnp.where(zero, 1.0, angle))


def taps(fracs):
    count = len(fracs)
    spread = jnp.concatenate([jnp.broadcast_to(frac, (8, BLK)) for frac in fracs], axis=0)
    lag = (lax.broadcasted_iota(jnp.int32, (8 * count, BLK), 0) & 7) - 2
    values = lag.astype(F32) - spread
    weight = jnp.where(jnp.abs(values) < 3.0, sinc(values) * sinc(values / 3.0), 0.0)
    return [weight[8 * n : 8 * n + 8] for n in range(count)]


def split(values):
    high = values.astype(BF16)
    return high, (values - high.astype(F32)).astype(BF16)


def banded(weight, shift, depth, offset):
    lag = (
        lax.broadcasted_iota(jnp.int32, (depth, BLK), 0)
        - lax.broadcasted_iota(jnp.int32, (depth, BLK), 1)
        + (offset - shift)
    )
    total = jnp.zeros((depth, BLK), F32)
    for tap in range(6):
        total = jnp.where(lag == tap - 2, weight[tap : tap + 1], total)
    return total


def dot3(left, right, dims):
    lh, ll = left
    rh, rl = right
    dot = functools.partial(
        lax.dot_general, dimension_numbers=(dims, ((), ())), preferred_element_type=F32
    )
    return dot(lh, rh) + dot(lh, rl) + dot(ll, rh)


MATMUL = ((1,), (0,))
LEFT_T = ((0,), (0,))


def row_depth(b, nb):
    return BLK if b in (0, nb - 1) else 3 * BLK


def row_start(b, nb):
    return sum(row_depth(a, nb) for a in range(b))


def row_source(b, nb):
    first = b if b in (0, nb - 1) else b - 1
    return slice(first * BLK, first * BLK + row_depth(b, nb))


def pack_kernel(nb, frame, row_frac, col_frac, row_shift, col_shift, to_right, to_left, to_up, to_down):
    side = nb * BLK

    @pl.when(lax.axis_index("segment") == 0)
    def _():
        for out, lane, b in ((to_right, side - BLK, nb - 1), (to_left, 0, 0)):
            out[:side, :] = frame[:, lane : lane + BLK]
            out[side : side + 1, :] = col_frac[b : b + 1, :]
            out[side + 1 : side + 2, :] = jnp.full((1, BLK), col_shift[b].astype(F32))
        for out, b in ((to_up, 0), (to_down, nb - 1)):
            out[0:1, :] = row_frac[b : b + 1, :]
            out[1:2, :] = jnp.full((1, BLK), row_shift[b].astype(F32))


def center_kernel(
    nb, nu, nv,
    frame, row_frac, col_frac, row_shift, col_shift, prof_cols, prof_rows, table, ids,
    own, across, src_hi, src_lo, mid_hi, mid_lo, row_hi, row_lo, edge_hi, edge_lo, kernels, band,
    coefs, padded,
):
    side = nb * BLK
    warper = lax.axis_index("segment") == 0

    @pl.when(warper)
    def _():
        weights = taps([col_frac[b : b + 1, :] for b in range(nb)] + [row_frac[b : b + 1, :] for b in range(nb)])
        hi, lo = split(frame[...])
        src_hi[...] = hi
        src_lo[...] = lo
        for b in range(1, nb - 1):
            mat = split(banded(weights[b], col_shift[b], 3 * BLK, -BLK))
            cols = slice((b - 1) * BLK, (b + 2) * BLK)
            hi, lo = split(dot3((src_hi[:, cols], src_lo[:, cols]), mat, MATMUL))
            mid_hi[:, (b - 1) * BLK : b * BLK] = hi
            mid_lo[:, (b - 1) * BLK : b * BLK] = lo
        for b in range(nb):
            offset = 0 if b in (0, nb - 1) else -BLK
            depth = row_depth(b, nb)
            hi, lo = split(banded(weights[nb + b], row_shift[b], depth, offset))
            kept = slice(row_start(b, nb), row_start(b, nb) + depth)
            row_hi[kept, :] = hi
            row_lo[kept, :] = lo
            rows = row_source(b, nb)
            got = dot3((hi, lo), (mid_hi[rows, :], mid_lo[rows, :]), LEFT_T).astype(BF16)
            own[b * BLK : (b + 1) * BLK, :] = got
            low = max(b * BLK, ROW0)
            high = min((b + 1) * BLK, side - ROW0)
            across[low - ROW0 : high - ROW0, :] = got[low - b * BLK : high - b * BLK, :]
        for n, (b, offset) in enumerate(((0, -BLK), (nb - 1, 0))):
            hi, lo = split(banded(weights[b], col_shift[b], 2 * BLK, offset))
            edge_hi[n * 2 * BLK : (n + 1) * 2 * BLK, :] = hi
            edge_lo[n * 2 * BLK : (n + 1) * 2 * BLK, :] = lo

    @pl.when(jnp.logical_not(warper))
    def _():
        for bi in range(nb):
            for bj in range(nb):
                cell = bi * nb + bj
                coefs[cell : cell + 1, :] = table[pl.ds(ids[bi, bj], 1), :]
        width = nu * 160
        padded[...] = jnp.zeros_like(padded)
        padded[0:nv, 0:KW] = prof_rows[...].astype(F32)
        profile = padded[0:nv, :]
        spread = jnp.concatenate(
            [pltpu.roll(profile, p * 160 + 1, 1) for p in range(nu)], axis=0
        )
        base = jnp.dot(coefs[...], spread, precision=HIGHEST, preferred_element_type=F32)
        for cell in range(nb * nb):
            row = jnp.broadcast_to(base[cell : cell + 1, :], (BLK, width))
            kernels[cell] = pltpu.roll(row, 0, 1, stride=1, stride_axis=0).astype(BF16)
        padded[...] = jnp.zeros_like(padded)
        padded[0:nu, 0:KW] = prof_cols[...].astype(F32)
        for p in range(nu):
            row = jnp.broadcast_to(padded[p : p + 1, : 3 * BLK], (BLK, 3 * BLK))
            band[p * BLK : (p + 1) * BLK, :] = pltpu.roll(
                row, BLK - HALF, 1, stride=1, stride_axis=0
            ).astype(BF16)


def edge_kernel(
    nb, nx, ny,
    left, right, meta_up, meta_down, src_hi, src_lo, mid_hi, mid_lo, row_hi, row_lo, edge_hi, edge_lo,
    own, across, side_up, side_down,
    end_hi, end_lo,
):
    side = nb * BLK
    kept = side - 2 * ROW0
    half = side // 2
    i = lax.axis_index("skyx")
    j = lax.axis_index("skyy")

    @pl.when(lax.axis_index("segment") == 0)
    def _():
        lanes = lax.broadcasted_iota(jnp.int32, (8, BLK), 1)
        weights = taps([left[side : side + 1, :], right[side : side + 1, :], meta_up[0:1, :], meta_down[0:1, :]])
        shifts = [
            part[row : row + 1, :].astype(jnp.int32)
            for part, row in ((left, side + 1), (right, side + 1), (meta_up, 1), (meta_down, 1))
        ]
        parts = [split(left[:side, :]), split(right[:side, :])]
        for n, col in ((0, 0), (1, side - BLK)):
            source = []
            for part, src in zip(parts[n], (src_hi, src_lo)):
                inner = src[:, col : col + BLK]
                source.append(jnp.concatenate([part, inner] if n == 0 else [inner, part], axis=1))
            mat = tuple(edge[n * 2 * BLK : (n + 1) * 2 * BLK, :] for edge in (edge_hi, edge_lo))
            hi, lo = split(dot3(source, mat, MATMUL))
            end_hi[:, n * BLK : (n + 1) * BLK] = hi
            end_lo[:, n * BLK : (n + 1) * BLK] = lo
        low_ok = jnp.logical_and(lanes >= BLK - HALF, j > 0)
        high_ok = jnp.logical_and(lanes < HALF, j < ny - 1)
        low = split(banded(jnp.where(low_ok, weights[0], 0.0), shifts[0], BLK, BLK))
        high = split(banded(jnp.where(high_ok, weights[1], 0.0), shifts[1], BLK, -BLK))
        mat = [jnp.concatenate(pair, axis=0) for pair in zip(low, high)]
        source = [
            jnp.concatenate([src[:, :BLK], src[:, side - BLK :]], axis=1) for src in (src_hi, src_lo)
        ]
        hi, lo = split(dot3(source, mat, MATMUL))
        end_hi[:, 2 * BLK :] = hi
        end_lo[:, 2 * BLK :] = lo
        outer = []
        for n, b in ((0, 0), (1, nb - 1)):
            there = (i > 0) if n == 0 else (i < nx - 1)
            mat = split(banded(jnp.where(there, weights[2 + n], 0.0), shifts[2 + n], BLK, BLK if n == 0 else -BLK))
            rows = slice(b * BLK, (b + 1) * BLK)
            end = dot3(mat, (end_hi[rows, : 2 * BLK], end_lo[rows, : 2 * BLK]), LEFT_T).astype(BF16)
            mid = dot3(mat, (mid_hi[rows, :], mid_lo[rows, :]), LEFT_T).astype(BF16)
            turned = dot3((end_hi[rows, 2 * BLK :], end_lo[rows, 2 * BLK :]), mat, LEFT_T)
            out = side_up if n == 0 else side_down
            out[:BLK, :BLK] = end[:, :BLK]
            out[:BLK, BLK : side - BLK] = mid
            out[:BLK, side - BLK :] = end[:, BLK:]
            out[BLK:, :BLK] = turned[:16].astype(BF16)
            out[BLK:, BLK : 2 * BLK] = turned[BLK - 16 :].astype(BF16)
            outer.append(turned)
        across[kept : kept + 16, :] = side_down[:16, :half]
        across[kept + 16 : kept + 32, :] = side_up[BLK - 16 : BLK, :half]
        across[kept + 32 : kept + 48, :] = side_down[:16, half:]
        across[kept + 48 : kept + 64, :] = side_up[BLK - 16 : BLK, half:]
        columns = lax.broadcasted_iota(jnp.int32, (BLK, BLK), 1)
        for b in range(nb):
            hi, lo = (mat[row_start(b, nb) : row_start(b, nb) + row_depth(b, nb), :] for mat in (row_hi, row_lo))
            rows = row_source(b, nb)
            got = dot3((hi, lo), (end_hi[rows, : 2 * BLK], end_lo[rows, : 2 * BLK]), LEFT_T).astype(BF16)
            own[b * BLK : (b + 1) * BLK, :] = got
            low = max(b * BLK, ROW0)
            high = min((b + 1) * BLK, side - ROW0)
            across[low - ROW0 : high - ROW0, :] = got[low - b * BLK : high - b * BLK, :]
            turned = dot3((end_hi[rows, 2 * BLK :], end_lo[rows, 2 * BLK :]), (hi, lo), LEFT_T)
            if b == 0:
                turned = jnp.where(columns < ROW0, pltpu.roll(outer[0], ROW0, 1), turned)
            if b == nb - 1:
                turned = jnp.where(columns >= BLK - ROW0, pltpu.roll(outer[1], BLK - ROW0, 1), turned)
            half_at, lane = divmod(b * BLK, half)
            base = kept + 64 + 32 * half_at
            across[base : base + 16, lane : lane + BLK] = turned[:16].astype(BF16)
            across[base + 16 : base + 32, lane : lane + BLK] = turned[BLK - 16 :].astype(BF16)


def finish_kernel(
    nb, nu,
    frame, own_mid, own_end, side_up, side_down, mid, end, kernels, band, got_up, got_down,
    out, full, passed,
):
    side = nb * BLK
    half = side // 2
    warper = lax.axis_index("segment") == 0
    last = side - BLK

    @pl.when(warper)
    def _():
        for b in range(nb):
            rows = slice(b * BLK, (b + 1) * BLK)
            pieces = ((0, own_end[rows, :BLK]), (BLK, own_mid[rows, :]), (last, own_end[rows, BLK:]))
            for lane, piece in pieces:
                cols = slice(lane, lane + piece.shape[1])
                total = piece.astype(F32)
                if b == 0:
                    total = (total + got_up[:BLK, cols].astype(F32)).astype(BF16).astype(F32)
                if b == nb - 1:
                    total = (total + got_down[:BLK, cols].astype(F32)).astype(BF16).astype(F32)
                out[rows, cols] = total

    @pl.when(jnp.logical_not(warper))
    def _():
        kept = side - 2 * ROW0
        both = BLK - ROW0
        stop = 16 + side

        def added(one, two):
            return (one.astype(F32) + two.astype(F32)).astype(BF16)

        def fill(at, width, own, above, below):
            cols = slice(at, at + width)
            full[16 : 16 + ROW0, cols] = above[:ROW0]
            full[16 + ROW0 : 16 + BLK, cols] = added(own[:both], above[ROW0:])
            full[16 + BLK : 16 + last, cols] = own[both : kept - both]
            full[16 + last : stop - ROW0, cols] = added(own[kept - both :], below[:both])
            full[stop - ROW0 : stop, cols] = below[both:]

        fill(2 * BLK, side - 2 * BLK, mid[:kept, :], side_up[:BLK, BLK:last], side_down[:BLK, BLK:last])
        fill(BLK, BLK, end[:kept, :BLK], side_up[:BLK, :BLK], side_down[:BLK, :BLK])
        fill(side, BLK, end[:kept, BLK:], side_up[:BLK, last:], side_down[:BLK, last:])
        full[:16, BLK : BLK + half] = end[kept + 16 : kept + 32, :]
        full[:16, BLK + half : BLK + side] = end[kept + 48 : kept + 64, :]
        full[stop:, BLK : BLK + half] = end[kept : kept + 16, :]
        full[stop:, BLK + half : BLK + side] = end[kept + 32 : kept + 48, :]
        k = lax.broadcasted_iota(jnp.int32, (32, BLK), 0)
        lanes = lax.broadcasted_iota(jnp.int32, (32, BLK), 1)
        pick = (lanes == jnp.where(k < 16, k, k + BLK - 32)).astype(BF16)

        def turned(rows):
            return lax.dot_general(
                rows, pick, (LEFT_T, ((), ())), preferred_element_type=F32
            ).astype(BF16)

        base = kept + 64
        own = jnp.concatenate([turned(end[base : base + 32, :]), turned(end[base + 32 : base + 64, :])], axis=0)
        above, below = (
            turned(jnp.concatenate([part[BLK:, :BLK], part[BLK:, BLK : 2 * BLK]], axis=0))
            for part in (side_up, side_down)
        )
        fill(0, BLK, own[ROW0 : side - ROW0], above, below)
        full[:16, :BLK] = own[ROW0 - 16 : ROW0]
        full[stop:, :BLK] = own[side - ROW0 : side - ROW0 + 16]
        full[:, BLK + side :] = full[:, :BLK]
        for bj in range(nb):
            got = lax.dot_general(
                full[:, bj * BLK : (bj + 3) * BLK], band[...], (((1,), (1,)), ((), ())),
                preferred_element_type=F32,
            ).astype(BF16)
            for p in range(nu):
                passed[p, :, bj * BLK : (bj + 1) * BLK] = got[:, p * BLK : (p + 1) * BLK]
        for bi in range(nb):
            for bj in range(nb):
                cols = slice(bj * BLK, (bj + 1) * BLK)
                window = jnp.concatenate(
                    [passed[p, bi * BLK : bi * BLK + 160, cols] for p in range(nu)], axis=0
                )
                total = jnp.dot(kernels[bi * nb + bj], window, preferred_element_type=F32)
                rows = slice(bi * BLK, (bi + 1) * BLK)
                out[rows, cols] = frame[rows, cols] - total


def call(kernel, name, out_shape, in_specs, scratch=(), flops=0):
    many = isinstance(out_shape, tuple)
    return pl.pallas_call(
        kernel,
        out_shape=out_shape,
        in_specs=in_specs,
        out_specs=(VM,) * len(out_shape) if many else VM,
        scratch_shapes=list(scratch),
        compiler_params=pltpu.CompilerParams(vmem_limit_bytes=40 << 20),
        cost_estimate=pl.CostEstimate(flops=flops, bytes_accessed=flops // 500, transcendentals=0),
        name=name,
    )


def local(
    frames, row_shift, row_frac, col_shift, col_frac,
    profile_cols, profile_rows, coef_table, weight_ids,
):
    frame = frames[0]
    side = frame.shape[0]
    nb = side // BLK
    nu, nv = profile_cols.shape[0], profile_rows.shape[0]
    nx, ny = lax.axis_size("skyx"), lax.axis_size("skyy")
    row_frac = row_frac.reshape(nb, BLK)
    col_frac = col_frac.reshape(nb, BLK)
    width = nu * 160
    kept = side - 2 * ROW0
    inner = side - 2 * BLK
    cells = nb * nb
    shape = jax.ShapeDtypeStruct
    to_right, to_left, to_up, to_down = call(
        functools.partial(pack_kernel, nb), "pack",
        (shape((side + 8, BLK), F32),) * 2 + (shape((8, BLK), F32),) * 2,
        [VM] * 3 + [SM] * 2,
    )(frame, row_frac, col_frac, row_shift, col_shift)
    left = moved(to_right, (0, 0, 1), (0,))
    right = moved(to_left, (0, 0, -1), (0,))
    meta_up = moved(to_down, (0, 1, 0), (0,))
    meta_down = moved(to_up, (0, -1, 0), (0,))
    depth = row_start(nb, nb)
    own_mid, mid, *parts, kernels, band = call(
        functools.partial(center_kernel, nb, nu, nv), "center",
        (shape((side, inner), BF16), shape((kept, inner), BF16))
        + (shape((side, side), BF16),) * 2
        + (shape((side, inner), BF16),) * 2
        + (shape((depth, BLK), BF16),) * 2
        + (shape((4 * BLK, BLK), BF16),) * 2
        + (shape((cells, BLK, width), BF16), shape((nu * BLK, 3 * BLK), BF16)),
        [VM] * 3 + [SM] * 2 + [VM] * 3 + [SM],
        [pltpu.VMEM((cells, nu * nv), F32), pltpu.VMEM((8, width), F32)],
        flops=1 << 30,
    )(frame, row_frac, col_frac, row_shift, col_shift, profile_cols, profile_rows, coef_table, weight_ids)
    mid = moved(mid, (1, 0, 0), (0,))
    own_end, end, to_up, to_down = call(
        functools.partial(edge_kernel, nb, nx, ny), "edges",
        (shape((side, 2 * BLK), BF16), shape((kept + 128, side // 2), BF16))
        + (shape((BLK + 16, side), BF16),) * 2,
        [VM] * 12,
        [pltpu.VMEM((side, 3 * BLK), BF16)] * 2,
        flops=1 << 30,
    )(left, right, meta_up, meta_down, *parts)
    end = moved(end, (1, 0, 0), (0,))
    side_down = moved(to_up, (1, -1, 0), (0,))
    side_up = moved(to_down, (1, 1, 0), (0,))
    got_down = moved(to_up, (0, -1, 0), (0,))
    got_up = moved(to_down, (0, 1, 0), (0,))
    result = call(
        functools.partial(finish_kernel, nb, nu), "finish",
        shape((side, side), F32),
        [VM] * 11,
        [pltpu.VMEM((side + 32, side + 2 * BLK), BF16), pltpu.VMEM((nu, side + 32, side), BF16)],
        flops=1 << 30,
    )(frame, own_mid, own_end, side_up, side_down, mid, end, kernels, band, got_up, got_down)
    return result[None]


def solution(mesh):
    placed = (
        P("segment", "skyx", "skyy"), P("skyx"), P("skyx"), P("skyy"), P("skyy"),
        P(), P(), P(), P("skyx", "skyy"),
    )
    return jax.shard_map(
        local, mesh=mesh, in_specs=placed, out_specs=P("segment", "skyx", "skyy"), check_vma=False
    )
```

time: 54.4 us -> 43.8 us (0.81)
  the two profiles are of different devices: /device:TPU:11 before, /device:TPU:14 now
where the time goes in v2:
time: 43.8 us; the launch traced here: 43.1 us
  waiting for transfers between devices  21.4 us (49%)
  starting transfers between devices  9.31 us (21%)
  local copies, waits for them, and re-layouts  6.63 us (15%)
  Pallas kernels  5.58 us (13%)
    ppermute x10, waiting for transfers between devices, moved(): return lax.ppermute(block, axes, route)  21.4 us
    ppermute x10, starting transfers between devices, moved(): return lax.ppermute(block, axes, route)  9.31 us
    unnamed x20, local copies, waits for them, and re-layouts  6.63 us
    pallas_call x1, Pallas kernels, local(): call(functools.partial(finish_kernel, nb, nu), 'finish', shape((side, sid...  3.3 us
    pallas_call x1, Pallas kernels, local(): call(functools.partial(center_kernel, nb, nu, nv), 'center', (shape((side...  1.71 us
  transfers between devices with their start and end apart: 10, of which 3 were waited for; matrix products, arithmetic and copies ran while one was open for 0% of the time, Pallas kernels for 4%

profile of v2, /device:TPU:14, one launch (start us, length us, event | category | flops | bytes accessed | tf_op | source)
XLA Modules:
  0.0 43.1 jit_solution(9730350588704722822)
XLA Ops:
  0.0 0.0 copy-start
  0.0 1.2 %copy-done = f32[1,512,512]{2,1,0:T(8,128)S(1)} copy-done((f32[1,512,512]{2,1,0:T(8,128)S(1)}, f32[1,512,512]{2,1,0:T(8,128)}, u32[]{:S(2)}) %copy-start) | copy-done | bytes 1048600
  1.2 0.0 copy-start.2
  1.2 0.7 %copy-done.2 = f32[512]{0:T(512)S(1)} copy-done((f32[512]{0:T(512)S(1)}, f32[512]{0:T(512)}, u32[]{:S(2)}) %copy-start.2) | copy-done | bytes 2072
  1.9 0.0 copy-start.3
  1.9 0.7 %copy-done.3 = f32[512]{0:T(512)S(1)} copy-done((f32[512]{0:T(512)S(1)}, f32[512]{0:T(512)}, u32[]{:S(2)}) %copy-start.3) | copy-done | bytes 2072
  2.6 0.0 copy-start.4
  2.6 0.7 %copy-done.4 = s32[4]{0:T(128)S(1)} copy-done((s32[4]{0:T(128)S(1)}, s32[4]{0:T(128)}, u32[]{:S(2)}) %copy-start.4) | copy-done | bytes 40
  3.2 0.0 copy-start.5
  3.2 0.7 %copy-done.5 = s32[4]{0:T(128)S(1)} copy-done((s32[4]{0:T(128)S(1)}, s32[4]{0:T(128)}, u32[]{:S(2)}) %copy-start.5) | copy-done | bytes 40
  3.9 0.6 %pack.1 = (f32[520,128]{1,0:T(8,128)S(1)}, f32[520,128]{1,0:T(8,128)S(1)}, f32[8,128]{1,0:T(8,128)S(1)}, f32[8,128]{1,0:T(8,128)S(1)}) custom-call(f32[512,512]{1,0:T(8,128)S(1)} %bitcast.4, f32[4,128]{1,0:T(4,128)S(1)} %bitcast.7, f32[4,128]{1,0:T(4,128)S(1)} %bitcast.9, s32[4]{0:T(128)S(1)} %copy-done.4, s32[4]{0:T(128)S(1)} %copy-done.5), custom_call_target="tpu_custom_call" | custom-call | tf_op jit(solution)/shard_map/pack/pallas_call | solution.py:368
  4.5 0.7 %collective-permute-start = (f32[520,128]{1,0:T(8,128)S(1)}, f32[520,128]{1,0:T(8,128)S(1)}, u32[]{:S(2)}, u32[]{:S(2)}) collective-permute-start(f32[520,128]{1,0:T(8,128)S(1)} %get-tuple-element.26), channel_id=1, source_target_pairs={{0,1},{1,2},{2,3},{4,5},{5,6},{6,7},{8,9},{9,10},{10,11},{12,13},{... | collective-permute-start | bytes 798728 | tf_op jit(solution)/shard_map/ppermute | solution.py:33
  5.2 0.7 %collective-permute-start.1 = (f32[520,128]{1,0:T(8,128)S(1)}, f32[520,128]{1,0:T(8,128)S(1)}, u32[]{:S(2)}, u32[]{:S(2)}) collective-permute-start(f32[520,128]{1,0:T(8,128)S(1)} %get-tuple-element.27), channel_id=1, source_target_pairs={{1,0},{2,1},{3,2},{5,4},{6,5},{7,6},{9,8},{10,9},{11,10},{13,12},{... | collective-permute-start | bytes 798728 | tf_op jit(solution)/shard_map/ppermute | solution.py:33
  5.8 0.7 %collective-permute-start.2 = (f32[8,128]{1,0:T(8,128)S(1)}, f32[8,128]{1,0:T(8,128)S(1)}, u32[]{:S(2)}, u32[]{:S(2)}) collective-permute-start(f32[8,128]{1,0:T(8,128)S(1)} %get-tuple-element.28), channel_id=1, source_target_pairs={{0,4},{1,5},{2,6},{3,7},{4,8},{5,9},{6,10},{7,11},{8,12},{9,13},{1... | collective-permute-start | bytes 12296 | tf_op jit(solution)/shard_map/ppermute | solution.py:33
  6.5 0.7 %collective-permute-start.3 = (f32[8,128]{1,0:T(8,128)S(1)}, f32[8,128]{1,0:T(8,128)S(1)}, u32[]{:S(2)}, u32[]{:S(2)}) collective-permute-start(f32[8,128]{1,0:T(8,128)S(1)} %get-tuple-element.29), channel_id=1, source_target_pairs={{4,0},{5,1},{6,2},{7,3},{8,4},{9,5},{10,6},{11,7},{12,8},{13,9},{1... | collective-permute-start | bytes 12296 | tf_op jit(solution)/shard_map/ppermute | solution.py:33
  7.2 0.0 copy-start.6
  7.2 0.7 %copy-done.6 = f32[16,32]{1,0:T(8,128)S(1)} copy-done((f32[16,32]{1,0:T(8,128)S(1)}, f32[16,32]{1,0:T(8,128)}, u32[]{:S(2)}) %copy-start.6) | copy-done | bytes 2072
  7.9 0.0 copy-start.7
  7.9 0.7 %copy-done.7 = bf16[8,31]{1,0:T(8,128)(2,1)S(1)} copy-done((bf16[8,31]{1,0:T(8,128)(2,1)S(1)}, bf16[8,31]{1,0:T(8,128)(2,1)}, u32[]{:S(2)}) %copy-start.7) | copy-done | bytes 520
  8.6 0.0 copy-start.8
  8.6 0.7 %copy-done.8 = s32[4,4]{1,0:T(4,128)S(1)} copy-done((s32[4,4]{1,0:T(4,128)S(1)}, s32[4,4]{1,0:T(4,128)}, u32[]{:S(2)}) %copy-start.8) | copy-done | bytes 88
  9.2 0.0 copy-start.9
  9.2 0.7 %copy-done.9 = bf16[4,31]{1,0:T(4,128)(2,1)S(1)} copy-done((bf16[4,31]{1,0:T(4,128)(2,1)S(1)}, bf16[4,31]{1,0:T(4,128)(2,1)}, u32[]{:S(2)}) %copy-start.9) | copy-done | bytes 272
  9.9 1.7 %center.1 = (bf16[512,256]{1,0:T(8,128)(2,1)S(1)}, bf16[416,256]{1,0:T(8,128)(2,1)S(1)}, bf16[512,512]{1,0:T(8,128)(2,1)S(1)}, bf16[512,512]{1,0:T(8,128)(2,1)S(...) custom-call(f32[512,512]{1,0:T(8,128)S(1)} %bitcast.5, ...), custom_call_target="tpu_custom_call" | custom-call | flops 1073741824 | bytes 2147483 | tf_op jit(solution)/shard_map/center/pallas_call | solution.py:378
  11.6 0.0 copy-start.1
  11.7 1.4 %collective-permute-start.6 = (bf16[416,256]{1,0:T(8,128)(2,1)S(1)}, bf16[416,256]{1,0:T(8,128)(2,1)S(1)}, u32[]{:S(2)}, u32[]{:S(2)}) collective-permute-start(bf16[416,256]{1,0:T(8,128)(2,1)S(1)} %get-tuple-element.41), channel_id=1, source_target_pairs={{0,16},{1,17},{2,18},{3,19},{4,20},{5,21},{6,22},{7,23},{8,24},{9,... | collective-permute-start | bytes 638984 | tf_op jit(solution)/shard_map/ppermute | solution.py:33
  13.1 0.0 collective-permute-done.2.meta_up
  13.1 0.0 collective-permute-done.3.meta_down
  13.1 0.0 collective-permute-done.left
  13.1 0.0 collective-permute-done.1.right
  13.2 1.3 %collective-permute-start.7 = (bf16[544,256]{1,0:T(8,128)(2,1)S(1)}, bf16[544,256]{1,0:T(8,128)(2,1)S(1)}, u32[]{:S(2)}, u32[]{:S(2)}) collective-permute-start(bf16[544,256]{1,0:T(8,128)(2,1)S(1)} %get-tuple-element.42), channel_id=1, source_target_pairs={{0,16},{1,17},{2,18},{3,19},{4,20},{5,21},{6,22},{7,23},{8,24},{9,... | collective-permute-start | bytes 835592 | tf_op jit(solution)/shard_map/ppermute | solution.py:33
  14.5 0.7 %collective-permute-start.8 = (bf16[144,512]{1,0:T(8,128)(2,1)S(1)}, bf16[144,512]{1,0:T(8,128)(2,1)S(1)}, u32[]{:S(2)}, u32[]{:S(2)}) collective-permute-start(bf16[144,512]{1,0:T(8,128)(2,1)S(1)} %get-tuple-element.39), channel_id=1, source_target_pairs={{0,4},{1,5},{2,6},{3,7},{4,8},{5,9},{6,10},{7,11},{8,12},{9,13},{1... | collective-permute-start | bytes 442376 | tf_op jit(solution)/shard_map/ppermute | solution.py:33
  15.1 1.3 %collective-permute-start.4 = (bf16[144,512]{1,0:T(8,128)(2,1)S(1)}, bf16[144,512]{1,0:T(8,128)(2,1)S(1)}, u32[]{:S(2)}, u32[]{:S(2)}) collective-permute-start(bf16[144,512]{1,0:T(8,128)(2,1)S(1)} %get-tuple-element.39), channel_id=1, source_target_pairs={{0,20},{1,21},{2,22},{3,23},{4,24},{5,25},{6,26},{7,27},{8,28},{9,... | collective-permute-start | bytes 442376 | tf_op jit(solution)/shard_map/ppermute | solution.py:33
  16.4 0.7 %collective-permute-start.9 = (bf16[144,512]{1,0:T(8,128)(2,1)S(1)}, bf16[144,512]{1,0:T(8,128)(2,1)S(1)}, u32[]{:S(2)}, u32[]{:S(2)}) collective-permute-start(bf16[144,512]{1,0:T(8,128)(2,1)S(1)} %get-tuple-element.40), channel_id=1, source_target_pairs={{4,0},{5,1},{6,2},{7,3},{8,4},{9,5},{10,6},{11,7},{12,8},{13,9},{1... | collective-permute-start | bytes 442376 | tf_op jit(solution)/shard_map/ppermute | solution.py:33
  17.1 11.1 %collective-permute-done.6.mid = bf16[416,256]{1,0:T(8,128)(2,1)S(1)} collective-permute-done((bf16[416,256]{1,0:T(8,128)(2,1)S(1)}, bf16[416,256]{1,0:T(8,128)(2,1)S(1)}, u32[]{:S(2)}, u32[]{:S(2)}) %collective-permute-start.6) | collective-permute-done | bytes 213024 | tf_op jit(solution)/shard_map/ppermute | solution.py:33
  28.2 1.3 %collective-permute-start.5 = (bf16[144,512]{1,0:T(8,128)(2,1)S(1)}, bf16[144,512]{1,0:T(8,128)(2,1)S(1)}, u32[]{:S(2)}, u32[]{:S(2)}) collective-permute-start(bf16[144,512]{1,0:T(8,128)(2,1)S(1)} %get-tuple-element.40), channel_id=1, source_target_pairs={{4,16},{5,17},{6,18},{7,19},{8,20},{9,21},{10,22},{11,23},{12,24},... | collective-permute-start | bytes 442376 | tf_op jit(solution)/shard_map/ppermute | solution.py:33
  29.5 0.0 collective-permute-done.8.got_up
  29.5 5.9 %collective-permute-done.4.side_up = bf16[144,512]{1,0:T(8,128)(2,1)S(1)} collective-permute-done((bf16[144,512]{1,0:T(8,128)(2,1)S(1)}, bf16[144,512]{1,0:T(8,128)(2,1)S(1)}, u32[]{:S(2)}, u32[]{:S(2)}) %collective-permute-start.4) | collective-permute-done | bytes 147488 | tf_op jit(solution)/shard_map/ppermute | solution.py:33
  35.4 0.0 collective-permute-done.9.got_down
  35.4 4.4 %collective-permute-done.5.side_down = bf16[144,512]{1,0:T(8,128)(2,1)S(1)} collective-permute-done((bf16[144,512]{1,0:T(8,128)(2,1)S(1)}, bf16[144,512]{1,0:T(8,128)(2,1)S(1)}, u32[]{:S(2)}, u32[]{:S(2)}) %collective-permute-start.5) | collective-permute-done | bytes 147488 | tf_op jit(solution)/shard_map/ppermute | solution.py:33
  39.8 0.0 collective-permute-done.7.end
  39.8 0.0 copy-done.1
  39.8 3.3 %finish.1 = f32[512,512]{1,0:T(8,128)} custom-call(f32[512,512]{1,0:T(8,128)S(1)} %bitcast.6, bf16[512,256]{1,0:T(8,128)(2,1)S(1)} %get-tuple-element.25.own_mid, bf16[512,256]{1,0:T(8,128)(2,1)S(1)} %get-tuple-element.38.own_end, bf16[144,512]{1,0:T(8,128)(2,1)S(1)} %collective-permute-done.4.side_up, ...), custom_call_target="tpu_custom_call" | custom-call | flops 1073741824 | bytes 2147483 | tf_op jit(solution)/shard_map/finish/pallas_call | solution.py:404
  (1 shorter events, 0.0 us)
Async XLA Ops:
  0.0 1.2 %copy-start = (f32[1,512,512]{2,1,0:T(8,128)S(1)}, f32[1,512,512]{2,1,0:T(8,128)}, u32[]{:S(2)}) copy-start(f32[1,512,512]{2,1,0:T(8,128)} %param.9) | copy-start | bytes 3145732
  1.2 0.7 %copy-start.2 = (f32[512]{0:T(512)S(1)}, f32[512]{0:T(512)}, u32[]{:S(2)}) copy-start(f32[512]{0:T(512)} %param.11) | copy-start | bytes 6148
  1.9 0.7 %copy-start.3 = (f32[512]{0:T(512)S(1)}, f32[512]{0:T(512)}, u32[]{:S(2)}) copy-start(f32[512]{0:T(512)} %param.13) | copy-start | bytes 6148
  2.6 0.7 %copy-start.4 = (s32[4]{0:T(128)S(1)}, s32[4]{0:T(128)}, u32[]{:S(2)}) copy-start(s32[4]{0:T(128)} %row_shift.3) | copy-start | bytes 52
  3.2 0.7 %copy-start.5 = (s32[4]{0:T(128)S(1)}, s32[4]{0:T(128)}, u32[]{:S(2)}) copy-start(s32[4]{0:T(128)} %col_shift.3) | copy-start | bytes 52
  4.5 8.6 %collective-permute-start = (f32[520,128]{1,0:T(8,128)S(1)}, f32[520,128]{1,0:T(8,128)S(1)}, u32[]{:S(2)}, u32[]{:S(2)}) collective-permute-start(f32[520,128]{1,0:T(8,128)S(1)} %get-tuple-element.26), channel_id=1, source_target_pairs={{0,1},{1,2},{2,3},{4,5},{5,6},{6,7},{8,9},{9,10},{10,11},{12,13},{... | collective-permute-start | bytes 798728 | tf_op jit(solution)/shard_map/ppermute | solution.py:33
  5.2 8.0 %collective-permute-start.1 = (f32[520,128]{1,0:T(8,128)S(1)}, f32[520,128]{1,0:T(8,128)S(1)}, u32[]{:S(2)}, u32[]{:S(2)}) collective-permute-start(f32[520,128]{1,0:T(8,128)S(1)} %get-tuple-element.27), channel_id=1, source_target_pairs={{1,0},{2,1},{3,2},{5,4},{6,5},{7,6},{9,8},{10,9},{11,10},{13,12},{... | collective-permute-start | bytes 798728 | tf_op jit(solution)/shard_map/ppermute | solution.py:33
  5.8 7.2 %collective-permute-start.2 = (f32[8,128]{1,0:T(8,128)S(1)}, f32[8,128]{1,0:T(8,128)S(1)}, u32[]{:S(2)}, u32[]{:S(2)}) collective-permute-start(f32[8,128]{1,0:T(8,128)S(1)} %get-tuple-element.28), channel_id=1, source_target_pairs={{0,4},{1,5},{2,6},{3,7},{4,8},{5,9},{6,10},{7,11},{8,12},{9,13},{1... | collective-permute-start | bytes 12296 | tf_op jit(solution)/shard_map/ppermute | solution.py:33
  6.5 6.6 %collective-permute-start.3 = (f32[8,128]{1,0:T(8,128)S(1)}, f32[8,128]{1,0:T(8,128)S(1)}, u32[]{:S(2)}, u32[]{:S(2)}) collective-permute-start(f32[8,128]{1,0:T(8,128)S(1)} %get-tuple-element.29), channel_id=1, source_target_pairs={{4,0},{5,1},{6,2},{7,3},{8,4},{9,5},{10,6},{11,7},{12,8},{13,9},{1... | collective-permute-start | bytes 12296 | tf_op jit(solution)/shard_map/ppermute | solution.py:33
  7.2 0.7 %copy-start.6 = (f32[16,32]{1,0:T(8,128)S(1)}, f32[16,32]{1,0:T(8,128)}, u32[]{:S(2)}) copy-start(f32[16,32]{1,0:T(8,128)} %table.1) | copy-start | bytes 6148
  7.9 0.7 %copy-start.7 = (bf16[8,31]{1,0:T(8,128)(2,1)S(1)}, bf16[8,31]{1,0:T(8,128)(2,1)}, u32[]{:S(2)}) copy-start(bf16[8,31]{1,0:T(8,128)(2,1)} %prof_rows.1) | copy-start | bytes 1492
  8.6 0.7 %copy-start.8 = (s32[4,4]{1,0:T(4,128)S(1)}, s32[4,4]{1,0:T(4,128)}, u32[]{:S(2)}) copy-start(s32[4,4]{1,0:T(4,128)} %ids.1) | copy-start | bytes 196
  9.2 0.7 %copy-start.9 = (bf16[4,31]{1,0:T(4,128)(2,1)S(1)}, bf16[4,31]{1,0:T(4,128)(2,1)}, u32[]{:S(2)}) copy-start(bf16[4,31]{1,0:T(4,128)(2,1)} %prof_cols.1) | copy-start | bytes 748
  11.6 28.1 %copy-start.1 = (f32[1,512,512]{2,1,0:T(8,128)S(1)}, f32[1,512,512]{2,1,0:T(8,128)}, u32[]{:S(2)}) copy-start(f32[1,512,512]{2,1,0:T(8,128)} %param.9) | copy-start | bytes 3145732
  11.7 16.6 %collective-permute-start.6 = (bf16[416,256]{1,0:T(8,128)(2,1)S(1)}, bf16[416,256]{1,0:T(8,128)(2,1)S(1)}, u32[]{:S(2)}, u32[]{:S(2)}) collective-permute-start(bf16[416,256]{1,0:T(8,128)(2,1)S(1)} %get-tuple-element.41), channel_id=1, source_target_pairs={{0,16},{1,17},{2,18},{3,19},{4,20},{5,21},{6,22},{7,23},{8,24},{9,... | collective-permute-start | bytes 638984 | tf_op jit(solution)/shard_map/ppermute | solution.py:33
  13.2 26.6 %collective-permute-start.7 = (bf16[544,256]{1,0:T(8,128)(2,1)S(1)}, bf16[544,256]{1,0:T(8,128)(2,1)S(1)}, u32[]{:S(2)}, u32[]{:S(2)}) collective-permute-start(bf16[544,256]{1,0:T(8,128)(2,1)S(1)} %get-tuple-element.42), channel_id=1, source_target_pairs={{0,16},{1,17},{2,18},{3,19},{4,20},{5,21},{6,22},{7,23},{8,24},{9,... | collective-permute-start | bytes 835592 | tf_op jit(solution)/shard_map/ppermute | solution.py:33
  14.5 15.1 %collective-permute-start.8 = (bf16[144,512]{1,0:T(8,128)(2,1)S(1)}, bf16[144,512]{1,0:T(8,128)(2,1)S(1)}, u32[]{:S(2)}, u32[]{:S(2)}) collective-permute-start(bf16[144,512]{1,0:T(8,128)(2,1)S(1)} %get-tuple-element.39), channel_id=1, source_target_pairs={{0,4},{1,5},{2,6},{3,7},{4,8},{5,9},{6,10},{7,11},{8,12},{9,13},{1... | collective-permute-start | bytes 442376 | tf_op jit(solution)/shard_map/ppermute | solution.py:33
  15.1 20.3 %collective-permute-start.4 = (bf16[144,512]{1,0:T(8,128)(2,1)S(1)}, bf16[144,512]{1,0:T(8,128)(2,1)S(1)}, u32[]{:S(2)}, u32[]{:S(2)}) collective-permute-start(bf16[144,512]{1,0:T(8,128)(2,1)S(1)} %get-tuple-element.39), channel_id=1, source_target_pairs={{0,20},{1,21},{2,22},{3,23},{4,24},{5,25},{6,26},{7,27},{8,28},{9,... | collective-permute-start | bytes 442376 | tf_op jit(solution)/shard_map/ppermute | solution.py:33
  16.4 19.0 %collective-permute-start.9 = (bf16[144,512]{1,0:T(8,128)(2,1)S(1)}, bf16[144,512]{1,0:T(8,128)(2,1)S(1)}, u32[]{:S(2)}, u32[]{:S(2)}) collective-permute-start(bf16[144,512]{1,0:T(8,128)(2,1)S(1)} %get-tuple-element.40), channel_id=1, source_target_pairs={{4,0},{5,1},{6,2},{7,3},{8,4},{9,5},{10,6},{11,7},{12,8},{13,9},{1... | collective-permute-start | bytes 442376 | tf_op jit(solution)/shard_map/ppermute | solution.py:33
  28.2 11.5 %collective-permute-start.5 = (bf16[144,512]{1,0:T(8,128)(2,1)S(1)}, bf16[144,512]{1,0:T(8,128)(2,1)S(1)}, u32[]{:S(2)}, u32[]{:S(2)}) collective-permute-start(bf16[144,512]{1,0:T(8,128)(2,1)S(1)} %get-tuple-element.40), channel_id=1, source_target_pairs={{4,16},{5,17},{6,18},{7,19},{8,20},{9,21},{10,22},{11,23},{12,24},... | collective-permute-start | bytes 442376 | tf_op jit(solution)/shard_map/ppermute | solution.py:33

commit v3 on v2

--- a/solution.py
+++ b/solution.py
@@ -16,7 +16,8 @@
 BF16 = jnp.bfloat16
 HIGHEST = lax.Precision.HIGHEST
 VM = pl.BlockSpec(memory_space=pltpu.VMEM)
-SM = pl.BlockSpec(memory_space=pltpu.SMEM)
+ANY = pl.BlockSpec(memory_space=pl.ANY)
+FULL = 64 << 20
 
 
 def moved(block, step, sources):
@@ -91,32 +92,54 @@
     return slice(first * BLK, first * BLK + row_depth(b, nb))
 
 
-def pack_kernel(nb, frame, row_frac, col_frac, row_shift, col_shift, to_right, to_left, to_up, to_down):
-    side = nb * BLK
-
-    @pl.when(lax.axis_index("segment") == 0)
-    def _():
-        for out, lane, b in ((to_right, side - BLK, nb - 1), (to_left, 0, 0)):
-            out[:side, :] = frame[:, lane : lane + BLK]
-            out[side : side + 1, :] = col_frac[b : b + 1, :]
-            out[side + 1 : side + 2, :] = jnp.full((1, BLK), col_shift[b].astype(F32))
-        for out, b in ((to_up, 0), (to_down, nb - 1)):
-            out[0:1, :] = row_frac[b : b + 1, :]
-            out[1:2, :] = jnp.full((1, BLK), row_shift[b].astype(F32))
-
-
-def center_kernel(
-    nb, nu, nv,
-    frame, row_frac, col_frac, row_shift, col_shift, prof_cols, prof_rows, table, ids,
-    own, across, src_hi, src_lo, mid_hi, mid_lo, row_hi, row_lo, edge_hi, edge_lo, kernels, band,
-    coefs, padded,
+def gather_kernel(
+    nb, frame, row_frac, col_frac, row_shift, col_shift, table, prof_rows, prof_cols, ids,
+    meta, row_meta, to_right, to_left,
+    table_v, rows_v, cols_v, ids_v, row_s, col_s, sems,
 ):
     side = nb * BLK
-    warper = lax.axis_index("segment") == 0
-
-    @pl.when(warper)
-    def _():
-        weights = taps([col_frac[b : b + 1, :] for b in range(nb)] + [row_frac[b : b + 1, :] for b in range(nb)])
+    pairs = (
+        (row_frac, meta.at[0:nb, :]),
+        (col_frac, meta.at[2 * nb : 3 * nb, :]),
+        (row_shift, row_s),
+        (col_shift, col_s),
+        (table, table_v),
+        (prof_rows, rows_v),
+        (prof_cols, cols_v),
+        (ids, ids_v),
+        (frame.at[:, side - BLK :], to_right.at[:side, :]),
+        (frame.at[:, :BLK], to_left.at[:side, :]),
+    )
+    copies = [pltpu.make_async_copy(src, dst, sems.at[n]) for n, (src, dst) in enumerate(pairs)]
+    for copy in copies:
+        copy.start()
+    for copy in copies:
+        copy.wait()
+    for b in range(nb):
+        meta[nb + b : nb + b + 1, :] = jnp.full((1, BLK), row_s[b].astype(F32))
+        meta[3 * nb + b : 3 * nb + b + 1, :] = jnp.full((1, BLK), col_s[b].astype(F32))
+    base = 4 * nb
+    for part in (table_v, rows_v, cols_v, ids_v):
+        meta[base : base + part.shape[0], : part.shape[1]] = part[...].astype(F32)
+        base += part.shape[0]
+    row_meta[...] = meta[: 2 * nb, :]
+    for out, b in ((to_right, nb - 1), (to_left, 0)):
+        out[side : side + 1, :] = meta[2 * nb + b : 2 * nb + b + 1, :]
+        out[side + 1 : side + 2, :] = meta[3 * nb + b : 3 * nb + b + 1, :]
+
+
+def center_kernel(
+    nb, frame, meta,
+    own, across, src_hi, src_lo, mid_hi, mid_lo, row_hi, row_lo, edge_hi, edge_lo,
+):
+    side = nb * BLK
+
+    @pl.when(lax.axis_index("segment") == 0)
+    def _():
+        fracs = [meta[2 * nb + b : 2 * nb + b + 1, :] for b in range(nb)]
+        weights = taps(fracs + [meta[b : b + 1, :] for b in range(nb)])
+        col_shift = [meta[3 * nb + b : 3 * nb + b + 1, :].astype(jnp.int32) for b in range(nb)]
+        row_shift = [meta[nb + b : nb + b + 1, :].astype(jnp.int32) for b in range(nb)]
         hi, lo = split(frame[...])
         src_hi[...] = hi
         src_lo[...] = lo
@@ -144,25 +167,39 @@
             edge_hi[n * 2 * BLK : (n + 1) * 2 * BLK, :] = hi
             edge_lo[n * 2 * BLK : (n + 1) * 2 * BLK, :] = lo
 
-    @pl.when(jnp.logical_not(warper))
-    def _():
+
+def matrices_kernel(nb, nu, nv, sets, meta, after, kernels, band, padded):
+    @pl.when(lax.axis_index("segment") != 0)
+    def _():
+        base = 4 * nb
+        table = meta[base : base + sets, : nu * nv]
+        base += sets
+        prof_rows = meta[base : base + nv, :KW]
+        base += nv
+        prof_cols = meta[base : base + nu, :KW]
+        base += nu
+        entry = lax.broadcasted_iota(jnp.int32, (1, sets), 1)
+        cells = []
         for bi in range(nb):
             for bj in range(nb):
-                cell = bi * nb + bj
-                coefs[cell : cell + 1, :] = table[pl.ds(ids[bi, bj], 1), :]
+                chosen = jnp.broadcast_to(meta[base + bi : base + bi + 1, bj : bj + 1], (1, sets))
+                cells.append((chosen.astype(jnp.int32) == entry).astype(F32))
+        coefs = jnp.dot(
+            jnp.concatenate(cells, axis=0), table, precision=HIGHEST, preferred_element_type=F32
+        )
         width = nu * 160
         padded[...] = jnp.zeros_like(padded)
-        padded[0:nv, 0:KW] = prof_rows[...].astype(F32)
+        padded[0:nv, 0:KW] = prof_rows
         profile = padded[0:nv, :]
         spread = jnp.concatenate(
             [pltpu.roll(profile, p * 160 + 1, 1) for p in range(nu)], axis=0
         )
-        base = jnp.dot(coefs[...], spread, precision=HIGHEST, preferred_element_type=F32)
+        base = jnp.dot(coefs, spread, precision=HIGHEST, preferred_element_type=F32)
         for cell in range(nb * nb):
             row = jnp.broadcast_to(base[cell : cell + 1, :], (BLK, width))
             kernels[cell] = pltpu.roll(row, 0, 1, stride=1, stride_axis=0).astype(BF16)
         padded[...] = jnp.zeros_like(padded)
-        padded[0:nu, 0:KW] = prof_cols[...].astype(F32)
+        padded[0:nu, 0:KW] = prof_cols
         for p in range(nu):
             row = jnp.broadcast_to(padded[p : p + 1, : 3 * BLK], (BLK, 3 * BLK))
             band[p * BLK : (p + 1) * BLK, :] = pltpu.roll(
@@ -185,10 +222,10 @@
     @pl.when(lax.axis_index("segment") == 0)
     def _():
         lanes = lax.broadcasted_iota(jnp.int32, (8, BLK), 1)
-        weights = taps([left[side : side + 1, :], right[side : side + 1, :], meta_up[0:1, :], meta_down[0:1, :]])
+        weights = taps([left[side : side + 1, :], right[side : side + 1, :], meta_up[nb - 1 : nb, :], meta_down[0:1, :]])
         shifts = [
             part[row : row + 1, :].astype(jnp.int32)
-            for part, row in ((left, side + 1), (right, side + 1), (meta_up, 1), (meta_down, 1))
+            for part, row in ((left, side + 1), (right, side + 1), (meta_up, 2 * nb - 1), (meta_down, nb))
         ]
         parts = [split(left[:side, :]), split(right[:side, :])]
         for n, col in ((0, 0), (1, side - BLK)):
@@ -250,6 +287,13 @@
             across[base + 16 : base + 32, lane : lane + BLK] = turned[BLK - 16 :].astype(BF16)
 
 
+def relay_kernel(up_in, down_in, end_in, up, down):
+    @pl.when(lax.axis_index("segment") == 0)
+    def _():
+        up[...] = up_in[:BLK, :]
+        down[...] = down_in[:BLK, :]
+
+
 def finish_kernel(
     nb, nu,
     frame, own_mid, own_end, side_up, side_down, mid, end, kernels, band, got_up, got_down,
@@ -335,7 +379,7 @@
                 out[rows, cols] = frame[rows, cols] - total
 
 
-def call(kernel, name, out_shape, in_specs, scratch=(), flops=0):
+def call(kernel, name, out_shape, in_specs, scratch=(), flops=0, limit=40 << 20):
     many = isinstance(out_shape, tuple)
     return pl.pallas_call(
         kernel,
@@ -343,7 +387,7 @@
         in_specs=in_specs,
         out_specs=(VM,) * len(out_shape) if many else VM,
         scratch_shapes=list(scratch),
-        compiler_params=pltpu.CompilerParams(vmem_limit_bytes=40 << 20),
+        compiler_params=pltpu.CompilerParams(vmem_limit_bytes=limit),
         cost_estimate=pl.CostEstimate(flops=flops, bytes_accessed=flops // 500, transcendentals=0),
         name=name,
     )
@@ -358,35 +402,43 @@
     nb = side // BLK
     nu, nv = profile_cols.shape[0], profile_rows.shape[0]
     nx, ny = lax.axis_size("skyx"), lax.axis_size("skyy")
+    sets = coef_table.shape[0]
     row_frac = row_frac.reshape(nb, BLK)
     col_frac = col_frac.reshape(nb, BLK)
+
     width = nu * 160
     kept = side - 2 * ROW0
     inner = side - 2 * BLK
     cells = nb * nb
     shape = jax.ShapeDtypeStruct
-    to_right, to_left, to_up, to_down = call(
-        functools.partial(pack_kernel, nb), "pack",
-        (shape((side + 8, BLK), F32),) * 2 + (shape((8, BLK), F32),) * 2,
-        [VM] * 3 + [SM] * 2,
-    )(frame, row_frac, col_frac, row_shift, col_shift)
+    slab = shape((side + 8, BLK), F32)
+    total = 4 * nb + sets + nv + nu + nb
+    meta, row_meta, to_right, to_left = call(
+        functools.partial(gather_kernel, nb), "gather",
+        (shape((total + -total % 8, BLK), F32), shape((2 * nb, BLK), F32), slab, slab),
+        [ANY] * 9,
+        [
+            pltpu.VMEM(coef_table.shape, F32), pltpu.VMEM(profile_rows.shape, BF16),
+            pltpu.VMEM(profile_cols.shape, BF16), pltpu.VMEM(weight_ids.shape, jnp.int32),
+            pltpu.SMEM((nb,), jnp.int32), pltpu.SMEM((nb,), jnp.int32), pltpu.SemaphoreType.DMA((10,)),
+        ],
+        limit=FULL,
+    )(frame, row_frac, col_frac, row_shift, col_shift, coef_table, profile_rows, profile_cols, weight_ids)
+    meta_up = moved(row_meta, (-1, 1, 0), (1,))
+    meta_down = moved(row_meta, (-1, -1, 0), (1,))
     left = moved(to_right, (0, 0, 1), (0,))
     right = moved(to_left, (0, 0, -1), (0,))
-    meta_up = moved(to_down, (0, 1, 0), (0,))
-    meta_down = moved(to_up, (0, -1, 0), (0,))
     depth = row_start(nb, nb)
-    own_mid, mid, *parts, kernels, band = call(
-        functools.partial(center_kernel, nb, nu, nv), "center",
+    own_mid, mid, *parts = call(
+        functools.partial(center_kernel, nb), "center",
         (shape((side, inner), BF16), shape((kept, inner), BF16))
         + (shape((side, side), BF16),) * 2
         + (shape((side, inner), BF16),) * 2
         + (shape((depth, BLK), BF16),) * 2
-        + (shape((4 * BLK, BLK), BF16),) * 2
-        + (shape((cells, BLK, width), BF16), shape((nu * BLK, 3 * BLK), BF16)),
-        [VM] * 3 + [SM] * 2 + [VM] * 3 + [SM],
-        [pltpu.VMEM((cells, nu * nv), F32), pltpu.VMEM((8, width), F32)],
+        + (shape((4 * BLK, BLK), BF16),) * 2,
+        [VM] * 2,
         flops=1 << 30,
-    )(frame, row_frac, col_frac, row_shift, col_shift, profile_cols, profile_rows, coef_table, weight_ids)
+    )(frame, meta)
     mid = moved(mid, (1, 0, 0), (0,))
     own_end, end, to_up, to_down = call(
         functools.partial(edge_kernel, nb, nx, ny), "edges",
@@ -399,8 +451,18 @@
     end = moved(end, (1, 0, 0), (0,))
     side_down = moved(to_up, (1, -1, 0), (0,))
     side_up = moved(to_down, (1, 1, 0), (0,))
+    to_up, to_down = call(
+        relay_kernel, "relay", (shape((BLK, side), BF16),) * 2, [VM] * 3
+    )(to_up, to_down, own_end)
     got_down = moved(to_up, (0, -1, 0), (0,))
     got_up = moved(to_down, (0, 1, 0), (0,))
+    kernels, band = call(
+        functools.partial(matrices_kernel, nb, nu, nv, sets), "matrices",
+        (shape((cells, BLK, width), BF16), shape((nu * BLK, 3 * BLK), BF16)),
+        [VM] * 2,
+        [pltpu.VMEM((8, width), F32)],
+        flops=1 << 30,
+    )(meta, own_end)
     result = call(
         functools.partial(finish_kernel, nb, nu), "finish",
         shape((side, side), F32),

time: 43.8 us -> 38.1 us (0.87)
  waiting for transfers between devices: 21.4 us -> 11.9 us
  starting transfers between devices: 9.31 us -> 17.1 us
  local copies, waits for them, and re-layouts: 6.63 us -> 1.97 us
  Pallas kernels: 5.58 us -> 6.57 us
    ppermute x10, waiting for transfers between devices: 21.4 us -> 11.9 us  [moved(): return lax.ppermute(block, axes, route)]
    ppermute x10, starting transfers between devices: 9.31 us -> 17.1 us  [moved(): return lax.ppermute(block, axes, route)]
    unnamed x20 -> x8, local copies, waits for them, and re-layouts: 6.63 us -> 1.97 us
    pallas_call x2 -> x4, Pallas kernels: 2.27 us -> 3.36 us  [the longest x1 2.03 us: local(): call(functools.partial(gather_kernel, nb), 'gather', (shape((total + -tot...]
  transfers between devices with their start and end apart: 10 -> 10, of which waited for: 3 -> 2; matrix products, arithmetic and copies ran while one was open for 0% -> 0% of each run, Pallas kernels for 4% -> 4%
where the time goes in v3:
time: 38.1 us; the launch traced here: 37.7 us
  starting transfers between devices  17.1 us (45%)
  waiting for transfers between devices  11.9 us (31%)
  Pallas kernels  6.57 us (17%)
  local copies, waits for them, and re-layouts  1.97 us (5%)
    ppermute x10, starting transfers between devices, moved(): return lax.ppermute(block, axes, route)  17.1 us
    ppermute x10, waiting for transfers between devices, moved(): return lax.ppermute(block, axes, route)  11.9 us
    pallas_call x1, Pallas kernels, local(): call(functools.partial(finish_kernel, nb, nu), 'finish', shape((side, sid...  3.19 us
    pallas_call x1, Pallas kernels, local(): call(functools.partial(gather_kernel, nb), 'gather', (shape((total + -tot...  2.03 us
    unnamed x8, local copies, waits for them, and re-layouts  1.97 us
    pallas_call x1, Pallas kernels, local(): call(functools.partial(matrices_kernel, nb, nu, nv, sets), 'matrices', (s...  1.31 us
  transfers between devices with their start and end apart: 10, of which 2 were waited for; matrix products, arithmetic and copies ran while one was open for 0% of the time, Pallas kernels for 4%

profile of v3, /device:TPU:14, one launch (start us, length us, event | category | flops | bytes accessed | tf_op | source)
XLA Modules:
  0.0 37.7 jit_solution(585299097685133650)
XLA Ops:
  0.0 2.0 %gather.1 = (f32[48,128]{1,0:T(8,128)}, f32[8,128]{1,0:T(8,128)}, f32[520,128]{1,0:T(8,128)}, f32[520,128]{1,0:T(8,128)}) custom-call(f32[512,512]{1,0:T(8,128)} %bitcast.4, f32[4,128]{1,0:T(4,128)} %bitcast.7, f32[4,128]{1,0:T(4,128)} %bitcast.8, s32[4]{0:T(128)} %row_shift.1, s32[4]{0:T(128)} %col_shift.1, f32[16,32]{1,0:T(8,128)} %table.1, ...), custom_call_target="tpu_custom_call" | custom-call | tf_op jit(solution)/shard_map/gather/pallas_call | solution.py:416
  2.0 0.7 %collective-permute-start = (f32[520,128]{1,0:T(8,128)}, f32[520,128]{1,0:T(8,128)S(1)}, u32[]{:S(2)}, u32[]{:S(2)}) collective-permute-start(f32[520,128]{1,0:T(8,128)} %get-tuple-element.29), channel_id=1, source_target_pairs={{0,1},{1,2},{2,3},{4,5},{5,6},{6,7},{8,9},{9,10},{10,11},{12,13},{... | collective-permute-start | bytes 798728 | tf_op jit(solution)/shard_map/ppermute | solution.py:34
  2.7 0.7 %collective-permute-start.1 = (f32[520,128]{1,0:T(8,128)}, f32[520,128]{1,0:T(8,128)S(1)}, u32[]{:S(2)}, u32[]{:S(2)}) collective-permute-start(f32[520,128]{1,0:T(8,128)} %get-tuple-element.30), channel_id=1, source_target_pairs={{1,0},{2,1},{3,2},{5,4},{6,5},{7,6},{9,8},{10,9},{11,10},{13,12},{... | collective-permute-start | bytes 798728 | tf_op jit(solution)/shard_map/ppermute | solution.py:34
  3.4 6.5 %collective-permute-start.3 = (f32[8,128]{1,0:T(8,128)}, f32[8,128]{1,0:T(8,128)S(1)}, u32[]{:S(2)}, u32[]{:S(2)}) collective-permute-start(f32[8,128]{1,0:T(8,128)} %get-tuple-element.31), channel_id=1, source_target_pairs={{20,0},{21,1},{22,2},{23,3},{24,4},{25,5},{26,6},{27,7},{28,8},{29... | collective-permute-start | bytes 12296 | tf_op jit(solution)/shard_map/ppermute | solution.py:34
  9.9 2.4 %collective-permute-start.2 = (f32[8,128]{1,0:T(8,128)}, f32[8,128]{1,0:T(8,128)S(1)}, u32[]{:S(2)}, u32[]{:S(2)}) collective-permute-start(f32[8,128]{1,0:T(8,128)} %get-tuple-element.31), channel_id=1, source_target_pairs={{16,4},{17,5},{18,6},{19,7},{20,8},{21,9},{22,10},{23,11},{24,12},... | collective-permute-start | bytes 12296 | tf_op jit(solution)/shard_map/ppermute | solution.py:34
  12.4 0.0 copy-start
  12.4 1.2 %copy-done = f32[1,512,512]{2,1,0:T(8,128)S(1)} copy-done((f32[1,512,512]{2,1,0:T(8,128)S(1)}, f32[1,512,512]{2,1,0:T(8,128)}, u32[]{:S(2)}) %copy-start) | copy-done | bytes 1048600
  13.6 0.0 copy-start.2
  13.6 0.7 %copy-done.2 = f32[48,128]{1,0:T(8,128)S(1)} copy-done((f32[48,128]{1,0:T(8,128)S(1)}, f32[48,128]{1,0:T(8,128)}, u32[]{:S(2)}) %copy-start.2) | copy-done | bytes 24600
  14.3 0.0 copy-start.3
  14.3 1.4 %collective-permute-start.6 = (bf16[416,256]{1,0:T(8,128)(2,1)S(1)}, bf16[416,256]{1,0:T(8,128)(2,1)S(1)}, u32[]{:S(2)}, u32[]{:S(2)}) collective-permute-start(bf16[416,256]{1,0:T(8,128)(2,1)S(1)} %get-tuple-element.43), channel_id=1, source_target_pairs={{0,16},{1,17},{2,18},{3,19},{4,20},{5,21},{6,22},{7,23},{8,24},{9,... | collective-permute-start | bytes 638984 | tf_op jit(solution)/shard_map/ppermute | solution.py:34
  15.8 0.0 collective-permute-done.3.meta_down
  15.8 0.0 collective-permute-done.2.meta_up
  15.8 0.0 collective-permute-done.left
  15.8 0.0 collective-permute-done.1.right
  15.8 0.0 copy-start.1
  15.8 1.4 %collective-permute-start.7 = (bf16[544,256]{1,0:T(8,128)(2,1)S(1)}, bf16[544,256]{1,0:T(8,128)(2,1)S(1)}, u32[]{:S(2)}, u32[]{:S(2)}) collective-permute-start(bf16[544,256]{1,0:T(8,128)(2,1)S(1)} %get-tuple-element.44), channel_id=1, source_target_pairs={{0,16},{1,17},{2,18},{3,19},{4,20},{5,21},{6,22},{7,23},{8,24},{9,... | collective-permute-start | bytes 835592 | tf_op jit(solution)/shard_map/ppermute | solution.py:34
  17.3 1.3 %collective-permute-start.4 = (bf16[144,512]{1,0:T(8,128)(2,1)S(1)}, bf16[144,512]{1,0:T(8,128)(2,1)S(1)}, u32[]{:S(2)}, u32[]{:S(2)}) collective-permute-start(bf16[144,512]{1,0:T(8,128)(2,1)S(1)} %get-tuple-element.41.down_in), channel_id=1, source_target_pairs={{0,20},{1,21},{2,22},{3,23},{4,24},{5,25},{6,26},{7,27},{8,28},{9,... | collective-permute-start | bytes 442376 | tf_op jit(solution)/shard_map/ppermute | solution.py:34
  18.6 1.3 %collective-permute-start.5 = (bf16[144,512]{1,0:T(8,128)(2,1)S(1)}, bf16[144,512]{1,0:T(8,128)(2,1)S(1)}, u32[]{:S(2)}, u32[]{:S(2)}) collective-permute-start(bf16[144,512]{1,0:T(8,128)(2,1)S(1)} %get-tuple-element.42.up_in), channel_id=1, source_target_pairs={{4,16},{5,17},{6,18},{7,19},{8,20},{9,21},{10,22},{11,23},{12,24},... | collective-permute-start | bytes 442376 | tf_op jit(solution)/shard_map/ppermute | solution.py:34
  19.9 0.7 %collective-permute-start.8 = (bf16[128,512]{1,0:T(8,128)(2,1)S(1)}, bf16[128,512]{1,0:T(8,128)(2,1)S(1)}, u32[]{:S(2)}, u32[]{:S(2)}) collective-permute-start(bf16[128,512]{1,0:T(8,128)(2,1)S(1)} %get-tuple-element.47), channel_id=1, source_target_pairs={{0,4},{1,5},{2,6},{3,7},{4,8},{5,9},{6,10},{7,11},{8,12},{9,13},{1... | collective-permute-start | bytes 393224 | tf_op jit(solution)/shard_map/ppermute | solution.py:34
  20.6 9.2 %collective-permute-done.6.mid = bf16[416,256]{1,0:T(8,128)(2,1)S(1)} collective-permute-done((bf16[416,256]{1,0:T(8,128)(2,1)S(1)}, bf16[416,256]{1,0:T(8,128)(2,1)S(1)}, u32[]{:S(2)}, u32[]{:S(2)}) %collective-permute-start.6) | collective-permute-done | bytes 213024 | tf_op jit(solution)/shard_map/ppermute | solution.py:34
  29.7 0.7 %collective-permute-start.9 = (bf16[128,512]{1,0:T(8,128)(2,1)S(1)}, bf16[128,512]{1,0:T(8,128)(2,1)S(1)}, u32[]{:S(2)}, u32[]{:S(2)}) collective-permute-start(bf16[128,512]{1,0:T(8,128)(2,1)S(1)} %get-tuple-element.48), channel_id=1, source_target_pairs={{4,0},{5,1},{6,2},{7,3},{8,4},{9,5},{10,6},{11,7},{12,8},{13,9},{1... | collective-permute-start | bytes 393224 | tf_op jit(solution)/shard_map/ppermute | solution.py:34
  30.4 0.0 copy-done.3
  30.4 1.3 %matrices.1 = (bf16[16,128,640]{2,1,0:T(8,128)(2,1)S(1)}, bf16[512,384]{1,0:T(8,128)(2,1)S(1)}) custom-call(f32[48,128]{1,0:T(8,128)S(1)} %copy-done.3, bf16[512,256]{1,0:T(8,128)(2,1)S(1)} %get-tuple-element.40.after.end_in.own_end), custom_call_target="tpu_custom_call" | custom-call | flops 1073741824 | bytes 2147483 | tf_op jit(solution)/shard_map/matrices/pallas_call | solution.py:459
  31.7 0.0 collective-permute-done.8.got_up
  31.7 0.0 collective-permute-done.9.got_down
  31.8 0.0 collective-permute-done.4.side_up
  31.8 0.0 collective-permute-done.5.side_down
  31.8 2.7 %collective-permute-done.7.end = bf16[544,256]{1,0:T(8,128)(2,1)S(1)} collective-permute-done((bf16[544,256]{1,0:T(8,128)(2,1)S(1)}, bf16[544,256]{1,0:T(8,128)(2,1)S(1)}, u32[]{:S(2)}, u32[]{:S(2)}) %collective-permute-start.7) | collective-permute-done | bytes 278560 | tf_op jit(solution)/shard_map/ppermute | solution.py:34
  34.5 0.0 copy-done.1
  34.5 3.2 %finish.1 = f32[512,512]{1,0:T(8,128)} custom-call(f32[512,512]{1,0:T(8,128)S(1)} %bitcast.6, bf16[512,256]{1,0:T(8,128)(2,1)S(1)} %get-tuple-element.28.own_mid, bf16[512,256]{1,0:T(8,128)(2,1)S(1)} %get-tuple-element.40.after.end_in.own_end, bf16[144,512]{1,0:T(8,128)(2,1)S(1)} %collective-permute-done.4.side_up, ...), custom_call_target="tpu_custom_call" | custom-call | flops 1073741824 | bytes 2147483 | tf_op jit(solution)/shard_map/finish/pallas_call | solution.py:466
  (3 shorter events, 0.0 us)
Async XLA Ops:
  2.0 13.7 %collective-permute-start = (f32[520,128]{1,0:T(8,128)}, f32[520,128]{1,0:T(8,128)S(1)}, u32[]{:S(2)}, u32[]{:S(2)}) collective-permute-start(f32[520,128]{1,0:T(8,128)} %get-tuple-element.29), channel_id=1, source_target_pairs={{0,1},{1,2},{2,3},{4,5},{5,6},{6,7},{8,9},{9,10},{10,11},{12,13},{... | collective-permute-start | bytes 798728 | tf_op jit(solution)/shard_map/ppermute | solution.py:34
  2.7 13.1 %collective-permute-start.1 = (f32[520,128]{1,0:T(8,128)}, f32[520,128]{1,0:T(8,128)S(1)}, u32[]{:S(2)}, u32[]{:S(2)}) collective-permute-start(f32[520,128]{1,0:T(8,128)} %get-tuple-element.30), channel_id=1, source_target_pairs={{1,0},{2,1},{3,2},{5,4},{6,5},{7,6},{9,8},{10,9},{11,10},{13,12},{... | collective-permute-start | bytes 798728 | tf_op jit(solution)/shard_map/ppermute | solution.py:34
  3.4 12.4 %collective-permute-start.3 = (f32[8,128]{1,0:T(8,128)}, f32[8,128]{1,0:T(8,128)S(1)}, u32[]{:S(2)}, u32[]{:S(2)}) collective-permute-start(f32[8,128]{1,0:T(8,128)} %get-tuple-element.31), channel_id=1, source_target_pairs={{20,0},{21,1},{22,2},{23,3},{24,4},{25,5},{26,6},{27,7},{28,8},{29... | collective-permute-start | bytes 12296 | tf_op jit(solution)/shard_map/ppermute | solution.py:34
  9.9 5.8 %collective-permute-start.2 = (f32[8,128]{1,0:T(8,128)}, f32[8,128]{1,0:T(8,128)S(1)}, u32[]{:S(2)}, u32[]{:S(2)}) collective-permute-start(f32[8,128]{1,0:T(8,128)} %get-tuple-element.31), channel_id=1, source_target_pairs={{16,4},{17,5},{18,6},{19,7},{20,8},{21,9},{22,10},{23,11},{24,12},... | collective-permute-start | bytes 12296 | tf_op jit(solution)/shard_map/ppermute | solution.py:34
  12.4 1.2 %copy-start = (f32[1,512,512]{2,1,0:T(8,128)S(1)}, f32[1,512,512]{2,1,0:T(8,128)}, u32[]{:S(2)}) copy-start(f32[1,512,512]{2,1,0:T(8,128)} %param.9) | copy-start | bytes 3145732
  13.6 0.7 %copy-start.2 = (f32[48,128]{1,0:T(8,128)S(1)}, f32[48,128]{1,0:T(8,128)}, u32[]{:S(2)}) copy-start(f32[48,128]{1,0:T(8,128)} %get-tuple-element.27.meta) | copy-start | bytes 73732
  14.3 16.1 %copy-start.3 = (f32[48,128]{1,0:T(8,128)S(1)}, f32[48,128]{1,0:T(8,128)}, u32[]{:S(2)}) copy-start(f32[48,128]{1,0:T(8,128)} %get-tuple-element.27.meta) | copy-start | bytes 73732
  14.3 15.4 %collective-permute-start.6 = (bf16[416,256]{1,0:T(8,128)(2,1)S(1)}, bf16[416,256]{1,0:T(8,128)(2,1)S(1)}, u32[]{:S(2)}, u32[]{:S(2)}) collective-permute-start(bf16[416,256]{1,0:T(8,128)(2,1)S(1)} %get-tuple-element.43), channel_id=1, source_target_pairs={{0,16},{1,17},{2,18},{3,19},{4,20},{5,21},{6,22},{7,23},{8,24},{9,... | collective-permute-start | bytes 638984 | tf_op jit(solution)/shard_map/ppermute | solution.py:34
  15.8 18.7 %copy-start.1 = (f32[1,512,512]{2,1,0:T(8,128)S(1)}, f32[1,512,512]{2,1,0:T(8,128)}, u32[]{:S(2)}) copy-start(f32[1,512,512]{2,1,0:T(8,128)} %param.9) | copy-start | bytes 3145732
  15.8 18.6 %collective-permute-start.7 = (bf16[544,256]{1,0:T(8,128)(2,1)S(1)}, bf16[544,256]{1,0:T(8,128)(2,1)S(1)}, u32[]{:S(2)}, u32[]{:S(2)}) collective-permute-start(bf16[544,256]{1,0:T(8,128)(2,1)S(1)} %get-tuple-element.44), channel_id=1, source_target_pairs={{0,16},{1,17},{2,18},{3,19},{4,20},{5,21},{6,22},{7,23},{8,24},{9,... | collective-permute-start | bytes 835592 | tf_op jit(solution)/shard_map/ppermute | solution.py:34
  17.3 14.5 %collective-permute-start.4 = (bf16[144,512]{1,0:T(8,128)(2,1)S(1)}, bf16[144,512]{1,0:T(8,128)(2,1)S(1)}, u32[]{:S(2)}, u32[]{:S(2)}) collective-permute-start(bf16[144,512]{1,0:T(8,128)(2,1)S(1)} %get-tuple-element.41.down_in), channel_id=1, source_target_pairs={{0,20},{1,21},{2,22},{3,23},{4,24},{5,25},{6,26},{7,27},{8,28},{9,... | collective-permute-start | bytes 442376 | tf_op jit(solution)/shard_map/ppermute | solution.py:34
  18.6 13.2 %collective-permute-start.5 = (bf16[144,512]{1,0:T(8,128)(2,1)S(1)}, bf16[144,512]{1,0:T(8,128)(2,1)S(1)}, u32[]{:S(2)}, u32[]{:S(2)}) collective-permute-start(bf16[144,512]{1,0:T(8,128)(2,1)S(1)} %get-tuple-element.42.up_in), channel_id=1, source_target_pairs={{4,16},{5,17},{6,18},{7,19},{8,20},{9,21},{10,22},{11,23},{12,24},... | collective-permute-start | bytes 442376 | tf_op jit(solution)/shard_map/ppermute | solution.py:34
  19.9 11.8 %collective-permute-start.8 = (bf16[128,512]{1,0:T(8,128)(2,1)S(1)}, bf16[128,512]{1,0:T(8,128)(2,1)S(1)}, u32[]{:S(2)}, u32[]{:S(2)}) collective-permute-start(bf16[128,512]{1,0:T(8,128)(2,1)S(1)} %get-tuple-element.47), channel_id=1, source_target_pairs={{0,4},{1,5},{2,6},{3,7},{4,8},{5,9},{6,10},{7,11},{8,12},{9,13},{1... | collective-permute-start | bytes 393224 | tf_op jit(solution)/shard_map/ppermute | solution.py:34
  29.7 2.0 %collective-permute-start.9 = (bf16[128,512]{1,0:T(8,128)(2,1)S(1)}, bf16[128,512]{1,0:T(8,128)(2,1)S(1)}, u32[]{:S(2)}, u32[]{:S(2)}) collective-permute-start(bf16[128,512]{1,0:T(8,128)(2,1)S(1)} %get-tuple-element.48), channel_id=1, source_target_pairs={{4,0},{5,1},{6,2},{7,3},{8,4},{9,5},{10,6},{11,7},{12,8},{13,9},{1... | collective-permute-start | bytes 393224 | tf_op jit(solution)/shard_map/ppermute | solution.py:34

commit v4 on v3

--- a/solution.py
+++ b/solution.py
@@ -18,6 +18,7 @@
 VM = pl.BlockSpec(memory_space=pltpu.VMEM)
 ANY = pl.BlockSpec(memory_space=pl.ANY)
 FULL = 64 << 20
+SPARE = 1 << 15
 
 
 def moved(block, step, sources):
@@ -94,23 +95,40 @@
 
 def gather_kernel(
     nb, frame, row_frac, col_frac, row_shift, col_shift, table, prof_rows, prof_cols, ids,
-    meta, row_meta, to_right, to_left,
-    table_v, rows_v, cols_v, ids_v, row_s, col_s, sems,
+    meta_out, row_meta, to_right, to_left,
+    meta, marks, table_v, rows_v, cols_v, ids_v, row_s, col_s, sems, done,
 ):
     side = nb * BLK
-    pairs = (
-        (row_frac, meta.at[0:nb, :]),
-        (col_frac, meta.at[2 * nb : 3 * nb, :]),
-        (row_shift, row_s),
-        (col_shift, col_s),
-        (table, table_v),
-        (prof_rows, rows_v),
-        (prof_cols, cols_v),
-        (ids, ids_v),
-        (frame.at[:, side - BLK :], to_right.at[:side, :]),
-        (frame.at[:, :BLK], to_left.at[:side, :]),
-    )
-    copies = [pltpu.make_async_copy(src, dst, sems.at[n]) for n, (src, dst) in enumerate(pairs)]
+    warper = lax.axis_index("segment") == 0
+    copies = [
+        pltpu.make_async_copy(src, dst, sems.at[n])
+        for n, (src, dst) in enumerate((
+            (row_frac, meta.at[0:nb, :]),
+            (col_frac, meta.at[2 * nb : 3 * nb, :]),
+            (row_shift, row_s),
+            (col_shift, col_s),
+            (table, table_v),
+            (prof_rows, rows_v),
+            (prof_cols, cols_v),
+            (ids, ids_v),
+        ))
+    ]
+    slabs = [
+        pltpu.make_async_copy(frame.at[:, side - BLK :], marks.at[0, :side, :], done.at[0]),
+        pltpu.make_async_copy(frame.at[:, :BLK], marks.at[1, :side, :], done.at[1]),
+    ]
+    sends = [
+        pltpu.make_async_copy(marks.at[0], to_right, done.at[2]),
+        pltpu.make_async_copy(marks.at[1], to_left, done.at[3]),
+    ]
+    summary = pltpu.make_async_copy(meta, meta_out.at[: meta.shape[0], :], done.at[4])
+    rows = pltpu.make_async_copy(meta.at[: 2 * nb, :], row_meta, done.at[5])
+
+    @pl.when(warper)
+    def _():
+        for copy in slabs:
+            copy.start()
+
     for copy in copies:
         copy.start()
     for copy in copies:
@@ -122,30 +140,50 @@
     for part in (table_v, rows_v, cols_v, ids_v):
         meta[base : base + part.shape[0], : part.shape[1]] = part[...].astype(F32)
         base += part.shape[0]
-    row_meta[...] = meta[: 2 * nb, :]
-    for out, b in ((to_right, nb - 1), (to_left, 0)):
-        out[side : side + 1, :] = meta[2 * nb + b : 2 * nb + b + 1, :]
-        out[side + 1 : side + 2, :] = meta[3 * nb + b : 3 * nb + b + 1, :]
+    for n, b in ((0, nb - 1), (1, 0)):
+        marks[n, side : side + 1, :] = meta[2 * nb + b : 2 * nb + b + 1, :]
+        marks[n, side + 1 : side + 2, :] = meta[3 * nb + b : 3 * nb + b + 1, :]
+    summary.start()
+    rows.start()
+
+    @pl.when(warper)
+    def _():
+        for copy, send in zip(slabs, sends):
+            copy.wait()
+            send.start()
+        for send in sends:
+            send.wait()
+
+    summary.wait()
+    rows.wait()
 
 
 def center_kernel(
-    nb, frame, meta,
-    own, across, src_hi, src_lo, mid_hi, mid_lo, row_hi, row_lo, edge_hi, edge_lo,
+    nb, frame, meta_in,
+    own, across, tip_hi, tip_lo, mid_hi, mid_lo, row_hi, row_lo, edge_hi, edge_lo,
+    meta, src_hi, src_lo, sem,
 ):
     side = nb * BLK
 
     @pl.when(lax.axis_index("segment") == 0)
     def _():
+        small = pltpu.make_async_copy(meta_in.at[: meta.shape[0], :], meta, sem)
+        small.start()
+        for b in range(nb):
+            rows = slice(b * BLK, (b + 1) * BLK)
+            hi, lo = split(frame[rows, :])
+            for whole, tip, part in ((src_hi, tip_hi, hi), (src_lo, tip_lo, lo)):
+                whole[rows, :] = part
+                tip[rows, :BLK] = part[:, :BLK]
+                tip[rows, BLK:] = part[:, side - BLK :]
+        small.wait()
         fracs = [meta[2 * nb + b : 2 * nb + b + 1, :] for b in range(nb)]
         weights = taps(fracs + [meta[b : b + 1, :] for b in range(nb)])
         col_shift = [meta[3 * nb + b : 3 * nb + b + 1, :].astype(jnp.int32) for b in range(nb)]
         row_shift = [meta[nb + b : nb + b + 1, :].astype(jnp.int32) for b in range(nb)]
-        hi, lo = split(frame[...])
-        src_hi[...] = hi
-        src_lo[...] = lo
         for b in range(1, nb - 1):
+            cols = slice((b - 1) * BLK, (b + 2) * BLK)
             mat = split(banded(weights[b], col_shift[b], 3 * BLK, -BLK))
-            cols = slice((b - 1) * BLK, (b + 2) * BLK)
             hi, lo = split(dot3((src_hi[:, cols], src_lo[:, cols]), mat, MATMUL))
             mid_hi[:, (b - 1) * BLK : b * BLK] = hi
             mid_lo[:, (b - 1) * BLK : b * BLK] = lo
@@ -168,9 +206,12 @@
             edge_lo[n * 2 * BLK : (n + 1) * 2 * BLK, :] = lo
 
 
-def matrices_kernel(nb, nu, nv, sets, meta, after, kernels, band, padded):
+def matrices_kernel(nb, nu, nv, sets, meta_in, after, kernels, band, padded, meta, sem):
     @pl.when(lax.axis_index("segment") != 0)
     def _():
+        small = pltpu.make_async_copy(meta_in.at[: meta.shape[0], :], meta, sem)
+        small.start()
+        small.wait()
         base = 4 * nb
         table = meta[base : base + sets, : nu * nv]
         base += sets
@@ -209,7 +250,7 @@
 
 def edge_kernel(
     nb, nx, ny,
-    left, right, meta_up, meta_down, src_hi, src_lo, mid_hi, mid_lo, row_hi, row_lo, edge_hi, edge_lo,
+    left, right, meta_up, meta_down, tip_hi, tip_lo, mid_hi, mid_lo, row_hi, row_lo, edge_hi, edge_lo,
     own, across, side_up, side_down,
     end_hi, end_lo,
 ):
@@ -228,10 +269,10 @@
             for part, row in ((left, side + 1), (right, side + 1), (meta_up, 2 * nb - 1), (meta_down, nb))
         ]
         parts = [split(left[:side, :]), split(right[:side, :])]
-        for n, col in ((0, 0), (1, side - BLK)):
+        for n in range(2):
             source = []
-            for part, src in zip(parts[n], (src_hi, src_lo)):
-                inner = src[:, col : col + BLK]
+            for part, tip in zip(parts[n], (tip_hi, tip_lo)):
+                inner = tip[:, n * BLK : (n + 1) * BLK]
                 source.append(jnp.concatenate([part, inner] if n == 0 else [inner, part], axis=1))
             mat = tuple(edge[n * 2 * BLK : (n + 1) * 2 * BLK, :] for edge in (edge_hi, edge_lo))
             hi, lo = split(dot3(source, mat, MATMUL))
@@ -242,10 +283,7 @@
         low = split(banded(jnp.where(low_ok, weights[0], 0.0), shifts[0], BLK, BLK))
         high = split(banded(jnp.where(high_ok, weights[1], 0.0), shifts[1], BLK, -BLK))
         mat = [jnp.concatenate(pair, axis=0) for pair in zip(low, high)]
-        source = [
-            jnp.concatenate([src[:, :BLK], src[:, side - BLK :]], axis=1) for src in (src_hi, src_lo)
-        ]
-        hi, lo = split(dot3(source, mat, MATMUL))
+        hi, lo = split(dot3((tip_hi[...], tip_lo[...]), mat, MATMUL))
         end_hi[:, 2 * BLK :] = hi
         end_lo[:, 2 * BLK :] = lo
         outer = []
@@ -413,16 +451,22 @@
     shape = jax.ShapeDtypeStruct
     slab = shape((side + 8, BLK), F32)
     total = 4 * nb + sets + nv + nu + nb
-    meta, row_meta, to_right, to_left = call(
-        functools.partial(gather_kernel, nb), "gather",
-        (shape((total + -total % 8, BLK), F32), shape((2 * nb, BLK), F32), slab, slab),
-        [ANY] * 9,
-        [
+    total += -total % 8
+    meta_shape = pltpu.VMEM((total, BLK), F32)
+    meta, row_meta, to_right, to_left = pl.pallas_call(
+        functools.partial(gather_kernel, nb),
+        out_shape=(shape((SPARE, BLK), F32), shape((2 * nb, BLK), F32), slab, slab),
+        in_specs=[ANY] * 9,
+        out_specs=(ANY,) * 4,
+        scratch_shapes=[
+            meta_shape, pltpu.VMEM((2, side + 8, BLK), F32),
             pltpu.VMEM(coef_table.shape, F32), pltpu.VMEM(profile_rows.shape, BF16),
             pltpu.VMEM(profile_cols.shape, BF16), pltpu.VMEM(weight_ids.shape, jnp.int32),
-            pltpu.SMEM((nb,), jnp.int32), pltpu.SMEM((nb,), jnp.int32), pltpu.SemaphoreType.DMA((10,)),
+            pltpu.SMEM((nb,), jnp.int32), pltpu.SMEM((nb,), jnp.int32),
+            pltpu.SemaphoreType.DMA((8,)), pltpu.SemaphoreType.DMA((6,)),
         ],
-        limit=FULL,
+        compiler_params=pltpu.CompilerParams(vmem_limit_bytes=FULL),
+        name="gather",
     )(frame, row_frac, col_frac, row_shift, col_shift, coef_table, profile_rows, profile_cols, weight_ids)
     meta_up = moved(row_meta, (-1, 1, 0), (1,))
     meta_down = moved(row_meta, (-1, -1, 0), (1,))
@@ -432,12 +476,16 @@
     own_mid, mid, *parts = call(
         functools.partial(center_kernel, nb), "center",
         (shape((side, inner), BF16), shape((kept, inner), BF16))
-        + (shape((side, side), BF16),) * 2
+        + (shape((side, 2 * BLK), BF16),) * 2
         + (shape((side, inner), BF16),) * 2
         + (shape((depth, BLK), BF16),) * 2
         + (shape((4 * BLK, BLK), BF16),) * 2,
-        [VM] * 2,
-        flops=1 << 30,
+        [VM, ANY],
+        [
+            meta_shape, pltpu.VMEM((side, side), BF16), pltpu.VMEM((side, side), BF16),
+            pltpu.SemaphoreType.DMA(()),
+        ],
+        flops=1 << 33,
     )(frame, meta)
     mid = moved(mid, (1, 0, 0), (0,))
     own_end, end, to_up, to_down = call(
@@ -446,7 +494,7 @@
         + (shape((BLK + 16, side), BF16),) * 2,
         [VM] * 12,
         [pltpu.VMEM((side, 3 * BLK), BF16)] * 2,
-        flops=1 << 30,
+        flops=1 << 33,
     )(left, right, meta_up, meta_down, *parts)
     end = moved(end, (1, 0, 0), (0,))
     side_down = moved(to_up, (1, -1, 0), (0,))
@@ -459,16 +507,16 @@
     kernels, band = call(
         functools.partial(matrices_kernel, nb, nu, nv, sets), "matrices",
         (shape((cells, BLK, width), BF16), shape((nu * BLK, 3 * BLK), BF16)),
-        [VM] * 2,
-        [pltpu.VMEM((8, width), F32)],
-        flops=1 << 30,
+        [ANY, VM],
+        [pltpu.VMEM((8, width), F32), meta_shape, pltpu.SemaphoreType.DMA(())],
+        flops=0,
     )(meta, own_end)
     result = call(
         functools.partial(finish_kernel, nb, nu), "finish",
         shape((side, side), F32),
         [VM] * 11,
         [pltpu.VMEM((side + 32, side + 2 * BLK), BF16), pltpu.VMEM((nu, side + 32, side), BF16)],
-        flops=1 << 30,
+        flops=0,
     )(frame, own_mid, own_end, side_up, side_down, mid, end, kernels, band, got_up, got_down)
     return result[None]
 

time: 38.1 us -> 35.9 us (0.942)
  starting transfers between devices: 17.1 us -> 13.1 us
  waiting for transfers between devices: 11.9 us -> 13.9 us
  local copies, waits for them, and re-layouts: 1.97 us -> 1.23 us
    ppermute x10, starting transfers between devices: 17.1 us -> 13.1 us  [moved(): return lax.ppermute(block, axes, route)]
    ppermute x10, waiting for transfers between devices: 11.9 us -> 13.9 us  [moved(): return lax.ppermute(block, axes, route)]
    pallas_call x1, Pallas kernels: 1.31 us -> 2.06 us  [local(): call(functools.partial(matrices_kernel, nb, nu, nv, sets), 'matrices', (s...]
    unnamed x8 -> x4, local copies, waits for them, and re-layouts: 1.97 us -> 1.23 us
    pallas_call x1, Pallas kernels: 2.03 us -> 1.54 us  [local(): pl.pallas_call(functools.partial(gather_kernel, nb), out_shape=(shape((SP...]
  transfers between devices with their start and end apart: 10 -> 10, of which waited for: 2 -> 2; matrix products, arithmetic and copies ran while one was open for 0% -> 0% of each run, Pallas kernels for 4% -> 6%
where the time goes in v4:
time: 35.9 us; the launch traced here: 35.5 us
  waiting for transfers between devices  13.9 us (39%)
  starting transfers between devices  13.1 us (36%)
  Pallas kernels  6.95 us (19%)
  local copies, waits for them, and re-layouts  1.23 us (3%)
    ppermute x10, waiting for transfers between devices, moved(): return lax.ppermute(block, axes, route)  13.9 us
    ppermute x10, starting transfers between devices, moved(): return lax.ppermute(block, axes, route)  13.1 us
    pallas_call x1, Pallas kernels, local(): call(functools.partial(finish_kernel, nb, nu), 'finish', shape((side, sid...  3.29 us
    pallas_call x1, Pallas kernels, local(): call(functools.partial(matrices_kernel, nb, nu, nv, sets), 'matrices', (s...  2.06 us
    pallas_call x1, Pallas kernels, local(): pl.pallas_call(functools.partial(gather_kernel, nb), out_shape=(shape((SP...  1.54 us
    unnamed x4, local copies, waits for them, and re-layouts  1.23 us
  transfers between devices with their start and end apart: 10, of which 2 were waited for; matrix products, arithmetic and copies ran while one was open for 0% of the time, Pallas kernels for 6%

profile of v4, /device:TPU:14, one launch (start us, length us, event | category | flops | bytes accessed | tf_op | source)
XLA Modules:
  0.0 35.5 jit_solution(7739122750361009937)
XLA Ops:
  0.0 1.5 %gather.1 = (f32[32768,128]{1,0:T(8,128)}, f32[8,128]{1,0:T(8,128)}, f32[520,128]{1,0:T(8,128)}, f32[520,128]{1,0:T(8,128)}) custom-call(f32[512,512]{1,0:T(8,128)} %bitcast.4, f32[4,128]{1,0:T(4,128)} %bitcast.7, f32[4,128]{1,0:T(4,128)} %bitcast.8, s32[4]{0:T(128)} %row_shift.1, s32[4]{0:T(128)} %col_shift.1, f32[16,32]{1,0:T(8,128)} %table.1, ...), custom_call_target="tpu_custom_call" | custom-call | tf_op jit(solution)/shard_map/gather/pallas_call | solution.py:456
  1.6 2.7 %collective-permute-start.3 = (f32[8,128]{1,0:T(8,128)}, f32[8,128]{1,0:T(8,128)S(1)}, u32[]{:S(2)}, u32[]{:S(2)}) collective-permute-start(f32[8,128]{1,0:T(8,128)} %get-tuple-element.31), channel_id=1, source_target_pairs={{20,0},{21,1},{22,2},{23,3},{24,4},{25,5},{26,6},{27,7},{28,8},{29... | collective-permute-start | bytes 12296 | tf_op jit(solution)/shard_map/ppermute | solution.py:35
  4.3 2.4 %collective-permute-start.2 = (f32[8,128]{1,0:T(8,128)}, f32[8,128]{1,0:T(8,128)S(1)}, u32[]{:S(2)}, u32[]{:S(2)}) collective-permute-start(f32[8,128]{1,0:T(8,128)} %get-tuple-element.31), channel_id=1, source_target_pairs={{16,4},{17,5},{18,6},{19,7},{20,8},{21,9},{22,10},{23,11},{24,12},... | collective-permute-start | bytes 12296 | tf_op jit(solution)/shard_map/ppermute | solution.py:35
  6.7 0.7 %collective-permute-start = (f32[520,128]{1,0:T(8,128)}, f32[520,128]{1,0:T(8,128)S(1)}, u32[]{:S(2)}, u32[]{:S(2)}) collective-permute-start(f32[520,128]{1,0:T(8,128)} %get-tuple-element.29), channel_id=1, source_target_pairs={{0,1},{1,2},{2,3},{4,5},{5,6},{6,7},{8,9},{9,10},{10,11},{12,13},{... | collective-permute-start | bytes 798728 | tf_op jit(solution)/shard_map/ppermute | solution.py:35
  7.4 0.7 %collective-permute-start.1 = (f32[520,128]{1,0:T(8,128)}, f32[520,128]{1,0:T(8,128)S(1)}, u32[]{:S(2)}, u32[]{:S(2)}) collective-permute-start(f32[520,128]{1,0:T(8,128)} %get-tuple-element.30), channel_id=1, source_target_pairs={{1,0},{2,1},{3,2},{5,4},{6,5},{7,6},{9,8},{10,9},{11,10},{13,12},{... | collective-permute-start | bytes 798728 | tf_op jit(solution)/shard_map/ppermute | solution.py:35
  8.1 0.0 copy-start
  8.1 1.2 %copy-done = f32[1,512,512]{2,1,0:T(8,128)S(1)} copy-done((f32[1,512,512]{2,1,0:T(8,128)S(1)}, f32[1,512,512]{2,1,0:T(8,128)}, u32[]{:S(2)}) %copy-start) | copy-done | bytes 1048600
  9.3 1.3 %collective-permute-start.6 = (bf16[416,256]{1,0:T(8,128)(2,1)S(1)}, bf16[416,256]{1,0:T(8,128)(2,1)S(1)}, u32[]{:S(2)}, u32[]{:S(2)}) collective-permute-start(bf16[416,256]{1,0:T(8,128)(2,1)S(1)} %get-tuple-element.43), channel_id=1, source_target_pairs={{0,16},{1,17},{2,18},{3,19},{4,20},{5,21},{6,22},{7,23},{8,24},{9,... | collective-permute-start | bytes 638984 | tf_op jit(solution)/shard_map/ppermute | solution.py:35
  10.6 0.0 collective-permute-done.3.meta_down
  10.6 0.0 collective-permute-done.2.meta_up
  10.7 0.0 collective-permute-done.left
  10.7 0.0 collective-permute-done.1.right
  10.7 0.0 copy-start.1
  10.7 1.4 %collective-permute-start.7 = (bf16[544,256]{1,0:T(8,128)(2,1)S(1)}, bf16[544,256]{1,0:T(8,128)(2,1)S(1)}, u32[]{:S(2)}, u32[]{:S(2)}) collective-permute-start(bf16[544,256]{1,0:T(8,128)(2,1)S(1)} %get-tuple-element.44), channel_id=1, source_target_pairs={{0,16},{1,17},{2,18},{3,19},{4,20},{5,21},{6,22},{7,23},{8,24},{9,... | collective-permute-start | bytes 835592 | tf_op jit(solution)/shard_map/ppermute | solution.py:35
  12.2 1.3 %collective-permute-start.4 = (bf16[144,512]{1,0:T(8,128)(2,1)S(1)}, bf16[144,512]{1,0:T(8,128)(2,1)S(1)}, u32[]{:S(2)}, u32[]{:S(2)}) collective-permute-start(bf16[144,512]{1,0:T(8,128)(2,1)S(1)} %get-tuple-element.41.down_in), channel_id=1, source_target_pairs={{0,20},{1,21},{2,22},{3,23},{4,24},{5,25},{6,26},{7,27},{8,28},{9,... | collective-permute-start | bytes 442376 | tf_op jit(solution)/shard_map/ppermute | solution.py:35
  13.5 1.3 %collective-permute-start.5 = (bf16[144,512]{1,0:T(8,128)(2,1)S(1)}, bf16[144,512]{1,0:T(8,128)(2,1)S(1)}, u32[]{:S(2)}, u32[]{:S(2)}) collective-permute-start(bf16[144,512]{1,0:T(8,128)(2,1)S(1)} %get-tuple-element.42.up_in), channel_id=1, source_target_pairs={{4,16},{5,17},{6,18},{7,19},{8,20},{9,21},{10,22},{11,23},{12,24},... | collective-permute-start | bytes 442376 | tf_op jit(solution)/shard_map/ppermute | solution.py:35
  14.8 0.7 %collective-permute-start.8 = (bf16[128,512]{1,0:T(8,128)(2,1)S(1)}, bf16[128,512]{1,0:T(8,128)(2,1)S(1)}, u32[]{:S(2)}, u32[]{:S(2)}) collective-permute-start(bf16[128,512]{1,0:T(8,128)(2,1)S(1)} %get-tuple-element.47), channel_id=1, source_target_pairs={{0,4},{1,5},{2,6},{3,7},{4,8},{5,9},{6,10},{7,11},{8,12},{9,13},{1... | collective-permute-start | bytes 393224 | tf_op jit(solution)/shard_map/ppermute | solution.py:35
  15.5 11.8 %collective-permute-done.6.mid = bf16[416,256]{1,0:T(8,128)(2,1)S(1)} collective-permute-done((bf16[416,256]{1,0:T(8,128)(2,1)S(1)}, bf16[416,256]{1,0:T(8,128)(2,1)S(1)}, u32[]{:S(2)}, u32[]{:S(2)}) %collective-permute-start.6) | collective-permute-done | bytes 213024 | tf_op jit(solution)/shard_map/ppermute | solution.py:35
  27.3 0.7 %collective-permute-start.9 = (bf16[128,512]{1,0:T(8,128)(2,1)S(1)}, bf16[128,512]{1,0:T(8,128)(2,1)S(1)}, u32[]{:S(2)}, u32[]{:S(2)}) collective-permute-start(bf16[128,512]{1,0:T(8,128)(2,1)S(1)} %get-tuple-element.48), channel_id=1, source_target_pairs={{4,0},{5,1},{6,2},{7,3},{8,4},{9,5},{10,6},{11,7},{12,8},{13,9},{1... | collective-permute-start | bytes 393224 | tf_op jit(solution)/shard_map/ppermute | solution.py:35
  27.9 2.1 %matrices.1 = (bf16[16,128,640]{2,1,0:T(8,128)(2,1)S(1)}, bf16[512,384]{1,0:T(8,128)(2,1)S(1)}) custom-call(f32[32768,128]{1,0:T(8,128)} %get-tuple-element.27.meta_in, bf16[512,256]{1,0:T(8,128)(2,1)S(1)} %get-tuple-element.40.after.end_in.own_end), custom_call_target="tpu_custom_call" | custom-call | tf_op jit(solution)/shard_map/matrices/pallas_call | solution.py:507
  30.0 0.0 collective-permute-done.8.got_up
  30.0 0.0 collective-permute-done.9.got_down
  30.0 0.0 collective-permute-done.4.side_up
  30.0 0.0 collective-permute-done.5.side_down
  30.1 2.1 %collective-permute-done.7.end = bf16[544,256]{1,0:T(8,128)(2,1)S(1)} collective-permute-done((bf16[544,256]{1,0:T(8,128)(2,1)S(1)}, bf16[544,256]{1,0:T(8,128)(2,1)S(1)}, u32[]{:S(2)}, u32[]{:S(2)}) %collective-permute-start.7) | collective-permute-done | bytes 278560 | tf_op jit(solution)/shard_map/ppermute | solution.py:35
  32.2 0.0 copy-done.1
  32.2 3.3 %finish.1 = f32[512,512]{1,0:T(8,128)} custom-call(f32[512,512]{1,0:T(8,128)S(1)} %bitcast.6, bf16[512,256]{1,0:T(8,128)(2,1)S(1)} %get-tuple-element.28.own_mid, bf16[512,256]{1,0:T(8,128)(2,1)S(1)} %get-tuple-element.40.after.end_in.own_end, bf16[144,512]{1,0:T(8,128)(2,1)S(1)} %collective-permute-done.4.side_up, ...), custom_call_target="tpu_custom_call" | custom-call | tf_op jit(solution)/shard_map/finish/pallas_call | solution.py:514
  (3 shorter events, 0.0 us)
Async XLA Ops:
  1.6 9.1 %collective-permute-start.3 = (f32[8,128]{1,0:T(8,128)}, f32[8,128]{1,0:T(8,128)S(1)}, u32[]{:S(2)}, u32[]{:S(2)}) collective-permute-start(f32[8,128]{1,0:T(8,128)} %get-tuple-element.31), channel_id=1, source_target_pairs={{20,0},{21,1},{22,2},{23,3},{24,4},{25,5},{26,6},{27,7},{28,8},{29... | collective-permute-start | bytes 12296 | tf_op jit(solution)/shard_map/ppermute | solution.py:35
  4.3 6.4 %collective-permute-start.2 = (f32[8,128]{1,0:T(8,128)}, f32[8,128]{1,0:T(8,128)S(1)}, u32[]{:S(2)}, u32[]{:S(2)}) collective-permute-start(f32[8,128]{1,0:T(8,128)} %get-tuple-element.31), channel_id=1, source_target_pairs={{16,4},{17,5},{18,6},{19,7},{20,8},{21,9},{22,10},{23,11},{24,12},... | collective-permute-start | bytes 12296 | tf_op jit(solution)/shard_map/ppermute | solution.py:35
  6.7 3.9 %collective-permute-start = (f32[520,128]{1,0:T(8,128)}, f32[520,128]{1,0:T(8,128)S(1)}, u32[]{:S(2)}, u32[]{:S(2)}) collective-permute-start(f32[520,128]{1,0:T(8,128)} %get-tuple-element.29), channel_id=1, source_target_pairs={{0,1},{1,2},{2,3},{4,5},{5,6},{6,7},{8,9},{9,10},{10,11},{12,13},{... | collective-permute-start | bytes 798728 | tf_op jit(solution)/shard_map/ppermute | solution.py:35
  7.4 3.3 %collective-permute-start.1 = (f32[520,128]{1,0:T(8,128)}, f32[520,128]{1,0:T(8,128)S(1)}, u32[]{:S(2)}, u32[]{:S(2)}) collective-permute-start(f32[520,128]{1,0:T(8,128)} %get-tuple-element.30), channel_id=1, source_target_pairs={{1,0},{2,1},{3,2},{5,4},{6,5},{7,6},{9,8},{10,9},{11,10},{13,12},{... | collective-permute-start | bytes 798728 | tf_op jit(solution)/shard_map/ppermute | solution.py:35
  8.1 1.2 %copy-start = (f32[1,512,512]{2,1,0:T(8,128)S(1)}, f32[1,512,512]{2,1,0:T(8,128)}, u32[]{:S(2)}) copy-start(f32[1,512,512]{2,1,0:T(8,128)} %param.9) | copy-start | bytes 3145732
  9.3 17.9 %collective-permute-start.6 = (bf16[416,256]{1,0:T(8,128)(2,1)S(1)}, bf16[416,256]{1,0:T(8,128)(2,1)S(1)}, u32[]{:S(2)}, u32[]{:S(2)}) collective-permute-start(bf16[416,256]{1,0:T(8,128)(2,1)S(1)} %get-tuple-element.43), channel_id=1, source_target_pairs={{0,16},{1,17},{2,18},{3,19},{4,20},{5,21},{6,22},{7,23},{8,24},{9,... | collective-permute-start | bytes 638984 | tf_op jit(solution)/shard_map/ppermute | solution.py:35
  10.7 21.5 %copy-start.1 = (f32[1,512,512]{2,1,0:T(8,128)S(1)}, f32[1,512,512]{2,1,0:T(8,128)}, u32[]{:S(2)}) copy-start(f32[1,512,512]{2,1,0:T(8,128)} %param.9) | copy-start | bytes 3145732
  10.7 21.4 %collective-permute-start.7 = (bf16[544,256]{1,0:T(8,128)(2,1)S(1)}, bf16[544,256]{1,0:T(8,128)(2,1)S(1)}, u32[]{:S(2)}, u32[]{:S(2)}) collective-permute-start(bf16[544,256]{1,0:T(8,128)(2,1)S(1)} %get-tuple-element.44), channel_id=1, source_target_pairs={{0,16},{1,17},{2,18},{3,19},{4,20},{5,21},{6,22},{7,23},{8,24},{9,... | collective-permute-start | bytes 835592 | tf_op jit(solution)/shard_map/ppermute | solution.py:35
  12.2 17.9 %collective-permute-start.4 = (bf16[144,512]{1,0:T(8,128)(2,1)S(1)}, bf16[144,512]{1,0:T(8,128)(2,1)S(1)}, u32[]{:S(2)}, u32[]{:S(2)}) collective-permute-start(bf16[144,512]{1,0:T(8,128)(2,1)S(1)} %get-tuple-element.41.down_in), channel_id=1, source_target_pairs={{0,20},{1,21},{2,22},{3,23},{4,24},{5,25},{6,26},{7,27},{8,28},{9,... | collective-permute-start | bytes 442376 | tf_op jit(solution)/shard_map/ppermute | solution.py:35
  13.5 16.6 %collective-permute-start.5 = (bf16[144,512]{1,0:T(8,128)(2,1)S(1)}, bf16[144,512]{1,0:T(8,128)(2,1)S(1)}, u32[]{:S(2)}, u32[]{:S(2)}) collective-permute-start(bf16[144,512]{1,0:T(8,128)(2,1)S(1)} %get-tuple-element.42.up_in), channel_id=1, source_target_pairs={{4,16},{5,17},{6,18},{7,19},{8,20},{9,21},{10,22},{11,23},{12,24},... | collective-permute-start | bytes 442376 | tf_op jit(solution)/shard_map/ppermute | solution.py:35
  14.8 15.2 %collective-permute-start.8 = (bf16[128,512]{1,0:T(8,128)(2,1)S(1)}, bf16[128,512]{1,0:T(8,128)(2,1)S(1)}, u32[]{:S(2)}, u32[]{:S(2)}) collective-permute-start(bf16[128,512]{1,0:T(8,128)(2,1)S(1)} %get-tuple-element.47), channel_id=1, source_target_pairs={{0,4},{1,5},{2,6},{3,7},{4,8},{5,9},{6,10},{7,11},{8,12},{9,13},{1... | collective-permute-start | bytes 393224 | tf_op jit(solution)/shard_map/ppermute | solution.py:35
  27.3 2.7 %collective-permute-start.9 = (bf16[128,512]{1,0:T(8,128)(2,1)S(1)}, bf16[128,512]{1,0:T(8,128)(2,1)S(1)}, u32[]{:S(2)}, u32[]{:S(2)}) collective-permute-start(bf16[128,512]{1,0:T(8,128)(2,1)S(1)} %get-tuple-element.48), channel_id=1, source_target_pairs={{4,0},{5,1},{6,2},{7,3},{8,4},{9,5},{10,6},{11,7},{12,8},{13,9},{1... | collective-permute-start | bytes 393224 | tf_op jit(solution)/shard_map/ppermute | solution.py:35

commit v5 on v4

--- a/solution.py
+++ b/solution.py
@@ -80,17 +80,13 @@
 LEFT_T = ((0,), (0,))
 
 
-def row_depth(b, nb):
-    return BLK if b in (0, nb - 1) else 3 * BLK
-
-
-def row_start(b, nb):
-    return sum(row_depth(a, nb) for a in range(b))
-
-
-def row_source(b, nb):
-    first = b if b in (0, nb - 1) else b - 1
-    return slice(first * BLK, first * BLK + row_depth(b, nb))
+def packed3(left, right):
+    lh, ll = left
+    rh, rl = right
+    width = rh.shape[1]
+    dot = functools.partial(jnp.dot, preferred_element_type=F32)
+    both = dot(lh, jnp.concatenate([rh, rl], axis=1))
+    return both[:, :width] + both[:, width:] + dot(ll, rh)
 
 
 def gather_kernel(
@@ -182,21 +178,18 @@
         col_shift = [meta[3 * nb + b : 3 * nb + b + 1, :].astype(jnp.int32) for b in range(nb)]
         row_shift = [meta[nb + b : nb + b + 1, :].astype(jnp.int32) for b in range(nb)]
         for b in range(1, nb - 1):
+            mat = split(banded(weights[b], col_shift[b], 3 * BLK, -BLK))
             cols = slice((b - 1) * BLK, (b + 2) * BLK)
-            mat = split(banded(weights[b], col_shift[b], 3 * BLK, -BLK))
-            hi, lo = split(dot3((src_hi[:, cols], src_lo[:, cols]), mat, MATMUL))
+            hi, lo = split(packed3((src_hi[:, cols], src_lo[:, cols]), mat))
             mid_hi[:, (b - 1) * BLK : b * BLK] = hi
             mid_lo[:, (b - 1) * BLK : b * BLK] = lo
         for b in range(nb):
-            offset = 0 if b in (0, nb - 1) else -BLK
-            depth = row_depth(b, nb)
-            hi, lo = split(banded(weights[nb + b], row_shift[b], depth, offset))
-            kept = slice(row_start(b, nb), row_start(b, nb) + depth)
-            row_hi[kept, :] = hi
-            row_lo[kept, :] = lo
-            rows = row_source(b, nb)
-            got = dot3((hi, lo), (mid_hi[rows, :], mid_lo[rows, :]), LEFT_T).astype(BF16)
-            own[b * BLK : (b + 1) * BLK, :] = got
+            first, depth = (b, BLK) if b in (0, nb - 1) else (b - 1, 3 * BLK)
+            mat = split(banded(weights[nb + b], row_shift[b], depth, (first - b) * BLK).T)
+            rows, cols = slice(b * BLK, (b + 1) * BLK), slice(first * BLK, first * BLK + depth)
+            row_hi[rows, cols], row_lo[rows, cols] = mat
+            got = dot3(mat, (mid_hi[cols, :], mid_lo[cols, :]), MATMUL).astype(BF16)
+            own[rows, :] = got
             low = max(b * BLK, ROW0)
             high = min((b + 1) * BLK, side - ROW0)
             across[low - ROW0 : high - ROW0, :] = got[low - b * BLK : high - b * BLK, :]
@@ -242,10 +235,8 @@
         padded[...] = jnp.zeros_like(padded)
         padded[0:nu, 0:KW] = prof_cols
         for p in range(nu):
-            row = jnp.broadcast_to(padded[p : p + 1, : 3 * BLK], (BLK, 3 * BLK))
-            band[p * BLK : (p + 1) * BLK, :] = pltpu.roll(
-                row, BLK - HALF, 1, stride=1, stride_axis=0
-            ).astype(BF16)
+            row = jnp.broadcast_to(padded[p : p + 1, : 2 * BLK], (BLK, 2 * BLK))
+            band[p * BLK : (p + 1) * BLK, :] = pltpu.roll(row, 1, 1, stride=1, stride_axis=0).astype(BF16)
 
 
 def edge_kernel(
@@ -275,7 +266,7 @@
                 inner = tip[:, n * BLK : (n + 1) * BLK]
                 source.append(jnp.concatenate([part, inner] if n == 0 else [inner, part], axis=1))
             mat = tuple(edge[n * 2 * BLK : (n + 1) * 2 * BLK, :] for edge in (edge_hi, edge_lo))
-            hi, lo = split(dot3(source, mat, MATMUL))
+            hi, lo = split(packed3(source, mat))
             end_hi[:, n * BLK : (n + 1) * BLK] = hi
             end_lo[:, n * BLK : (n + 1) * BLK] = lo
         low_ok = jnp.logical_and(lanes >= BLK - HALF, j > 0)
@@ -283,46 +274,57 @@
         low = split(banded(jnp.where(low_ok, weights[0], 0.0), shifts[0], BLK, BLK))
         high = split(banded(jnp.where(high_ok, weights[1], 0.0), shifts[1], BLK, -BLK))
         mat = [jnp.concatenate(pair, axis=0) for pair in zip(low, high)]
-        hi, lo = split(dot3((tip_hi[...], tip_lo[...]), mat, MATMUL))
+        hi, lo = split(packed3((tip_hi[...], tip_lo[...]), mat))
         end_hi[:, 2 * BLK :] = hi
         end_lo[:, 2 * BLK :] = lo
         outer = []
         for n, b in ((0, 0), (1, nb - 1)):
             there = (i > 0) if n == 0 else (i < nx - 1)
-            mat = split(banded(jnp.where(there, weights[2 + n], 0.0), shifts[2 + n], BLK, BLK if n == 0 else -BLK))
+            weight = jnp.where(there, weights[2 + n], 0.0)
+            mat = split(banded(weight, shifts[2 + n], BLK, BLK if n == 0 else -BLK).T)
             rows = slice(b * BLK, (b + 1) * BLK)
-            end = dot3(mat, (end_hi[rows, : 2 * BLK], end_lo[rows, : 2 * BLK]), LEFT_T).astype(BF16)
-            mid = dot3(mat, (mid_hi[rows, :], mid_lo[rows, :]), LEFT_T).astype(BF16)
-            turned = dot3((end_hi[rows, 2 * BLK :], end_lo[rows, 2 * BLK :]), mat, LEFT_T)
+            source = [
+                jnp.concatenate([mid[rows, :], end[rows, :]], axis=1)
+                for mid, end in ((mid_hi, end_hi), (mid_lo, end_lo))
+            ]
+            got = dot3(mat, source, MATMUL)
+            outer.append(got)
             out = side_up if n == 0 else side_down
-            out[:BLK, :BLK] = end[:, :BLK]
-            out[:BLK, BLK : side - BLK] = mid
-            out[:BLK, side - BLK :] = end[:, BLK:]
+            inner = side - 2 * BLK
+            out[:BLK, BLK : side - BLK] = got[:, :inner].astype(BF16)
+            out[:BLK, :BLK] = got[:, inner : inner + BLK].astype(BF16)
+            out[:BLK, side - BLK :] = got[:, inner + BLK : side].astype(BF16)
+            turned = got[:, side:].T
             out[BLK:, :BLK] = turned[:16].astype(BF16)
             out[BLK:, BLK : 2 * BLK] = turned[BLK - 16 :].astype(BF16)
-            outer.append(turned)
         across[kept : kept + 16, :] = side_down[:16, :half]
         across[kept + 16 : kept + 32, :] = side_up[BLK - 16 : BLK, :half]
         across[kept + 32 : kept + 48, :] = side_down[:16, half:]
         across[kept + 48 : kept + 64, :] = side_up[BLK - 16 : BLK, half:]
-        columns = lax.broadcasted_iota(jnp.int32, (BLK, BLK), 1)
+        strips = []
         for b in range(nb):
-            hi, lo = (mat[row_start(b, nb) : row_start(b, nb) + row_depth(b, nb), :] for mat in (row_hi, row_lo))
-            rows = row_source(b, nb)
-            got = dot3((hi, lo), (end_hi[rows, : 2 * BLK], end_lo[rows, : 2 * BLK]), LEFT_T).astype(BF16)
-            own[b * BLK : (b + 1) * BLK, :] = got
+            first, depth = (b, BLK) if b in (0, nb - 1) else (b - 1, 3 * BLK)
+            rows, cols = slice(b * BLK, (b + 1) * BLK), slice(first * BLK, first * BLK + depth)
+            mat = (row_hi[rows, cols], row_lo[rows, cols])
+            got = dot3(mat, (end_hi[cols, : 2 * BLK], end_lo[cols, : 2 * BLK]), MATMUL).astype(BF16)
+            own[rows, :] = got
             low = max(b * BLK, ROW0)
             high = min((b + 1) * BLK, side - ROW0)
             across[low - ROW0 : high - ROW0, :] = got[low - b * BLK : high - b * BLK, :]
-            turned = dot3((end_hi[rows, 2 * BLK :], end_lo[rows, 2 * BLK :]), (hi, lo), LEFT_T)
-            if b == 0:
-                turned = jnp.where(columns < ROW0, pltpu.roll(outer[0], ROW0, 1), turned)
-            if b == nb - 1:
-                turned = jnp.where(columns >= BLK - ROW0, pltpu.roll(outer[1], BLK - ROW0, 1), turned)
-            half_at, lane = divmod(b * BLK, half)
-            base = kept + 64 + 32 * half_at
-            across[base : base + 16, lane : lane + BLK] = turned[:16].astype(BF16)
-            across[base + 16 : base + 32, lane : lane + BLK] = turned[BLK - 16 :].astype(BF16)
+            strips.append(packed3(mat, (end_hi[cols, 2 * BLK :], end_lo[cols, 2 * BLK :])))
+        strip = jnp.concatenate(strips, axis=0)
+        strip = jnp.concatenate(
+            [
+                strip[: ROW0 - 16], outer[0][BLK - 16 :, side:], strip[ROW0 : side - ROW0],
+                outer[1][:16, side:], strip[side - ROW0 + 16 :],
+            ],
+            axis=0,
+        ).T
+        for n in range(2):
+            base = kept + 64 + 32 * n
+            cols = slice(n * half, (n + 1) * half)
+            across[base : base + 16, :] = strip[:16, cols].astype(BF16)
+            across[base + 16 : base + 32, :] = strip[BLK - 16 :, cols].astype(BF16)
 
 
 def relay_kernel(up_in, down_in, end_in, up, down):
@@ -335,12 +337,16 @@
 def finish_kernel(
     nb, nu,
     frame, own_mid, own_end, side_up, side_down, mid, end, kernels, band, got_up, got_down,
-    out, full, passed,
+    out, result, wide, full, passed, sems,
 ):
     side = nb * BLK
     half = side // 2
     warper = lax.axis_index("segment") == 0
     last = side - BLK
+    sends = []
+    for b in range(nb):
+        rows = pl.ds(b * BLK, BLK)
+        sends.append(pltpu.make_async_copy(result.at[rows, :], out.at[rows, :], sems.at[b]))
 
     @pl.when(warper)
     def _():
@@ -354,7 +360,8 @@
                     total = (total + got_up[:BLK, cols].astype(F32)).astype(BF16).astype(F32)
                 if b == nb - 1:
                     total = (total + got_down[:BLK, cols].astype(F32)).astype(BF16).astype(F32)
-                out[rows, cols] = total
+                result[rows, cols] = total
+            sends[b].start()
 
     @pl.when(jnp.logical_not(warper))
     def _():
@@ -367,19 +374,19 @@
 
         def fill(at, width, own, above, below):
             cols = slice(at, at + width)
-            full[16 : 16 + ROW0, cols] = above[:ROW0]
-            full[16 + ROW0 : 16 + BLK, cols] = added(own[:both], above[ROW0:])
-            full[16 + BLK : 16 + last, cols] = own[both : kept - both]
-            full[16 + last : stop - ROW0, cols] = added(own[kept - both :], below[:both])
-            full[stop - ROW0 : stop, cols] = below[both:]
-
-        fill(2 * BLK, side - 2 * BLK, mid[:kept, :], side_up[:BLK, BLK:last], side_down[:BLK, BLK:last])
-        fill(BLK, BLK, end[:kept, :BLK], side_up[:BLK, :BLK], side_down[:BLK, :BLK])
-        fill(side, BLK, end[:kept, BLK:], side_up[:BLK, last:], side_down[:BLK, last:])
-        full[:16, BLK : BLK + half] = end[kept + 16 : kept + 32, :]
-        full[:16, BLK + half : BLK + side] = end[kept + 48 : kept + 64, :]
-        full[stop:, BLK : BLK + half] = end[kept : kept + 16, :]
-        full[stop:, BLK + half : BLK + side] = end[kept + 32 : kept + 48, :]
+            wide[16 : 16 + ROW0, cols] = above[:ROW0]
+            wide[16 + ROW0 : 16 + BLK, cols] = added(own[:both], above[ROW0:])
+            wide[16 + BLK : 16 + last, cols] = own[both : kept - both]
+            wide[16 + last : stop - ROW0, cols] = added(own[kept - both :], below[:both])
+            wide[stop - ROW0 : stop, cols] = below[both:]
+
+        fill(BLK, side - 2 * BLK, mid[:kept, :], side_up[:BLK, BLK:last], side_down[:BLK, BLK:last])
+        fill(0, BLK, end[:kept, :BLK], side_up[:BLK, :BLK], side_down[:BLK, :BLK])
+        fill(last, BLK, end[:kept, BLK:], side_up[:BLK, last:], side_down[:BLK, last:])
+        wide[:16, :half] = end[kept + 16 : kept + 32, :]
+        wide[:16, half:side] = end[kept + 48 : kept + 64, :]
+        wide[stop:, :half] = end[kept : kept + 16, :]
+        wide[stop:, half:side] = end[kept + 32 : kept + 48, :]
         k = lax.broadcasted_iota(jnp.int32, (32, BLK), 0)
         lanes = lax.broadcasted_iota(jnp.int32, (32, BLK), 1)
         pick = (lanes == jnp.where(k < 16, k, k + BLK - 32)).astype(BF16)
@@ -395,13 +402,14 @@
             turned(jnp.concatenate([part[BLK:, :BLK], part[BLK:, BLK : 2 * BLK]], axis=0))
             for part in (side_up, side_down)
         )
-        fill(0, BLK, own[ROW0 : side - ROW0], above, below)
-        full[:16, :BLK] = own[ROW0 - 16 : ROW0]
-        full[stop:, :BLK] = own[side - ROW0 : side - ROW0 + 16]
-        full[:, BLK + side :] = full[:, :BLK]
+        fill(side, BLK, own[ROW0 : side - ROW0], above, below)
+        wide[:16, side:] = own[ROW0 - 16 : ROW0]
+        wide[stop:, side:] = own[side - ROW0 : side - ROW0 + 16]
+        cut = side + BLK - 16
+        full[...] = jnp.concatenate([wide[:, cut:], wide[:, :cut]], axis=1)
         for bj in range(nb):
             got = lax.dot_general(
-                full[:, bj * BLK : (bj + 3) * BLK], band[...], (((1,), (1,)), ((), ())),
+                full[:, bj * BLK : (bj + 2) * BLK], band[...], (((1,), (1,)), ((), ())),
                 preferred_element_type=F32,
             ).astype(BF16)
             for p in range(nu):
@@ -414,7 +422,11 @@
                 )
                 total = jnp.dot(kernels[bi * nb + bj], window, preferred_element_type=F32)
                 rows = slice(bi * BLK, (bi + 1) * BLK)
-                out[rows, cols] = frame[rows, cols] - total
+                result[rows, cols] = frame[rows, cols] - total
+            sends[bi].start()
+
+    for send in sends:
+        send.wait()
 
 
 def call(kernel, name, out_shape, in_specs, scratch=(), flops=0, limit=40 << 20):
@@ -472,13 +484,12 @@
     meta_down = moved(row_meta, (-1, -1, 0), (1,))
     left = moved(to_right, (0, 0, 1), (0,))
     right = moved(to_left, (0, 0, -1), (0,))
-    depth = row_start(nb, nb)
     own_mid, mid, *parts = call(
         functools.partial(center_kernel, nb), "center",
         (shape((side, inner), BF16), shape((kept, inner), BF16))
         + (shape((side, 2 * BLK), BF16),) * 2
         + (shape((side, inner), BF16),) * 2
-        + (shape((depth, BLK), BF16),) * 2
+        + (shape((side, side), BF16),) * 2
         + (shape((4 * BLK, BLK), BF16),) * 2,
         [VM, ANY],
         [
@@ -506,17 +517,23 @@
     got_up = moved(to_down, (0, 1, 0), (0,))
     kernels, band = call(
         functools.partial(matrices_kernel, nb, nu, nv, sets), "matrices",
-        (shape((cells, BLK, width), BF16), shape((nu * BLK, 3 * BLK), BF16)),
+        (shape((cells, BLK, width), BF16), shape((nu * BLK, 2 * BLK), BF16)),
         [ANY, VM],
         [pltpu.VMEM((8, width), F32), meta_shape, pltpu.SemaphoreType.DMA(())],
         flops=0,
     )(meta, own_end)
-    result = call(
-        functools.partial(finish_kernel, nb, nu), "finish",
-        shape((side, side), F32),
-        [VM] * 11,
-        [pltpu.VMEM((side + 32, side + 2 * BLK), BF16), pltpu.VMEM((nu, side + 32, side), BF16)],
-        flops=0,
+    result = pl.pallas_call(
+        functools.partial(finish_kernel, nb, nu),
+        out_shape=shape((side, side), F32),
+        in_specs=[VM] * 11,
+        out_specs=ANY,
+        scratch_shapes=[
+            pltpu.VMEM((side, side), F32), pltpu.VMEM((side + 32, side + BLK), BF16),
+            pltpu.VMEM((side + 32, side + BLK), BF16), pltpu.VMEM((nu, side + 32, side), BF16),
+            pltpu.SemaphoreType.DMA((nb,)),
+        ],
+        compiler_params=pltpu.CompilerParams(vmem_limit_bytes=40 << 20),
+        name="finish",
     )(frame, own_mid, own_end, side_up, side_down, mid, end, kernels, band, got_up, got_down)
     return result[None]
 

time: 35.9 us -> 34.9 us (0.972)
  Pallas kernels: 6.95 us -> 6.16 us
    pallas_call x1, Pallas kernels: 3.29 us -> 2.54 us  [local(): pl.pallas_call(functools.partial(finish_kernel, nb, nu), out_shape=shape(...]
where the time goes in v5:
time: 34.9 us; the launch traced here: 34.5 us
  waiting for transfers between devices  13.8 us (40%)
  starting transfers between devices  13.1 us (38%)
  Pallas kernels  6.16 us (18%)
  local copies, waits for them, and re-layouts  1.23 us (4%)
    ppermute x10, waiting for transfers between devices, moved(): return lax.ppermute(block, axes, route)  13.8 us
    ppermute x10, starting transfers between devices, moved(): return lax.ppermute(block, axes, route)  13.1 us
    pallas_call x1, Pallas kernels, local(): pl.pallas_call(functools.partial(finish_kernel, nb, nu), out_shape=shape(...  2.54 us
    pallas_call x1, Pallas kernels, local(): call(functools.partial(matrices_kernel, nb, nu, nv, sets), 'matrices', (s...  2.03 us
    pallas_call x1, Pallas kernels, local(): pl.pallas_call(functools.partial(gather_kernel, nb), out_shape=(shape((SP...  1.54 us
    unnamed x4, local copies, waits for them, and re-layouts  1.23 us
  transfers between devices with their start and end apart: 10, of which 2 were waited for; matrix products, arithmetic and copies ran while one was open for 0% of the time, Pallas kernels for 6%

profile of v5, /device:TPU:14, one launch (start us, length us, event | category | flops | bytes accessed | tf_op | source)
XLA Modules:
  0.0 34.5 jit_solution(10325510148452767614)
XLA Ops:
  0.0 1.5 %gather.1 = (f32[32768,128]{1,0:T(8,128)}, f32[8,128]{1,0:T(8,128)}, f32[520,128]{1,0:T(8,128)}, f32[520,128]{1,0:T(8,128)}) custom-call(f32[512,512]{1,0:T(8,128)} %bitcast.4, f32[4,128]{1,0:T(4,128)} %bitcast.7, f32[4,128]{1,0:T(4,128)} %bitcast.8, s32[4]{0:T(128)} %row_shift.1, s32[4]{0:T(128)} %col_shift.1, f32[16,32]{1,0:T(8,128)} %table.1, ...), custom_call_target="tpu_custom_call" | custom-call | tf_op jit(solution)/shard_map/gather/pallas_call | solution.py:468
  1.6 2.7 %collective-permute-start.3 = (f32[8,128]{1,0:T(8,128)}, f32[8,128]{1,0:T(8,128)S(1)}, u32[]{:S(2)}, u32[]{:S(2)}) collective-permute-start(f32[8,128]{1,0:T(8,128)} %get-tuple-element.31), channel_id=1, source_target_pairs={{20,0},{21,1},{22,2},{23,3},{24,4},{25,5},{26,6},{27,7},{28,8},{29... | collective-permute-start | bytes 12296 | tf_op jit(solution)/shard_map/ppermute | solution.py:35
  4.3 2.4 %collective-permute-start.2 = (f32[8,128]{1,0:T(8,128)}, f32[8,128]{1,0:T(8,128)S(1)}, u32[]{:S(2)}, u32[]{:S(2)}) collective-permute-start(f32[8,128]{1,0:T(8,128)} %get-tuple-element.31), channel_id=1, source_target_pairs={{16,4},{17,5},{18,6},{19,7},{20,8},{21,9},{22,10},{23,11},{24,12},... | collective-permute-start | bytes 12296 | tf_op jit(solution)/shard_map/ppermute | solution.py:35
  6.7 0.7 %collective-permute-start = (f32[520,128]{1,0:T(8,128)}, f32[520,128]{1,0:T(8,128)S(1)}, u32[]{:S(2)}, u32[]{:S(2)}) collective-permute-start(f32[520,128]{1,0:T(8,128)} %get-tuple-element.29), channel_id=1, source_target_pairs={{0,1},{1,2},{2,3},{4,5},{5,6},{6,7},{8,9},{9,10},{10,11},{12,13},{... | collective-permute-start | bytes 798728 | tf_op jit(solution)/shard_map/ppermute | solution.py:35
  7.4 0.7 %collective-permute-start.1 = (f32[520,128]{1,0:T(8,128)}, f32[520,128]{1,0:T(8,128)S(1)}, u32[]{:S(2)}, u32[]{:S(2)}) collective-permute-start(f32[520,128]{1,0:T(8,128)} %get-tuple-element.30), channel_id=1, source_target_pairs={{1,0},{2,1},{3,2},{5,4},{6,5},{7,6},{9,8},{10,9},{11,10},{13,12},{... | collective-permute-start | bytes 798728 | tf_op jit(solution)/shard_map/ppermute | solution.py:35
  8.1 0.0 copy-start
  8.1 1.2 %copy-done = f32[1,512,512]{2,1,0:T(8,128)S(1)} copy-done((f32[1,512,512]{2,1,0:T(8,128)S(1)}, f32[1,512,512]{2,1,0:T(8,128)}, u32[]{:S(2)}) %copy-start) | copy-done | bytes 1048600
  9.3 1.3 %collective-permute-start.6 = (bf16[416,256]{1,0:T(8,128)(2,1)S(1)}, bf16[416,256]{1,0:T(8,128)(2,1)S(1)}, u32[]{:S(2)}, u32[]{:S(2)}) collective-permute-start(bf16[416,256]{1,0:T(8,128)(2,1)S(1)} %get-tuple-element.43), channel_id=1, source_target_pairs={{0,16},{1,17},{2,18},{3,19},{4,20},{5,21},{6,22},{7,23},{8,24},{9,... | collective-permute-start | bytes 638984 | tf_op jit(solution)/shard_map/ppermute | solution.py:35
  10.6 0.0 collective-permute-done.3.meta_down
  10.6 0.0 collective-permute-done.2.meta_up
  10.7 0.0 collective-permute-done.left
  10.7 0.0 collective-permute-done.1.right
  10.7 0.0 copy-start.1
  10.7 1.4 %collective-permute-start.7 = (bf16[544,256]{1,0:T(8,128)(2,1)S(1)}, bf16[544,256]{1,0:T(8,128)(2,1)S(1)}, u32[]{:S(2)}, u32[]{:S(2)}) collective-permute-start(bf16[544,256]{1,0:T(8,128)(2,1)S(1)} %get-tuple-element.44), channel_id=1, source_target_pairs={{0,16},{1,17},{2,18},{3,19},{4,20},{5,21},{6,22},{7,23},{8,24},{9,... | collective-permute-start | bytes 835592 | tf_op jit(solution)/shard_map/ppermute | solution.py:35
  12.2 1.3 %collective-permute-start.4 = (bf16[144,512]{1,0:T(8,128)(2,1)S(1)}, bf16[144,512]{1,0:T(8,128)(2,1)S(1)}, u32[]{:S(2)}, u32[]{:S(2)}) collective-permute-start(bf16[144,512]{1,0:T(8,128)(2,1)S(1)} %get-tuple-element.41.down_in), channel_id=1, source_target_pairs={{0,20},{1,21},{2,22},{3,23},{4,24},{5,25},{6,26},{7,27},{8,28},{9,... | collective-permute-start | bytes 442376 | tf_op jit(solution)/shard_map/ppermute | solution.py:35
  13.5 1.3 %collective-permute-start.5 = (bf16[144,512]{1,0:T(8,128)(2,1)S(1)}, bf16[144,512]{1,0:T(8,128)(2,1)S(1)}, u32[]{:S(2)}, u32[]{:S(2)}) collective-permute-start(bf16[144,512]{1,0:T(8,128)(2,1)S(1)} %get-tuple-element.42.up_in), channel_id=1, source_target_pairs={{4,16},{5,17},{6,18},{7,19},{8,20},{9,21},{10,22},{11,23},{12,24},... | collective-permute-start | bytes 442376 | tf_op jit(solution)/shard_map/ppermute | solution.py:35
  14.8 0.7 %collective-permute-start.8 = (bf16[128,512]{1,0:T(8,128)(2,1)S(1)}, bf16[128,512]{1,0:T(8,128)(2,1)S(1)}, u32[]{:S(2)}, u32[]{:S(2)}) collective-permute-start(bf16[128,512]{1,0:T(8,128)(2,1)S(1)} %get-tuple-element.47), channel_id=1, source_target_pairs={{0,4},{1,5},{2,6},{3,7},{4,8},{5,9},{6,10},{7,11},{8,12},{9,13},{1... | collective-permute-start | bytes 393224 | tf_op jit(solution)/shard_map/ppermute | solution.py:35
  15.5 12.1 %collective-permute-done.6.mid = bf16[416,256]{1,0:T(8,128)(2,1)S(1)} collective-permute-done((bf16[416,256]{1,0:T(8,128)(2,1)S(1)}, bf16[416,256]{1,0:T(8,128)(2,1)S(1)}, u32[]{:S(2)}, u32[]{:S(2)}) %collective-permute-start.6) | collective-permute-done | bytes 213024 | tf_op jit(solution)/shard_map/ppermute | solution.py:35
  27.6 0.7 %collective-permute-start.9 = (bf16[128,512]{1,0:T(8,128)(2,1)S(1)}, bf16[128,512]{1,0:T(8,128)(2,1)S(1)}, u32[]{:S(2)}, u32[]{:S(2)}) collective-permute-start(bf16[128,512]{1,0:T(8,128)(2,1)S(1)} %get-tuple-element.48), channel_id=1, source_target_pairs={{4,0},{5,1},{6,2},{7,3},{8,4},{9,5},{10,6},{11,7},{12,8},{13,9},{1... | collective-permute-start | bytes 393224 | tf_op jit(solution)/shard_map/ppermute | solution.py:35
  28.3 2.0 %matrices.1 = (bf16[16,128,640]{2,1,0:T(8,128)(2,1)S(1)}, bf16[512,256]{1,0:T(8,128)(2,1)S(1)}) custom-call(f32[32768,128]{1,0:T(8,128)} %get-tuple-element.27.meta_in, bf16[512,256]{1,0:T(8,128)(2,1)S(1)} %get-tuple-element.40.after.end_in.own_end), custom_call_target="tpu_custom_call" | custom-call | tf_op jit(solution)/shard_map/matrices/pallas_call | solution.py:518
  30.3 0.0 collective-permute-done.8.got_up
  30.3 0.0 collective-permute-done.9.got_down
  30.3 0.0 collective-permute-done.4.side_up
  30.3 0.0 collective-permute-done.5.side_down
  30.3 1.6 %collective-permute-done.7.end = bf16[544,256]{1,0:T(8,128)(2,1)S(1)} collective-permute-done((bf16[544,256]{1,0:T(8,128)(2,1)S(1)}, bf16[544,256]{1,0:T(8,128)(2,1)S(1)}, u32[]{:S(2)}, u32[]{:S(2)}) %collective-permute-start.7) | collective-permute-done | bytes 278560 | tf_op jit(solution)/shard_map/ppermute | solution.py:35
  32.0 0.0 copy-done.1
  32.0 2.5 %finish.1 = f32[512,512]{1,0:T(8,128)} custom-call(f32[512,512]{1,0:T(8,128)S(1)} %bitcast.6, bf16[512,256]{1,0:T(8,128)(2,1)S(1)} %get-tuple-element.28.own_mid, bf16[512,256]{1,0:T(8,128)(2,1)S(1)} %get-tuple-element.40.after.end_in.own_end, bf16[144,512]{1,0:T(8,128)(2,1)S(1)} %collective-permute-done.4.side_up, ...), custom_call_target="tpu_custom_call" | custom-call | tf_op jit(solution)/shard_map/finish/pallas_call | solution.py:525
  (3 shorter events, 0.0 us)
Async XLA Ops:
  1.6 9.1 %collective-permute-start.3 = (f32[8,128]{1,0:T(8,128)}, f32[8,128]{1,0:T(8,128)S(1)}, u32[]{:S(2)}, u32[]{:S(2)}) collective-permute-start(f32[8,128]{1,0:T(8,128)} %get-tuple-element.31), channel_id=1, source_target_pairs={{20,0},{21,1},{22,2},{23,3},{24,4},{25,5},{26,6},{27,7},{28,8},{29... | collective-permute-start | bytes 12296 | tf_op jit(solution)/shard_map/ppermute | solution.py:35
  4.3 6.4 %collective-permute-start.2 = (f32[8,128]{1,0:T(8,128)}, f32[8,128]{1,0:T(8,128)S(1)}, u32[]{:S(2)}, u32[]{:S(2)}) collective-permute-start(f32[8,128]{1,0:T(8,128)} %get-tuple-element.31), channel_id=1, source_target_pairs={{16,4},{17,5},{18,6},{19,7},{20,8},{21,9},{22,10},{23,11},{24,12},... | collective-permute-start | bytes 12296 | tf_op jit(solution)/shard_map/ppermute | solution.py:35
  6.7 3.9 %collective-permute-start = (f32[520,128]{1,0:T(8,128)}, f32[520,128]{1,0:T(8,128)S(1)}, u32[]{:S(2)}, u32[]{:S(2)}) collective-permute-start(f32[520,128]{1,0:T(8,128)} %get-tuple-element.29), channel_id=1, source_target_pairs={{0,1},{1,2},{2,3},{4,5},{5,6},{6,7},{8,9},{9,10},{10,11},{12,13},{... | collective-permute-start | bytes 798728 | tf_op jit(solution)/shard_map/ppermute | solution.py:35
  7.4 3.3 %collective-permute-start.1 = (f32[520,128]{1,0:T(8,128)}, f32[520,128]{1,0:T(8,128)S(1)}, u32[]{:S(2)}, u32[]{:S(2)}) collective-permute-start(f32[520,128]{1,0:T(8,128)} %get-tuple-element.30), channel_id=1, source_target_pairs={{1,0},{2,1},{3,2},{5,4},{6,5},{7,6},{9,8},{10,9},{11,10},{13,12},{... | collective-permute-start | bytes 798728 | tf_op jit(solution)/shard_map/ppermute | solution.py:35
  8.1 1.2 %copy-start = (f32[1,512,512]{2,1,0:T(8,128)S(1)}, f32[1,512,512]{2,1,0:T(8,128)}, u32[]{:S(2)}) copy-start(f32[1,512,512]{2,1,0:T(8,128)} %param.9) | copy-start | bytes 3145732
  9.3 18.3 %collective-permute-start.6 = (bf16[416,256]{1,0:T(8,128)(2,1)S(1)}, bf16[416,256]{1,0:T(8,128)(2,1)S(1)}, u32[]{:S(2)}, u32[]{:S(2)}) collective-permute-start(bf16[416,256]{1,0:T(8,128)(2,1)S(1)} %get-tuple-element.43), channel_id=1, source_target_pairs={{0,16},{1,17},{2,18},{3,19},{4,20},{5,21},{6,22},{7,23},{8,24},{9,... | collective-permute-start | bytes 638984 | tf_op jit(solution)/shard_map/ppermute | solution.py:35
  10.7 21.3 %copy-start.1 = (f32[1,512,512]{2,1,0:T(8,128)S(1)}, f32[1,512,512]{2,1,0:T(8,128)}, u32[]{:S(2)}) copy-start(f32[1,512,512]{2,1,0:T(8,128)} %param.9) | copy-start | bytes 3145732
  10.7 21.2 %collective-permute-start.7 = (bf16[544,256]{1,0:T(8,128)(2,1)S(1)}, bf16[544,256]{1,0:T(8,128)(2,1)S(1)}, u32[]{:S(2)}, u32[]{:S(2)}) collective-permute-start(bf16[544,256]{1,0:T(8,128)(2,1)S(1)} %get-tuple-element.44), channel_id=1, source_target_pairs={{0,16},{1,17},{2,18},{3,19},{4,20},{5,21},{6,22},{7,23},{8,24},{9,... | collective-permute-start | bytes 835592 | tf_op jit(solution)/shard_map/ppermute | solution.py:35
  12.2 18.2 %collective-permute-start.4 = (bf16[144,512]{1,0:T(8,128)(2,1)S(1)}, bf16[144,512]{1,0:T(8,128)(2,1)S(1)}, u32[]{:S(2)}, u32[]{:S(2)}) collective-permute-start(bf16[144,512]{1,0:T(8,128)(2,1)S(1)} %get-tuple-element.41.down_in), channel_id=1, source_target_pairs={{0,20},{1,21},{2,22},{3,23},{4,24},{5,25},{6,26},{7,27},{8,28},{9,... | collective-permute-start | bytes 442376 | tf_op jit(solution)/shard_map/ppermute | solution.py:35
  13.5 16.9 %collective-permute-start.5 = (bf16[144,512]{1,0:T(8,128)(2,1)S(1)}, bf16[144,512]{1,0:T(8,128)(2,1)S(1)}, u32[]{:S(2)}, u32[]{:S(2)}) collective-permute-start(bf16[144,512]{1,0:T(8,128)(2,1)S(1)} %get-tuple-element.42.up_in), channel_id=1, source_target_pairs={{4,16},{5,17},{6,18},{7,19},{8,20},{9,21},{10,22},{11,23},{12,24},... | collective-permute-start | bytes 442376 | tf_op jit(solution)/shard_map/ppermute | solution.py:35
  14.8 15.5 %collective-permute-start.8 = (bf16[128,512]{1,0:T(8,128)(2,1)S(1)}, bf16[128,512]{1,0:T(8,128)(2,1)S(1)}, u32[]{:S(2)}, u32[]{:S(2)}) collective-permute-start(bf16[128,512]{1,0:T(8,128)(2,1)S(1)} %get-tuple-element.47), channel_id=1, source_target_pairs={{0,4},{1,5},{2,6},{3,7},{4,8},{5,9},{6,10},{7,11},{8,12},{9,13},{1... | collective-permute-start | bytes 393224 | tf_op jit(solution)/shard_map/ppermute | solution.py:35
  27.6 2.7 %collective-permute-start.9 = (bf16[128,512]{1,0:T(8,128)(2,1)S(1)}, bf16[128,512]{1,0:T(8,128)(2,1)S(1)}, u32[]{:S(2)}, u32[]{:S(2)}) collective-permute-start(bf16[128,512]{1,0:T(8,128)(2,1)S(1)} %get-tuple-element.48), channel_id=1, source_target_pairs={{4,0},{5,1},{6,2},{7,3},{8,4},{9,5},{10,6},{11,7},{12,8},{13,9},{1... | collective-permute-start | bytes 393224 | tf_op jit(solution)/shard_map/ppermute | solution.py:35

commit v6 on v5

--- a/solution.py
+++ b/solution.py
@@ -154,8 +154,12 @@
     rows.wait()
 
 
+def marker_kernel(meta_in, mark):
+    mark[...] = jnp.zeros_like(mark)
+
+
 def center_kernel(
-    nb, frame, meta_in,
+    nb, frame, meta_in, mark,
     own, across, tip_hi, tip_lo, mid_hi, mid_lo, row_hi, row_lo, edge_hi, edge_lo,
     meta, src_hi, src_lo, sem,
 ):
@@ -484,6 +488,9 @@
     meta_down = moved(row_meta, (-1, -1, 0), (1,))
     left = moved(to_right, (0, 0, 1), (0,))
     right = moved(to_left, (0, 0, -1), (0,))
+    mark = call(
+        marker_kernel, "marker", shape((8, BLK), F32), [ANY], flops=1 << 31,
+    )(meta)
     own_mid, mid, *parts = call(
         functools.partial(center_kernel, nb), "center",
         (shape((side, inner), BF16), shape((kept, inner), BF16))
@@ -491,13 +498,13 @@
         + (shape((side, inner), BF16),) * 2
         + (shape((side, side), BF16),) * 2
         + (shape((4 * BLK, BLK), BF16),) * 2,
-        [VM, ANY],
+        [VM, ANY, ANY],
         [
             meta_shape, pltpu.VMEM((side, side), BF16), pltpu.VMEM((side, side), BF16),
             pltpu.SemaphoreType.DMA(()),
         ],
         flops=1 << 33,
-    )(frame, meta)
+    )(frame, meta, mark)
     mid = moved(mid, (1, 0, 0), (0,))
     own_end, end, to_up, to_down = call(
         functools.partial(edge_kernel, nb, nx, ny), "edges",

time: 34.9 us -> 33.9 us (0.971)
  local copies, waits for them, and re-layouts: 1.23 us -> 0.01 us
    unnamed x4 -> x2, local copies, waits for them, and re-layouts: 1.23 us -> 0.01 us
where the time goes in v6:
time: 33.9 us; the launch traced here: 33.3 us
  waiting for transfers between devices  13.9 us (41%)
  starting transfers between devices  13.1 us (39%)
  Pallas kernels  6.08 us (18%)
    ppermute x10, waiting for transfers between devices, moved(): return lax.ppermute(block, axes, route)  13.9 us
    ppermute x10, starting transfers between devices, moved(): return lax.ppermute(block, axes, route)  13.1 us
    pallas_call x1, Pallas kernels, local(): pl.pallas_call(functools.partial(finish_kernel, nb, nu), out_shape=shape(...  2.44 us
    pallas_call x1, Pallas kernels, local(): call(functools.partial(matrices_kernel, nb, nu, nv, sets), 'matrices', (s...  2.03 us
    pallas_call x1, Pallas kernels, local(): pl.pallas_call(functools.partial(gather_kernel, nb), out_shape=(shape((SP...  1.55 us
  transfers between devices with their start and end apart: 10, of which 2 were waited for; matrix products, arithmetic and copies ran while one was open for 0% of the time, Pallas kernels for 6%

profile of v6, /device:TPU:14, one launch (start us, length us, event | category | flops | bytes accessed | tf_op | source)
XLA Modules:
  0.0 33.3 jit_solution(4147108129751168952)
XLA Ops:
  0.0 1.5 %gather.1 = (f32[32768,128]{1,0:T(8,128)}, f32[8,128]{1,0:T(8,128)}, f32[520,128]{1,0:T(8,128)}, f32[520,128]{1,0:T(8,128)}) custom-call(f32[512,512]{1,0:T(8,128)} %bitcast.4, f32[4,128]{1,0:T(4,128)} %bitcast.7, f32[4,128]{1,0:T(4,128)} %bitcast.8, s32[4]{0:T(128)} %row_shift.1, s32[4]{0:T(128)} %col_shift.1, f32[16,32]{1,0:T(8,128)} %table.1, ...), custom_call_target="tpu_custom_call" | custom-call | tf_op jit(solution)/shard_map/gather/pallas_call | solution.py:472
  1.6 0.0 copy-start
  1.6 2.9 %collective-permute-start.3 = (f32[8,128]{1,0:T(8,128)}, f32[8,128]{1,0:T(8,128)S(1)}, u32[]{:S(2)}, u32[]{:S(2)}) collective-permute-start(f32[8,128]{1,0:T(8,128)} %get-tuple-element.31), channel_id=1, source_target_pairs={{20,0},{21,1},{22,2},{23,3},{24,4},{25,5},{26,6},{27,7},{28,8},{29... | collective-permute-start | bytes 12296 | tf_op jit(solution)/shard_map/ppermute | solution.py:35
  4.4 2.4 %collective-permute-start.2 = (f32[8,128]{1,0:T(8,128)}, f32[8,128]{1,0:T(8,128)S(1)}, u32[]{:S(2)}, u32[]{:S(2)}) collective-permute-start(f32[8,128]{1,0:T(8,128)} %get-tuple-element.31), channel_id=1, source_target_pairs={{16,4},{17,5},{18,6},{19,7},{20,8},{21,9},{22,10},{23,11},{24,12},... | collective-permute-start | bytes 12296 | tf_op jit(solution)/shard_map/ppermute | solution.py:35
  6.9 0.7 %collective-permute-start = (f32[520,128]{1,0:T(8,128)}, f32[520,128]{1,0:T(8,128)S(1)}, u32[]{:S(2)}, u32[]{:S(2)}) collective-permute-start(f32[520,128]{1,0:T(8,128)} %get-tuple-element.29), channel_id=1, source_target_pairs={{0,1},{1,2},{2,3},{4,5},{5,6},{6,7},{8,9},{9,10},{10,11},{12,13},{... | collective-permute-start | bytes 798728 | tf_op jit(solution)/shard_map/ppermute | solution.py:35
  7.6 0.7 %collective-permute-start.1 = (f32[520,128]{1,0:T(8,128)}, f32[520,128]{1,0:T(8,128)S(1)}, u32[]{:S(2)}, u32[]{:S(2)}) collective-permute-start(f32[520,128]{1,0:T(8,128)} %get-tuple-element.30), channel_id=1, source_target_pairs={{1,0},{2,1},{3,2},{5,4},{6,5},{7,6},{9,8},{10,9},{11,10},{13,12},{... | collective-permute-start | bytes 798728 | tf_op jit(solution)/shard_map/ppermute | solution.py:35
  8.2 0.0 copy-done
  8.3 1.3 %collective-permute-start.6 = (bf16[416,256]{1,0:T(8,128)(2,1)S(1)}, bf16[416,256]{1,0:T(8,128)(2,1)S(1)}, u32[]{:S(2)}, u32[]{:S(2)}) collective-permute-start(bf16[416,256]{1,0:T(8,128)(2,1)S(1)} %get-tuple-element.43), channel_id=1, source_target_pairs={{0,16},{1,17},{2,18},{3,19},{4,20},{5,21},{6,22},{7,23},{8,24},{9,... | collective-permute-start | bytes 638984 | tf_op jit(solution)/shard_map/ppermute | solution.py:35
  9.6 0.0 collective-permute-done.3.meta_down
  9.6 0.0 collective-permute-done.2.meta_up
  9.6 0.0 collective-permute-done.left
  9.6 0.0 collective-permute-done.1.right
  9.7 1.3 %collective-permute-start.7 = (bf16[544,256]{1,0:T(8,128)(2,1)S(1)}, bf16[544,256]{1,0:T(8,128)(2,1)S(1)}, u32[]{:S(2)}, u32[]{:S(2)}) collective-permute-start(bf16[544,256]{1,0:T(8,128)(2,1)S(1)} %get-tuple-element.44), channel_id=1, source_target_pairs={{0,16},{1,17},{2,18},{3,19},{4,20},{5,21},{6,22},{7,23},{8,24},{9,... | collective-permute-start | bytes 835592 | tf_op jit(solution)/shard_map/ppermute | solution.py:35
  11.0 1.3 %collective-permute-start.4 = (bf16[144,512]{1,0:T(8,128)(2,1)S(1)}, bf16[144,512]{1,0:T(8,128)(2,1)S(1)}, u32[]{:S(2)}, u32[]{:S(2)}) collective-permute-start(bf16[144,512]{1,0:T(8,128)(2,1)S(1)} %get-tuple-element.41.down_in), channel_id=1, source_target_pairs={{0,20},{1,21},{2,22},{3,23},{4,24},{5,25},{6,26},{7,27},{8,28},{9,... | collective-permute-start | bytes 442376 | tf_op jit(solution)/shard_map/ppermute | solution.py:35
  12.3 1.3 %collective-permute-start.5 = (bf16[144,512]{1,0:T(8,128)(2,1)S(1)}, bf16[144,512]{1,0:T(8,128)(2,1)S(1)}, u32[]{:S(2)}, u32[]{:S(2)}) collective-permute-start(bf16[144,512]{1,0:T(8,128)(2,1)S(1)} %get-tuple-element.42.up_in), channel_id=1, source_target_pairs={{4,16},{5,17},{6,18},{7,19},{8,20},{9,21},{10,22},{11,23},{12,24},... | collective-permute-start | bytes 442376 | tf_op jit(solution)/shard_map/ppermute | solution.py:35
  13.6 0.7 %collective-permute-start.8 = (bf16[128,512]{1,0:T(8,128)(2,1)S(1)}, bf16[128,512]{1,0:T(8,128)(2,1)S(1)}, u32[]{:S(2)}, u32[]{:S(2)}) collective-permute-start(bf16[128,512]{1,0:T(8,128)(2,1)S(1)} %get-tuple-element.47), channel_id=1, source_target_pairs={{0,4},{1,5},{2,6},{3,7},{4,8},{5,9},{6,10},{7,11},{8,12},{9,13},{1... | collective-permute-start | bytes 393224 | tf_op jit(solution)/shard_map/ppermute | solution.py:35
  14.3 12.3 %collective-permute-done.6.mid = bf16[416,256]{1,0:T(8,128)(2,1)S(1)} collective-permute-done((bf16[416,256]{1,0:T(8,128)(2,1)S(1)}, bf16[416,256]{1,0:T(8,128)(2,1)S(1)}, u32[]{:S(2)}, u32[]{:S(2)}) %collective-permute-start.6) | collective-permute-done | bytes 213024 | tf_op jit(solution)/shard_map/ppermute | solution.py:35
  26.6 0.7 %collective-permute-start.9 = (bf16[128,512]{1,0:T(8,128)(2,1)S(1)}, bf16[128,512]{1,0:T(8,128)(2,1)S(1)}, u32[]{:S(2)}, u32[]{:S(2)}) collective-permute-start(bf16[128,512]{1,0:T(8,128)(2,1)S(1)} %get-tuple-element.48), channel_id=1, source_target_pairs={{4,0},{5,1},{6,2},{7,3},{8,4},{9,5},{10,6},{11,7},{12,8},{13,9},{1... | collective-permute-start | bytes 393224 | tf_op jit(solution)/shard_map/ppermute | solution.py:35
  27.3 2.0 %matrices.1 = (bf16[16,128,640]{2,1,0:T(8,128)(2,1)S(1)}, bf16[512,256]{1,0:T(8,128)(2,1)S(1)}) custom-call(f32[32768,128]{1,0:T(8,128)} %get-tuple-element.27.meta_in, bf16[512,256]{1,0:T(8,128)(2,1)S(1)} %get-tuple-element.40.after.end_in.own_end), custom_call_target="tpu_custom_call" | custom-call | tf_op jit(solution)/shard_map/matrices/pallas_call | solution.py:525
  29.3 0.0 collective-permute-done.8.got_up
  29.3 0.0 collective-permute-done.9.got_down
  29.3 0.0 collective-permute-done.4.side_up
  29.3 0.0 collective-permute-done.5.side_down
  29.3 1.6 %collective-permute-done.7.end = bf16[544,256]{1,0:T(8,128)(2,1)S(1)} collective-permute-done((bf16[544,256]{1,0:T(8,128)(2,1)S(1)}, bf16[544,256]{1,0:T(8,128)(2,1)S(1)}, u32[]{:S(2)}, u32[]{:S(2)}) %collective-permute-start.7) | collective-permute-done | bytes 278560 | tf_op jit(solution)/shard_map/ppermute | solution.py:35
  30.9 2.4 %finish.1 = f32[512,512]{1,0:T(8,128)} custom-call(f32[512,512]{1,0:T(8,128)S(1)} %bitcast.6, bf16[512,256]{1,0:T(8,128)(2,1)S(1)} %get-tuple-element.28.own_mid, bf16[512,256]{1,0:T(8,128)(2,1)S(1)} %get-tuple-element.40.after.end_in.own_end, bf16[144,512]{1,0:T(8,128)(2,1)S(1)} %collective-permute-done.4.side_up, ...), custom_call_target="tpu_custom_call" | custom-call | tf_op jit(solution)/shard_map/finish/pallas_call | solution.py:532
  (4 shorter events, 0.1 us)
Async XLA Ops:
  1.6 6.7 %copy-start = (f32[1,512,512]{2,1,0:T(8,128)S(1)}, f32[1,512,512]{2,1,0:T(8,128)}, u32[]{:S(2)}) copy-start(f32[1,512,512]{2,1,0:T(8,128)} %param.9) | copy-start | bytes 3145732
  1.6 8.0 %collective-permute-start.3 = (f32[8,128]{1,0:T(8,128)}, f32[8,128]{1,0:T(8,128)S(1)}, u32[]{:S(2)}, u32[]{:S(2)}) collective-permute-start(f32[8,128]{1,0:T(8,128)} %get-tuple-element.31), channel_id=1, source_target_pairs={{20,0},{21,1},{22,2},{23,3},{24,4},{25,5},{26,6},{27,7},{28,8},{29... | collective-permute-start | bytes 12296 | tf_op jit(solution)/shard_map/ppermute | solution.py:35
  4.4 5.2 %collective-permute-start.2 = (f32[8,128]{1,0:T(8,128)}, f32[8,128]{1,0:T(8,128)S(1)}, u32[]{:S(2)}, u32[]{:S(2)}) collective-permute-start(f32[8,128]{1,0:T(8,128)} %get-tuple-element.31), channel_id=1, source_target_pairs={{16,4},{17,5},{18,6},{19,7},{20,8},{21,9},{22,10},{23,11},{24,12},... | collective-permute-start | bytes 12296 | tf_op jit(solution)/shard_map/ppermute | solution.py:35
  6.9 2.8 %collective-permute-start = (f32[520,128]{1,0:T(8,128)}, f32[520,128]{1,0:T(8,128)S(1)}, u32[]{:S(2)}, u32[]{:S(2)}) collective-permute-start(f32[520,128]{1,0:T(8,128)} %get-tuple-element.29), channel_id=1, source_target_pairs={{0,1},{1,2},{2,3},{4,5},{5,6},{6,7},{8,9},{9,10},{10,11},{12,13},{... | collective-permute-start | bytes 798728 | tf_op jit(solution)/shard_map/ppermute | solution.py:35
  7.6 2.1 %collective-permute-start.1 = (f32[520,128]{1,0:T(8,128)}, f32[520,128]{1,0:T(8,128)S(1)}, u32[]{:S(2)}, u32[]{:S(2)}) collective-permute-start(f32[520,128]{1,0:T(8,128)} %get-tuple-element.30), channel_id=1, source_target_pairs={{1,0},{2,1},{3,2},{5,4},{6,5},{7,6},{9,8},{10,9},{11,10},{13,12},{... | collective-permute-start | bytes 798728 | tf_op jit(solution)/shard_map/ppermute | solution.py:35
  8.3 18.3 %collective-permute-start.6 = (bf16[416,256]{1,0:T(8,128)(2,1)S(1)}, bf16[416,256]{1,0:T(8,128)(2,1)S(1)}, u32[]{:S(2)}, u32[]{:S(2)}) collective-permute-start(bf16[416,256]{1,0:T(8,128)(2,1)S(1)} %get-tuple-element.43), channel_id=1, source_target_pairs={{0,16},{1,17},{2,18},{3,19},{4,20},{5,21},{6,22},{7,23},{8,24},{9,... | collective-permute-start | bytes 638984 | tf_op jit(solution)/shard_map/ppermute | solution.py:35
  9.7 21.2 %collective-permute-start.7 = (bf16[544,256]{1,0:T(8,128)(2,1)S(1)}, bf16[544,256]{1,0:T(8,128)(2,1)S(1)}, u32[]{:S(2)}, u32[]{:S(2)}) collective-permute-start(bf16[544,256]{1,0:T(8,128)(2,1)S(1)} %get-tuple-element.44), channel_id=1, source_target_pairs={{0,16},{1,17},{2,18},{3,19},{4,20},{5,21},{6,22},{7,23},{8,24},{9,... | collective-permute-start | bytes 835592 | tf_op jit(solution)/shard_map/ppermute | solution.py:35
  11.0 18.3 %collective-permute-start.4 = (bf16[144,512]{1,0:T(8,128)(2,1)S(1)}, bf16[144,512]{1,0:T(8,128)(2,1)S(1)}, u32[]{:S(2)}, u32[]{:S(2)}) collective-permute-start(bf16[144,512]{1,0:T(8,128)(2,1)S(1)} %get-tuple-element.41.down_in), channel_id=1, source_target_pairs={{0,20},{1,21},{2,22},{3,23},{4,24},{5,25},{6,26},{7,27},{8,28},{9,... | collective-permute-start | bytes 442376 | tf_op jit(solution)/shard_map/ppermute | solution.py:35
  12.3 17.1 %collective-permute-start.5 = (bf16[144,512]{1,0:T(8,128)(2,1)S(1)}, bf16[144,512]{1,0:T(8,128)(2,1)S(1)}, u32[]{:S(2)}, u32[]{:S(2)}) collective-permute-start(bf16[144,512]{1,0:T(8,128)(2,1)S(1)} %get-tuple-element.42.up_in), channel_id=1, source_target_pairs={{4,16},{5,17},{6,18},{7,19},{8,20},{9,21},{10,22},{11,23},{12,24},... | collective-permute-start | bytes 442376 | tf_op jit(solution)/shard_map/ppermute | solution.py:35
  13.6 15.7 %collective-permute-start.8 = (bf16[128,512]{1,0:T(8,128)(2,1)S(1)}, bf16[128,512]{1,0:T(8,128)(2,1)S(1)}, u32[]{:S(2)}, u32[]{:S(2)}) collective-permute-start(bf16[128,512]{1,0:T(8,128)(2,1)S(1)} %get-tuple-element.47), channel_id=1, source_target_pairs={{0,4},{1,5},{2,6},{3,7},{4,8},{5,9},{6,10},{7,11},{8,12},{9,13},{1... | collective-permute-start | bytes 393224 | tf_op jit(solution)/shard_map/ppermute | solution.py:35
  26.6 2.7 %collective-permute-start.9 = (bf16[128,512]{1,0:T(8,128)(2,1)S(1)}, bf16[128,512]{1,0:T(8,128)(2,1)S(1)}, u32[]{:S(2)}, u32[]{:S(2)}) collective-permute-start(bf16[128,512]{1,0:T(8,128)(2,1)S(1)} %get-tuple-element.48), channel_id=1, source_target_pairs={{4,0},{5,1},{6,2},{7,3},{8,4},{9,5},{10,6},{11,7},{12,8},{13,9},{1... | collective-permute-start | bytes 393224 | tf_op jit(solution)/shard_map/ppermute | solution.py:35

commit v7 on v6

--- a/solution.py
+++ b/solution.py
@@ -11,7 +11,7 @@
 BLK = 128
 KW = 31
 HALF = 15
-ROW0 = 48
+ROW0 = 56
 F32 = jnp.float32
 BF16 = jnp.bfloat16
 HIGHEST = lax.Precision.HIGHEST
@@ -192,11 +192,11 @@
             mat = split(banded(weights[nb + b], row_shift[b], depth, (first - b) * BLK).T)
             rows, cols = slice(b * BLK, (b + 1) * BLK), slice(first * BLK, first * BLK + depth)
             row_hi[rows, cols], row_lo[rows, cols] = mat
-            got = dot3(mat, (mid_hi[cols, :], mid_lo[cols, :]), MATMUL).astype(BF16)
-            own[rows, :] = got
+            got = dot3(mat, (mid_hi[cols, :], mid_lo[cols, :]), MATMUL)
+            own[rows, :] = got.astype(BF16)
             low = max(b * BLK, ROW0)
             high = min((b + 1) * BLK, side - ROW0)
-            across[low - ROW0 : high - ROW0, :] = got[low - b * BLK : high - b * BLK, :]
+            across[low - ROW0 : high - ROW0, :] = got[low - b * BLK : high - b * BLK, :].astype(BF16)
         for n, (b, offset) in enumerate(((0, -BLK), (nb - 1, 0))):
             hi, lo = split(banded(weights[b], col_shift[b], 2 * BLK, offset))
             edge_hi[n * 2 * BLK : (n + 1) * 2 * BLK, :] = hi
@@ -240,7 +240,8 @@
         padded[0:nu, 0:KW] = prof_cols
         for p in range(nu):
             row = jnp.broadcast_to(padded[p : p + 1, : 2 * BLK], (BLK, 2 * BLK))
-            band[p * BLK : (p + 1) * BLK, :] = pltpu.roll(row, 1, 1, stride=1, stride_axis=0).astype(BF16)
+            turned = pltpu.roll(row, 1, 1, stride=1, stride_axis=0).T
+            band[:, p * BLK : (p + 1) * BLK] = turned.astype(BF16)
 
 
 def edge_kernel(
@@ -299,8 +300,8 @@
             out[:BLK, :BLK] = got[:, inner : inner + BLK].astype(BF16)
             out[:BLK, side - BLK :] = got[:, inner + BLK : side].astype(BF16)
             turned = got[:, side:].T
-            out[BLK:, :BLK] = turned[:16].astype(BF16)
-            out[BLK:, BLK : 2 * BLK] = turned[BLK - 16 :].astype(BF16)
+            for k, row in enumerate((0, 8, BLK - 16, BLK - 8)):
+                out[BLK:, k * BLK : (k + 1) * BLK] = turned[row : row + 8].astype(BF16)
         across[kept : kept + 16, :] = side_down[:16, :half]
         across[kept + 16 : kept + 32, :] = side_up[BLK - 16 : BLK, :half]
         across[kept + 32 : kept + 48, :] = side_down[:16, half:]
@@ -310,11 +311,11 @@
             first, depth = (b, BLK) if b in (0, nb - 1) else (b - 1, 3 * BLK)
             rows, cols = slice(b * BLK, (b + 1) * BLK), slice(first * BLK, first * BLK + depth)
             mat = (row_hi[rows, cols], row_lo[rows, cols])
-            got = dot3(mat, (end_hi[cols, : 2 * BLK], end_lo[cols, : 2 * BLK]), MATMUL).astype(BF16)
-            own[rows, :] = got
+            got = dot3(mat, (end_hi[cols, : 2 * BLK], end_lo[cols, : 2 * BLK]), MATMUL)
+            own[rows, :] = got.astype(BF16)
             low = max(b * BLK, ROW0)
             high = min((b + 1) * BLK, side - ROW0)
-            across[low - ROW0 : high - ROW0, :] = got[low - b * BLK : high - b * BLK, :]
+            across[low - ROW0 : high - ROW0, :] = got[low - b * BLK : high - b * BLK, :].astype(BF16)
             strips.append(packed3(mat, (end_hi[cols, 2 * BLK :], end_lo[cols, 2 * BLK :])))
         strip = jnp.concatenate(strips, axis=0)
         strip = jnp.concatenate(
@@ -373,16 +374,15 @@
         both = BLK - ROW0
         stop = 16 + side
 
-        def added(one, two):
-            return (one.astype(F32) + two.astype(F32)).astype(BF16)
-
         def fill(at, width, own, above, below):
             cols = slice(at, at + width)
-            wide[16 : 16 + ROW0, cols] = above[:ROW0]
-            wide[16 + ROW0 : 16 + BLK, cols] = added(own[:both], above[ROW0:])
-            wide[16 + BLK : 16 + last, cols] = own[both : kept - both]
-            wide[16 + last : stop - ROW0, cols] = added(own[kept - both :], below[:both])
-            wide[stop - ROW0 : stop, cols] = below[both:]
+            own = own.astype(F32)
+            above, below = above.astype(F32), below.astype(F32)
+            top = jnp.concatenate([above[:ROW0], own[:both] + above[ROW0:]], axis=0)
+            bottom = jnp.concatenate([own[kept - both :] + below[:both], below[both:]], axis=0)
+            wide[16 : 16 + BLK, cols] = top.astype(BF16)
+            wide[16 + BLK : 16 + last, cols] = own[both : kept - both].astype(BF16)
+            wide[16 + last : stop, cols] = bottom.astype(BF16)
 
         fill(BLK, side - 2 * BLK, mid[:kept, :], side_up[:BLK, BLK:last], side_down[:BLK, BLK:last])
         fill(0, BLK, end[:kept, :BLK], side_up[:BLK, :BLK], side_down[:BLK, :BLK])
@@ -401,20 +401,25 @@
             ).astype(BF16)
 
         base = kept + 64
-        own = jnp.concatenate([turned(end[base : base + 32, :]), turned(end[base + 32 : base + 64, :])], axis=0)
+        own = jnp.concatenate(
+            [turned(end[base : base + 32, :]), turned(end[base + 32 : base + 64, :])], axis=0
+        ).astype(F32)
         above, below = (
-            turned(jnp.concatenate([part[BLK:, :BLK], part[BLK:, BLK : 2 * BLK]], axis=0))
+            turned(
+                jnp.concatenate(
+                    [part[BLK:, k * BLK : (k + 1) * BLK].astype(F32) for k in range(4)], axis=0
+                ).astype(BF16)
+            )
             for part in (side_up, side_down)
         )
         fill(side, BLK, own[ROW0 : side - ROW0], above, below)
-        wide[:16, side:] = own[ROW0 - 16 : ROW0]
-        wide[stop:, side:] = own[side - ROW0 : side - ROW0 + 16]
+        wide[:16, side:] = own[ROW0 - 16 : ROW0].astype(BF16)
+        wide[stop:, side:] = own[side - ROW0 : side - ROW0 + 16].astype(BF16)
         cut = side + BLK - 16
         full[...] = jnp.concatenate([wide[:, cut:], wide[:, :cut]], axis=1)
         for bj in range(nb):
-            got = lax.dot_general(
-                full[:, bj * BLK : (bj + 2) * BLK], band[...], (((1,), (1,)), ((), ())),
-                preferred_element_type=F32,
+            got = jnp.dot(
+                full[:, bj * BLK : (bj + 2) * BLK], band[...], preferred_element_type=F32
             ).astype(BF16)
             for p in range(nu):
                 passed[p, :, bj * BLK : (bj + 1) * BLK] = got[:, p * BLK : (p + 1) * BLK]
@@ -509,7 +514,7 @@
     own_end, end, to_up, to_down = call(
         functools.partial(edge_kernel, nb, nx, ny), "edges",
         (shape((side, 2 * BLK), BF16), shape((kept + 128, side // 2), BF16))
-        + (shape((BLK + 16, side), BF16),) * 2,
+        + (shape((BLK + 8, side), BF16),) * 2,
         [VM] * 12,
         [pltpu.VMEM((side, 3 * BLK), BF16)] * 2,
         flops=1 << 33,
@@ -524,7 +529,7 @@
     got_up = moved(to_down, (0, 1, 0), (0,))
     kernels, band = call(
         functools.partial(matrices_kernel, nb, nu, nv, sets), "matrices",
-        (shape((cells, BLK, width), BF16), shape((nu * BLK, 2 * BLK), BF16)),
+        (shape((cells, BLK, width), BF16), shape((2 * BLK, nu * BLK), BF16)),
         [ANY, VM],
         [pltpu.VMEM((8, width), F32), meta_shape, pltpu.SemaphoreType.DMA(())],
         flops=0,

time: 33.9 us -> 33.2 us (0.979)
  waiting for transfers between devices: 13.9 us -> 13.1 us
    ppermute x10, waiting for transfers between devices: 13.9 us -> 13.1 us  [moved(): return lax.ppermute(block, axes, route)]
  transfers between devices with their start and end apart: 10 -> 10, of which waited for: 2 -> 2; matrix products, arithmetic and copies ran while one was open for 0% -> 0% of each run, Pallas kernels for 6% -> 7%
where the time goes in v7:
time: 33.2 us; the launch traced here: 32.6 us
  starting transfers between devices  13.1 us (39%)
  waiting for transfers between devices  13.1 us (39%)
  Pallas kernels  6.19 us (19%)
    ppermute x10, starting transfers between devices, moved(): return lax.ppermute(block, axes, route)  13.1 us
    ppermute x10, waiting for transfers between devices, moved(): return lax.ppermute(block, axes, route)  13.1 us
    pallas_call x1, Pallas kernels, local(): pl.pallas_call(functools.partial(finish_kernel, nb, nu), out_shape=shape(...  2.44 us
    pallas_call x1, Pallas kernels, local(): call(functools.partial(matrices_kernel, nb, nu, nv, sets), 'matrices', (s...  2.13 us
    pallas_call x1, Pallas kernels, local(): pl.pallas_call(functools.partial(gather_kernel, nb), out_shape=(shape((SP...  1.55 us
  transfers between devices with their start and end apart: 10, of which 2 were waited for; matrix products, arithmetic and copies ran while one was open for 0% of the time, Pallas kernels for 7%

profile of v7, /device:TPU:14, one launch (start us, length us, event | category | flops | bytes accessed | tf_op | source)
XLA Modules:
  0.0 32.6 jit_solution(12148203054395185874)
XLA Ops:
  0.0 1.5 %gather.1 = (f32[32768,128]{1,0:T(8,128)}, f32[8,128]{1,0:T(8,128)}, f32[520,128]{1,0:T(8,128)}, f32[520,128]{1,0:T(8,128)}) custom-call(f32[512,512]{1,0:T(8,128)} %bitcast.4, f32[4,128]{1,0:T(4,128)} %bitcast.7, f32[4,128]{1,0:T(4,128)} %bitcast.8, s32[4]{0:T(128)} %row_shift.1, s32[4]{0:T(128)} %col_shift.1, f32[16,32]{1,0:T(8,128)} %table.1, ...), custom_call_target="tpu_custom_call" | custom-call | tf_op jit(solution)/shard_map/gather/pallas_call | solution.py:477
  1.6 0.0 copy-start
  1.6 2.9 %collective-permute-start.3 = (f32[8,128]{1,0:T(8,128)}, f32[8,128]{1,0:T(8,128)S(1)}, u32[]{:S(2)}, u32[]{:S(2)}) collective-permute-start(f32[8,128]{1,0:T(8,128)} %get-tuple-element.31), channel_id=1, source_target_pairs={{20,0},{21,1},{22,2},{23,3},{24,4},{25,5},{26,6},{27,7},{28,8},{29... | collective-permute-start | bytes 12296 | tf_op jit(solution)/shard_map/ppermute | solution.py:35
  4.4 2.4 %collective-permute-start.2 = (f32[8,128]{1,0:T(8,128)}, f32[8,128]{1,0:T(8,128)S(1)}, u32[]{:S(2)}, u32[]{:S(2)}) collective-permute-start(f32[8,128]{1,0:T(8,128)} %get-tuple-element.31), channel_id=1, source_target_pairs={{16,4},{17,5},{18,6},{19,7},{20,8},{21,9},{22,10},{23,11},{24,12},... | collective-permute-start | bytes 12296 | tf_op jit(solution)/shard_map/ppermute | solution.py:35
  6.9 0.7 %collective-permute-start = (f32[520,128]{1,0:T(8,128)}, f32[520,128]{1,0:T(8,128)S(1)}, u32[]{:S(2)}, u32[]{:S(2)}) collective-permute-start(f32[520,128]{1,0:T(8,128)} %get-tuple-element.29), channel_id=1, source_target_pairs={{0,1},{1,2},{2,3},{4,5},{5,6},{6,7},{8,9},{9,10},{10,11},{12,13},{... | collective-permute-start | bytes 798728 | tf_op jit(solution)/shard_map/ppermute | solution.py:35
  7.6 0.7 %collective-permute-start.1 = (f32[520,128]{1,0:T(8,128)}, f32[520,128]{1,0:T(8,128)S(1)}, u32[]{:S(2)}, u32[]{:S(2)}) collective-permute-start(f32[520,128]{1,0:T(8,128)} %get-tuple-element.30), channel_id=1, source_target_pairs={{1,0},{2,1},{3,2},{5,4},{6,5},{7,6},{9,8},{10,9},{11,10},{13,12},{... | collective-permute-start | bytes 798728 | tf_op jit(solution)/shard_map/ppermute | solution.py:35
  8.2 0.0 copy-done
  8.3 1.3 %collective-permute-start.6 = (bf16[400,256]{1,0:T(8,128)(2,1)S(1)}, bf16[400,256]{1,0:T(8,128)(2,1)S(1)}, u32[]{:S(2)}, u32[]{:S(2)}) collective-permute-start(bf16[400,256]{1,0:T(8,128)(2,1)S(1)} %get-tuple-element.43), channel_id=1, source_target_pairs={{0,16},{1,17},{2,18},{3,19},{4,20},{5,21},{6,22},{7,23},{8,24},{9,... | collective-permute-start | bytes 614408 | tf_op jit(solution)/shard_map/ppermute | solution.py:35
  9.6 0.0 collective-permute-done.3.meta_down
  9.6 0.0 collective-permute-done.2.meta_up
  9.6 0.0 collective-permute-done.left
  9.6 0.0 collective-permute-done.1.right
  9.7 1.3 %collective-permute-start.7 = (bf16[528,256]{1,0:T(8,128)(2,1)S(1)}, bf16[528,256]{1,0:T(8,128)(2,1)S(1)}, u32[]{:S(2)}, u32[]{:S(2)}) collective-permute-start(bf16[528,256]{1,0:T(8,128)(2,1)S(1)} %get-tuple-element.44), channel_id=1, source_target_pairs={{0,16},{1,17},{2,18},{3,19},{4,20},{5,21},{6,22},{7,23},{8,24},{9,... | collective-permute-start | bytes 811016 | tf_op jit(solution)/shard_map/ppermute | solution.py:35
  11.0 1.3 %collective-permute-start.4 = (bf16[136,512]{1,0:T(8,128)(2,1)S(1)}, bf16[136,512]{1,0:T(8,128)(2,1)S(1)}, u32[]{:S(2)}, u32[]{:S(2)}) collective-permute-start(bf16[136,512]{1,0:T(8,128)(2,1)S(1)} %get-tuple-element.41.down_in), channel_id=1, source_target_pairs={{0,20},{1,21},{2,22},{3,23},{4,24},{5,25},{6,26},{7,27},{8,28},{9,... | collective-permute-start | bytes 417800 | tf_op jit(solution)/shard_map/ppermute | solution.py:35
  12.3 1.3 %collective-permute-start.5 = (bf16[136,512]{1,0:T(8,128)(2,1)S(1)}, bf16[136,512]{1,0:T(8,128)(2,1)S(1)}, u32[]{:S(2)}, u32[]{:S(2)}) collective-permute-start(bf16[136,512]{1,0:T(8,128)(2,1)S(1)} %get-tuple-element.42.up_in), channel_id=1, source_target_pairs={{4,16},{5,17},{6,18},{7,19},{8,20},{9,21},{10,22},{11,23},{12,24},... | collective-permute-start | bytes 417800 | tf_op jit(solution)/shard_map/ppermute | solution.py:35
  13.6 0.7 %collective-permute-start.8 = (bf16[128,512]{1,0:T(8,128)(2,1)S(1)}, bf16[128,512]{1,0:T(8,128)(2,1)S(1)}, u32[]{:S(2)}, u32[]{:S(2)}) collective-permute-start(bf16[128,512]{1,0:T(8,128)(2,1)S(1)} %get-tuple-element.47), channel_id=1, source_target_pairs={{0,4},{1,5},{2,6},{3,7},{4,8},{5,9},{6,10},{7,11},{8,12},{9,13},{1... | collective-permute-start | bytes 393224 | tf_op jit(solution)/shard_map/ppermute | solution.py:35
  14.3 11.6 %collective-permute-done.6.mid = bf16[400,256]{1,0:T(8,128)(2,1)S(1)} collective-permute-done((bf16[400,256]{1,0:T(8,128)(2,1)S(1)}, bf16[400,256]{1,0:T(8,128)(2,1)S(1)}, u32[]{:S(2)}, u32[]{:S(2)}) %collective-permute-start.6) | collective-permute-done | bytes 204832 | tf_op jit(solution)/shard_map/ppermute | solution.py:35
  25.9 0.7 %collective-permute-start.9 = (bf16[128,512]{1,0:T(8,128)(2,1)S(1)}, bf16[128,512]{1,0:T(8,128)(2,1)S(1)}, u32[]{:S(2)}, u32[]{:S(2)}) collective-permute-start(bf16[128,512]{1,0:T(8,128)(2,1)S(1)} %get-tuple-element.48), channel_id=1, source_target_pairs={{4,0},{5,1},{6,2},{7,3},{8,4},{9,5},{10,6},{11,7},{12,8},{13,9},{1... | collective-permute-start | bytes 393224 | tf_op jit(solution)/shard_map/ppermute | solution.py:35
  26.5 2.1 %matrices.1 = (bf16[16,128,640]{2,1,0:T(8,128)(2,1)S(1)}, bf16[256,512]{1,0:T(8,128)(2,1)S(1)}) custom-call(f32[32768,128]{1,0:T(8,128)} %get-tuple-element.27.meta_in, bf16[512,256]{1,0:T(8,128)(2,1)S(1)} %get-tuple-element.40.after.end_in.own_end), custom_call_target="tpu_custom_call" | custom-call | tf_op jit(solution)/shard_map/matrices/pallas_call | solution.py:530
  28.7 0.0 collective-permute-done.8.got_up
  28.7 0.0 collective-permute-done.9.got_down
  28.7 0.0 collective-permute-done.4.side_up
  28.7 0.0 collective-permute-done.5.side_down
  28.7 1.5 %collective-permute-done.7.end = bf16[528,256]{1,0:T(8,128)(2,1)S(1)} collective-permute-done((bf16[528,256]{1,0:T(8,128)(2,1)S(1)}, bf16[528,256]{1,0:T(8,128)(2,1)S(1)}, u32[]{:S(2)}, u32[]{:S(2)}) %collective-permute-start.7) | collective-permute-done | bytes 270368 | tf_op jit(solution)/shard_map/ppermute | solution.py:35
  30.2 2.4 %finish.1 = f32[512,512]{1,0:T(8,128)} custom-call(f32[512,512]{1,0:T(8,128)S(1)} %bitcast.6, bf16[512,256]{1,0:T(8,128)(2,1)S(1)} %get-tuple-element.28.own_mid, bf16[512,256]{1,0:T(8,128)(2,1)S(1)} %get-tuple-element.40.after.end_in.own_end, bf16[136,512]{1,0:T(8,128)(2,1)S(1)} %collective-permute-done.4.side_up, ...), custom_call_target="tpu_custom_call" | custom-call | tf_op jit(solution)/shard_map/finish/pallas_call | solution.py:537
  (4 shorter events, 0.1 us)
Async XLA Ops:
  1.6 6.7 %copy-start = (f32[1,512,512]{2,1,0:T(8,128)S(1)}, f32[1,512,512]{2,1,0:T(8,128)}, u32[]{:S(2)}) copy-start(f32[1,512,512]{2,1,0:T(8,128)} %param.9) | copy-start | bytes 3145732
  1.6 8.0 %collective-permute-start.3 = (f32[8,128]{1,0:T(8,128)}, f32[8,128]{1,0:T(8,128)S(1)}, u32[]{:S(2)}, u32[]{:S(2)}) collective-permute-start(f32[8,128]{1,0:T(8,128)} %get-tuple-element.31), channel_id=1, source_target_pairs={{20,0},{21,1},{22,2},{23,3},{24,4},{25,5},{26,6},{27,7},{28,8},{29... | collective-permute-start | bytes 12296 | tf_op jit(solution)/shard_map/ppermute | solution.py:35
  4.4 5.2 %collective-permute-start.2 = (f32[8,128]{1,0:T(8,128)}, f32[8,128]{1,0:T(8,128)S(1)}, u32[]{:S(2)}, u32[]{:S(2)}) collective-permute-start(f32[8,128]{1,0:T(8,128)} %get-tuple-element.31), channel_id=1, source_target_pairs={{16,4},{17,5},{18,6},{19,7},{20,8},{21,9},{22,10},{23,11},{24,12},... | collective-permute-start | bytes 12296 | tf_op jit(solution)/shard_map/ppermute | solution.py:35
  6.9 2.8 %collective-permute-start = (f32[520,128]{1,0:T(8,128)}, f32[520,128]{1,0:T(8,128)S(1)}, u32[]{:S(2)}, u32[]{:S(2)}) collective-permute-start(f32[520,128]{1,0:T(8,128)} %get-tuple-element.29), channel_id=1, source_target_pairs={{0,1},{1,2},{2,3},{4,5},{5,6},{6,7},{8,9},{9,10},{10,11},{12,13},{... | collective-permute-start | bytes 798728 | tf_op jit(solution)/shard_map/ppermute | solution.py:35
  7.6 2.1 %collective-permute-start.1 = (f32[520,128]{1,0:T(8,128)}, f32[520,128]{1,0:T(8,128)S(1)}, u32[]{:S(2)}, u32[]{:S(2)}) collective-permute-start(f32[520,128]{1,0:T(8,128)} %get-tuple-element.30), channel_id=1, source_target_pairs={{1,0},{2,1},{3,2},{5,4},{6,5},{7,6},{9,8},{10,9},{11,10},{13,12},{... | collective-permute-start | bytes 798728 | tf_op jit(solution)/shard_map/ppermute | solution.py:35
  8.3 17.6 %collective-permute-start.6 = (bf16[400,256]{1,0:T(8,128)(2,1)S(1)}, bf16[400,256]{1,0:T(8,128)(2,1)S(1)}, u32[]{:S(2)}, u32[]{:S(2)}) collective-permute-start(bf16[400,256]{1,0:T(8,128)(2,1)S(1)} %get-tuple-element.43), channel_id=1, source_target_pairs={{0,16},{1,17},{2,18},{3,19},{4,20},{5,21},{6,22},{7,23},{8,24},{9,... | collective-permute-start | bytes 614408 | tf_op jit(solution)/shard_map/ppermute | solution.py:35
  9.7 20.5 %collective-permute-start.7 = (bf16[528,256]{1,0:T(8,128)(2,1)S(1)}, bf16[528,256]{1,0:T(8,128)(2,1)S(1)}, u32[]{:S(2)}, u32[]{:S(2)}) collective-permute-start(bf16[528,256]{1,0:T(8,128)(2,1)S(1)} %get-tuple-element.44), channel_id=1, source_target_pairs={{0,16},{1,17},{2,18},{3,19},{4,20},{5,21},{6,22},{7,23},{8,24},{9,... | collective-permute-start | bytes 811016 | tf_op jit(solution)/shard_map/ppermute | solution.py:35
  11.0 17.7 %collective-permute-start.4 = (bf16[136,512]{1,0:T(8,128)(2,1)S(1)}, bf16[136,512]{1,0:T(8,128)(2,1)S(1)}, u32[]{:S(2)}, u32[]{:S(2)}) collective-permute-start(bf16[136,512]{1,0:T(8,128)(2,1)S(1)} %get-tuple-element.41.down_in), channel_id=1, source_target_pairs={{0,20},{1,21},{2,22},{3,23},{4,24},{5,25},{6,26},{7,27},{8,28},{9,... | collective-permute-start | bytes 417800 | tf_op jit(solution)/shard_map/ppermute | solution.py:35
  12.3 16.4 %collective-permute-start.5 = (bf16[136,512]{1,0:T(8,128)(2,1)S(1)}, bf16[136,512]{1,0:T(8,128)(2,1)S(1)}, u32[]{:S(2)}, u32[]{:S(2)}) collective-permute-start(bf16[136,512]{1,0:T(8,128)(2,1)S(1)} %get-tuple-element.42.up_in), channel_id=1, source_target_pairs={{4,16},{5,17},{6,18},{7,19},{8,20},{9,21},{10,22},{11,23},{12,24},... | collective-permute-start | bytes 417800 | tf_op jit(solution)/shard_map/ppermute | solution.py:35
  13.6 15.1 %collective-permute-start.8 = (bf16[128,512]{1,0:T(8,128)(2,1)S(1)}, bf16[128,512]{1,0:T(8,128)(2,1)S(1)}, u32[]{:S(2)}, u32[]{:S(2)}) collective-permute-start(bf16[128,512]{1,0:T(8,128)(2,1)S(1)} %get-tuple-element.47), channel_id=1, source_target_pairs={{0,4},{1,5},{2,6},{3,7},{4,8},{5,9},{6,10},{7,11},{8,12},{9,13},{1... | collective-permute-start | bytes 393224 | tf_op jit(solution)/shard_map/ppermute | solution.py:35
  25.9 2.8 %collective-permute-start.9 = (bf16[128,512]{1,0:T(8,128)(2,1)S(1)}, bf16[128,512]{1,0:T(8,128)(2,1)S(1)}, u32[]{:S(2)}, u32[]{:S(2)}) collective-permute-start(bf16[128,512]{1,0:T(8,128)(2,1)S(1)} %get-tuple-element.48), channel_id=1, source_target_pairs={{4,0},{5,1},{6,2},{7,3},{8,4},{9,5},{10,6},{11,7},{12,8},{13,9},{1... | collective-permute-start | bytes 393224 | tf_op jit(solution)/shard_map/ppermute | solution.py:35

commit v8 on v7

--- a/solution.py
+++ b/solution.py
@@ -91,7 +91,7 @@
 
 def gather_kernel(
     nb, frame, row_frac, col_frac, row_shift, col_shift, table, prof_rows, prof_cols, ids,
-    meta_out, row_meta, to_right, to_left,
+    meta_out, token, row_meta, to_right, to_left,
     meta, marks, table_v, rows_v, cols_v, ids_v, row_s, col_s, sems, done,
 ):
     side = nb * BLK
@@ -117,7 +117,7 @@
         pltpu.make_async_copy(marks.at[0], to_right, done.at[2]),
         pltpu.make_async_copy(marks.at[1], to_left, done.at[3]),
     ]
-    summary = pltpu.make_async_copy(meta, meta_out.at[: meta.shape[0], :], done.at[4])
+    summary = pltpu.make_async_copy(meta, meta_out, done.at[4])
     rows = pltpu.make_async_copy(meta.at[: 2 * nb, :], row_meta, done.at[5])
 
     @pl.when(warper)
@@ -159,24 +159,17 @@
 
 
 def center_kernel(
-    nb, frame, meta_in, mark,
-    own, across, tip_hi, tip_lo, mid_hi, mid_lo, row_hi, row_lo, edge_hi, edge_lo,
-    meta, src_hi, src_lo, sem,
+    nb, frame, meta, mark,
+    own, across, mid_hi, mid_lo, row_hi, row_lo,
+    src_hi, src_lo,
 ):
     side = nb * BLK
 
     @pl.when(lax.axis_index("segment") == 0)
     def _():
-        small = pltpu.make_async_copy(meta_in.at[: meta.shape[0], :], meta, sem)
-        small.start()
-        for b in range(nb):
-            rows = slice(b * BLK, (b + 1) * BLK)
-            hi, lo = split(frame[rows, :])
-            for whole, tip, part in ((src_hi, tip_hi, hi), (src_lo, tip_lo, lo)):
-                whole[rows, :] = part
-                tip[rows, :BLK] = part[:, :BLK]
-                tip[rows, BLK:] = part[:, side - BLK :]
-        small.wait()
+        hi, lo = split(frame[...])
+        src_hi[...] = hi
+        src_lo[...] = lo
         fracs = [meta[2 * nb + b : 2 * nb + b + 1, :] for b in range(nb)]
         weights = taps(fracs + [meta[b : b + 1, :] for b in range(nb)])
         col_shift = [meta[3 * nb + b : 3 * nb + b + 1, :].astype(jnp.int32) for b in range(nb)]
@@ -197,18 +190,45 @@
             low = max(b * BLK, ROW0)
             high = min((b + 1) * BLK, side - ROW0)
             across[low - ROW0 : high - ROW0, :] = got[low - b * BLK : high - b * BLK, :].astype(BF16)
-        for n, (b, offset) in enumerate(((0, -BLK), (nb - 1, 0))):
-            hi, lo = split(banded(weights[b], col_shift[b], 2 * BLK, offset))
-            edge_hi[n * 2 * BLK : (n + 1) * 2 * BLK, :] = hi
-            edge_lo[n * 2 * BLK : (n + 1) * 2 * BLK, :] = lo
-
-
-def matrices_kernel(nb, nu, nv, sets, meta_in, after, kernels, band, padded, meta, sem):
+
+
+def outer_kernel(
+    nb, nx, frame, meta, meta_up, meta_down, mid_hi, mid_lo, after,
+    early_up, early_down, tip_hi, tip_lo, edge_hi, edge_lo, out_hi, out_lo,
+):
+    side = nb * BLK
+    i = lax.axis_index("skyx")
+
+    @pl.when(lax.axis_index("segment") == 0)
+    def _():
+        weights = taps([
+            meta_up[nb - 1 : nb, :], meta_down[0:1, :],
+            meta[2 * nb : 2 * nb + 1, :], meta[3 * nb - 1 : 3 * nb, :],
+        ])
+        shifts = [
+            row.astype(jnp.int32)
+            for row in (
+                meta_up[2 * nb - 1 : 2 * nb, :], meta_down[nb : nb + 1, :],
+                meta[3 * nb : 3 * nb + 1, :], meta[4 * nb - 1 : 4 * nb, :],
+            )
+        ]
+        for n, b in ((0, 0), (1, nb - 1)):
+            there = (i > 0) if n == 0 else (i < nx - 1)
+            weight = jnp.where(there, weights[n], 0.0)
+            mat = split(banded(weight, shifts[n], BLK, BLK if n == 0 else -BLK).T)
+            rows = slice(b * BLK, (b + 1) * BLK)
+            early = early_up if n == 0 else early_down
+            early[...] = dot3(mat, (mid_hi[rows, :], mid_lo[rows, :]), MATMUL).astype(BF16)
+            out_hi[n * BLK : (n + 1) * BLK, :], out_lo[n * BLK : (n + 1) * BLK, :] = mat
+            mat = split(banded(weights[2 + n], shifts[2 + n], 2 * BLK, -BLK if n == 0 else 0))
+            edge_hi[n * 2 * BLK : (n + 1) * 2 * BLK, :], edge_lo[n * 2 * BLK : (n + 1) * 2 * BLK, :] = mat
+            cols = slice(n * BLK, (n + 1) * BLK)
+            tip_hi[:, cols], tip_lo[:, cols] = split(frame[:, b * BLK : (b + 1) * BLK])
+
+
+def matrices_kernel(nb, nu, nv, sets, meta, after, kernels, band, padded):
     @pl.when(lax.axis_index("segment") != 0)
     def _():
-        small = pltpu.make_async_copy(meta_in.at[: meta.shape[0], :], meta, sem)
-        small.start()
-        small.wait()
         base = 4 * nb
         table = meta[base : base + sets, : nu * nv]
         base += sets
@@ -225,16 +245,16 @@
         coefs = jnp.dot(
             jnp.concatenate(cells, axis=0), table, precision=HIGHEST, preferred_element_type=F32
         )
-        width = nu * 160
+        width = nu * 96
         padded[...] = jnp.zeros_like(padded)
         padded[0:nv, 0:KW] = prof_rows
         profile = padded[0:nv, :]
         spread = jnp.concatenate(
-            [pltpu.roll(profile, p * 160 + 1, 1) for p in range(nu)], axis=0
+            [pltpu.roll(profile, p * 96 + 1, 1) for p in range(nu)], axis=0
         )
         base = jnp.dot(coefs, spread, precision=HIGHEST, preferred_element_type=F32)
         for cell in range(nb * nb):
-            row = jnp.broadcast_to(base[cell : cell + 1, :], (BLK, width))
+            row = jnp.broadcast_to(base[cell : cell + 1, :], (BLK // 2, width))
             kernels[cell] = pltpu.roll(row, 0, 1, stride=1, stride_axis=0).astype(BF16)
         padded[...] = jnp.zeros_like(padded)
         padded[0:nu, 0:KW] = prof_cols
@@ -245,25 +265,21 @@
 
 
 def edge_kernel(
-    nb, nx, ny,
-    left, right, meta_up, meta_down, tip_hi, tip_lo, mid_hi, mid_lo, row_hi, row_lo, edge_hi, edge_lo,
+    nb, ny,
+    left, right, early_up, early_down, tip_hi, tip_lo, row_hi, row_lo, edge_hi, edge_lo, out_hi, out_lo,
     own, across, side_up, side_down,
     end_hi, end_lo,
 ):
     side = nb * BLK
     kept = side - 2 * ROW0
     half = side // 2
-    i = lax.axis_index("skyx")
     j = lax.axis_index("skyy")
 
     @pl.when(lax.axis_index("segment") == 0)
     def _():
         lanes = lax.broadcasted_iota(jnp.int32, (8, BLK), 1)
-        weights = taps([left[side : side + 1, :], right[side : side + 1, :], meta_up[nb - 1 : nb, :], meta_down[0:1, :]])
-        shifts = [
-            part[row : row + 1, :].astype(jnp.int32)
-            for part, row in ((left, side + 1), (right, side + 1), (meta_up, 2 * nb - 1), (meta_down, nb))
-        ]
+        weights = taps([left[side : side + 1, :], right[side : side + 1, :]])
+        shifts = [part[side + 1 : side + 2, :].astype(jnp.int32) for part in (left, right)]
         parts = [split(left[:side, :]), split(right[:side, :])]
         for n in range(2):
             source = []
@@ -284,22 +300,15 @@
         end_lo[:, 2 * BLK :] = lo
         outer = []
         for n, b in ((0, 0), (1, nb - 1)):
-            there = (i > 0) if n == 0 else (i < nx - 1)
-            weight = jnp.where(there, weights[2 + n], 0.0)
-            mat = split(banded(weight, shifts[2 + n], BLK, BLK if n == 0 else -BLK).T)
             rows = slice(b * BLK, (b + 1) * BLK)
-            source = [
-                jnp.concatenate([mid[rows, :], end[rows, :]], axis=1)
-                for mid, end in ((mid_hi, end_hi), (mid_lo, end_lo))
-            ]
-            got = dot3(mat, source, MATMUL)
-            outer.append(got)
+            mat = tuple(part[n * BLK : (n + 1) * BLK, :] for part in (out_hi, out_lo))
+            got = dot3(mat, (end_hi[rows, :], end_lo[rows, :]), MATMUL)
+            outer.append(got[:, 2 * BLK :])
             out = side_up if n == 0 else side_down
-            inner = side - 2 * BLK
-            out[:BLK, BLK : side - BLK] = got[:, :inner].astype(BF16)
-            out[:BLK, :BLK] = got[:, inner : inner + BLK].astype(BF16)
-            out[:BLK, side - BLK :] = got[:, inner + BLK : side].astype(BF16)
-            turned = got[:, side:].T
+            out[:BLK, :BLK] = got[:, :BLK].astype(BF16)
+            out[:BLK, BLK : side - BLK] = (early_up if n == 0 else early_down)[...]
+            out[:BLK, side - BLK :] = got[:, BLK : 2 * BLK].astype(BF16)
+            turned = got[:, 2 * BLK :].T
             for k, row in enumerate((0, 8, BLK - 16, BLK - 8)):
                 out[BLK:, k * BLK : (k + 1) * BLK] = turned[row : row + 8].astype(BF16)
         across[kept : kept + 16, :] = side_down[:16, :half]
@@ -320,8 +329,8 @@
         strip = jnp.concatenate(strips, axis=0)
         strip = jnp.concatenate(
             [
-                strip[: ROW0 - 16], outer[0][BLK - 16 :, side:], strip[ROW0 : side - ROW0],
-                outer[1][:16, side:], strip[side - ROW0 + 16 :],
+                strip[: ROW0 - 16], outer[0][BLK - 16 :], strip[ROW0 : side - ROW0],
+                outer[1][:16], strip[side - ROW0 + 16 :],
             ],
             axis=0,
         ).T
@@ -427,11 +436,19 @@
             for bj in range(nb):
                 cols = slice(bj * BLK, (bj + 1) * BLK)
                 window = jnp.concatenate(
-                    [passed[p, bi * BLK : bi * BLK + 160, cols] for p in range(nu)], axis=0
+                    [
+                        jnp.concatenate(
+                            [passed[p, row : row + 96, cols] for row in (bi * BLK, bi * BLK + BLK // 2)],
+                            axis=1,
+                        )
+                        for p in range(nu)
+                    ],
+                    axis=0,
                 )
                 total = jnp.dot(kernels[bi * nb + bj], window, preferred_element_type=F32)
-                rows = slice(bi * BLK, (bi + 1) * BLK)
-                result[rows, cols] = frame[rows, cols] - total
+                for n in range(2):
+                    rows = slice(bi * BLK + n * BLK // 2, bi * BLK + (n + 1) * BLK // 2)
+                    result[rows, cols] = frame[rows, cols] - total[:, n * BLK : (n + 1) * BLK]
             sends[bi].start()
 
     for send in sends:
@@ -465,7 +482,7 @@
     row_frac = row_frac.reshape(nb, BLK)
     col_frac = col_frac.reshape(nb, BLK)
 
-    width = nu * 160
+    width = nu * 96
     kept = side - 2 * ROW0
     inner = side - 2 * BLK
     cells = nb * nb
@@ -474,11 +491,13 @@
     total = 4 * nb + sets + nv + nu + nb
     total += -total % 8
     meta_shape = pltpu.VMEM((total, BLK), F32)
-    meta, row_meta, to_right, to_left = pl.pallas_call(
+    meta, token, row_meta, to_right, to_left = pl.pallas_call(
         functools.partial(gather_kernel, nb),
-        out_shape=(shape((SPARE, BLK), F32), shape((2 * nb, BLK), F32), slab, slab),
+        out_shape=(
+            shape((total, BLK), F32), shape((SPARE, BLK), F32), shape((2 * nb, BLK), F32), slab, slab,
+        ),
         in_specs=[ANY] * 9,
-        out_specs=(ANY,) * 4,
+        out_specs=(ANY,) * 5,
         scratch_shapes=[
             meta_shape, pltpu.VMEM((2, side + 8, BLK), F32),
             pltpu.VMEM(coef_table.shape, F32), pltpu.VMEM(profile_rows.shape, BF16),
@@ -495,30 +514,38 @@
     right = moved(to_left, (0, 0, -1), (0,))
     mark = call(
         marker_kernel, "marker", shape((8, BLK), F32), [ANY], flops=1 << 31,
-    )(meta)
-    own_mid, mid, *parts = call(
+    )(token)
+    own_mid, mid, mid_hi, mid_lo, row_hi, row_lo = call(
         functools.partial(center_kernel, nb), "center",
         (shape((side, inner), BF16), shape((kept, inner), BF16))
-        + (shape((side, 2 * BLK), BF16),) * 2
         + (shape((side, inner), BF16),) * 2
-        + (shape((side, side), BF16),) * 2
-        + (shape((4 * BLK, BLK), BF16),) * 2,
-        [VM, ANY, ANY],
-        [
-            meta_shape, pltpu.VMEM((side, side), BF16), pltpu.VMEM((side, side), BF16),
-            pltpu.SemaphoreType.DMA(()),
-        ],
+        + (shape((side, side), BF16),) * 2,
+        [VM, VM, ANY],
+        [pltpu.VMEM((side, side), BF16), pltpu.VMEM((side, side), BF16)],
         flops=1 << 33,
     )(frame, meta, mark)
+    early_up, early_down, *parts = call(
+        functools.partial(outer_kernel, nb, nx), "outer",
+        (shape((BLK, inner), BF16),) * 2
+        + (shape((side, 2 * BLK), BF16),) * 2
+        + (shape((4 * BLK, BLK), BF16),) * 2
+        + (shape((2 * BLK, BLK), BF16),) * 2,
+        [VM] * 6 + [ANY],
+        flops=1 << 33,
+    )(frame, meta, meta_up, meta_down, mid_hi, mid_lo, own_mid)
     mid = moved(mid, (1, 0, 0), (0,))
+    tip_hi, tip_lo, edge_hi, edge_lo, out_hi, out_lo = parts
     own_end, end, to_up, to_down = call(
-        functools.partial(edge_kernel, nb, nx, ny), "edges",
+        functools.partial(edge_kernel, nb, ny), "edges",
         (shape((side, 2 * BLK), BF16), shape((kept + 128, side // 2), BF16))
         + (shape((BLK + 8, side), BF16),) * 2,
         [VM] * 12,
         [pltpu.VMEM((side, 3 * BLK), BF16)] * 2,
         flops=1 << 33,
-    )(left, right, meta_up, meta_down, *parts)
+    )(
+        left, right, early_up, early_down, tip_hi, tip_lo, row_hi, row_lo, edge_hi, edge_lo,
+        out_hi, out_lo,
+    )
     end = moved(end, (1, 0, 0), (0,))
     side_down = moved(to_up, (1, -1, 0), (0,))
     side_up = moved(to_down, (1, 1, 0), (0,))
@@ -529,9 +556,9 @@
     got_up = moved(to_down, (0, 1, 0), (0,))
     kernels, band = call(
         functools.partial(matrices_kernel, nb, nu, nv, sets), "matrices",
-        (shape((cells, BLK, width), BF16), shape((2 * BLK, nu * BLK), BF16)),
-        [ANY, VM],
-        [pltpu.VMEM((8, width), F32), meta_shape, pltpu.SemaphoreType.DMA(())],
+        (shape((cells, BLK // 2, width), BF16), shape((2 * BLK, nu * BLK), BF16)),
+        [VM, ANY],
+        [pltpu.VMEM((8, width), F32)],
         flops=0,
     )(meta, own_end)
     result = pl.pallas_call(

time: 33.2 us -> 32.9 us (level)
  the two profiles are of different devices: /device:TPU:14 before, /device:TPU:1 now
where the time goes in v8:
time: 32.9 us; the launch traced here: 32.6 us
  starting transfers between devices  18.9 us (57%)
  waiting for transfers between devices  6.92 us (21%)
  Pallas kernels  6.61 us (20%)
    ppermute x10, starting transfers between devices, moved(): return lax.ppermute(block, axes, route)  18.9 us
    ppermute x10, waiting for transfers between devices, moved(): return lax.ppermute(block, axes, route)  6.92 us
    pallas_call x1, Pallas kernels, local(): pl.pallas_call(functools.partial(gather_kernel, nb), out_shape=(shape((to...  1.96 us
    pallas_call x1, Pallas kernels, local(): call(functools.partial(center_kernel, nb), 'center', (shape((side, inner)...  1.46 us
    pallas_call x1, Pallas kernels, local(): call(functools.partial(edge_kernel, nb, ny), 'edges', (shape((side, 2 * B...  1.43 us
    pallas_call x1, Pallas kernels, local(): pl.pallas_call(functools.partial(finish_kernel, nb, nu), out_shape=shape(...  1.05 us
    pallas_call x1, Pallas kernels, local(): call(functools.partial(outer_kernel, nb, nx), 'outer', (shape((BLK, inner...  0.66 us
  transfers between devices with their start and end apart: 10, of which 3 were waited for; matrix products, arithmetic and copies ran while one was open for 0% of the time, Pallas kernels for 11%

profile of v8, /device:TPU:1, one launch (start us, length us, event | category | flops | bytes accessed | tf_op | source)
XLA Modules:
  0.0 32.6 jit_solution(8730976199163454361)
XLA Ops:
  0.0 2.0 %gather.1 = (f32[48,128]{1,0:T(8,128)}, f32[32768,128]{1,0:T(8,128)}, f32[8,128]{1,0:T(8,128)}, f32[520,128]{1,0:T(8,128)}, f32[520,128]{1,0:T(8,128)}) custom-call(f32[512,512]{1,0:T(8,128)} %bitcast.4, f32[4,128]{1,0:T(4,128)} %bitcast.8, f32[4,128]{1,0:T(4,128)} %bitcast.9, s32[4]{0:T(128)} %row_shift.1, s32[4]{0:T(128)} %col_shift.1, f32[16,32]{1,0:T(8,128)} %table.1, ...), custom_call_target="tpu_custom_call" | custom-call | tf_op jit(solution)/shard_map/gather/pallas_call | solution.py:494
  2.0 0.0 copy-start
  2.0 0.0 copy-start.1
  2.0 1.4 %collective-permute-start.3 = (f32[8,128]{1,0:T(8,128)}, f32[8,128]{1,0:T(8,128)S(1)}, u32[]{:S(2)}, u32[]{:S(2)}) collective-permute-start(f32[8,128]{1,0:T(8,128)} %get-tuple-element.37), channel_id=1, source_target_pairs={{20,0},{21,1},{22,2},{23,3},{24,4},{25,5},{26,6},{27,7},{28,8},{29... | collective-permute-start | bytes 12296 | tf_op jit(solution)/shard_map/ppermute | solution.py:35
  3.4 0.7 %collective-permute-start.2 = (f32[8,128]{1,0:T(8,128)}, f32[8,128]{1,0:T(8,128)S(1)}, u32[]{:S(2)}, u32[]{:S(2)}) collective-permute-start(f32[8,128]{1,0:T(8,128)} %get-tuple-element.37), channel_id=1, source_target_pairs={{16,4},{17,5},{18,6},{19,7},{20,8},{21,9},{22,10},{23,11},{24,12},... | collective-permute-start | bytes 12296 | tf_op jit(solution)/shard_map/ppermute | solution.py:35
  4.1 4.5 %collective-permute-start = (f32[520,128]{1,0:T(8,128)}, f32[520,128]{1,0:T(8,128)S(1)}, u32[]{:S(2)}, u32[]{:S(2)}) collective-permute-start(f32[520,128]{1,0:T(8,128)} %get-tuple-element.35), channel_id=1, source_target_pairs={{0,1},{1,2},{2,3},{4,5},{5,6},{6,7},{8,9},{9,10},{10,11},{12,13},{... | collective-permute-start | bytes 798728 | tf_op jit(solution)/shard_map/ppermute | solution.py:35
  8.6 1.9 %collective-permute-start.1 = (f32[520,128]{1,0:T(8,128)}, f32[520,128]{1,0:T(8,128)S(1)}, u32[]{:S(2)}, u32[]{:S(2)}) collective-permute-start(f32[520,128]{1,0:T(8,128)} %get-tuple-element.36), channel_id=1, source_target_pairs={{1,0},{2,1},{3,2},{5,4},{6,5},{7,6},{9,8},{10,9},{11,10},{13,12},{... | collective-permute-start | bytes 798728 | tf_op jit(solution)/shard_map/ppermute | solution.py:35
  10.6 0.0 copy-done
  10.6 0.0 copy-done.1
  10.6 1.5 %center.1 = (bf16[512,256]{1,0:T(8,128)(2,1)S(1)}, bf16[400,256]{1,0:T(8,128)(2,1)S(1)}, bf16[512,256]{1,0:T(8,128)(2,1)S(1)}, bf16[512,256]{1,0:T(8,128)(2,1)S(...) custom-call(f32[512,512]{1,0:T(8,128)S(1)} %bitcast.5, f32[48,128]{1,0:T(8,128)S(1)} %copy-done.1, ...), custom_call_target="tpu_custom_call" | custom-call | flops 8589934592 | bytes 17179868 | tf_op jit(solution)/shard_map/center/pallas_call | solution.py:518
  12.1 1.3 %collective-permute-start.6 = (bf16[400,256]{1,0:T(8,128)(2,1)S(1)}, bf16[400,256]{1,0:T(8,128)(2,1)S(1)}, u32[]{:S(2)}, u32[]{:S(2)}) collective-permute-start(bf16[400,256]{1,0:T(8,128)(2,1)S(1)} %get-tuple-element.53), channel_id=1, source_target_pairs={{0,16},{1,17},{2,18},{3,19},{4,20},{5,21},{6,22},{7,23},{8,24},{9,... | collective-permute-start | bytes 614408 | tf_op jit(solution)/shard_map/ppermute | solution.py:35
  13.4 0.0 collective-permute-done.3.meta_down
  13.4 0.0 collective-permute-done.2.meta_up
  13.4 0.7 %outer.1 = (bf16[128,256]{1,0:T(8,128)(2,1)S(1)}, bf16[128,256]{1,0:T(8,128)(2,1)S(1)}, bf16[512,256]{1,0:T(8,128)(2,1)S(1)}, bf16[512,256]{1,0:T(8,128)(2,1)S(1...) custom-call(f32[512,512]{1,0:T(8,128)S(1)} %bitcast.6, ...), custom_call_target="tpu_custom_call" | custom-call | flops 8589934592 | bytes 17179868 | tf_op jit(solution)/shard_map/outer/pallas_call | solution.py:527
  14.1 0.0 collective-permute-done.left
  14.1 2.5 %collective-permute-done.1.right = f32[520,128]{1,0:T(8,128)S(1)} collective-permute-done((f32[520,128]{1,0:T(8,128)}, f32[520,128]{1,0:T(8,128)S(1)}, u32[]{:S(2)}, u32[]{:S(2)}) %collective-permute-start.1) | collective-permute-done | bytes 266272 | tf_op jit(solution)/shard_map/ppermute | solution.py:35
  16.6 1.4 %edges.1 = (bf16[512,256]{1,0:T(8,128)(2,1)S(1)}, bf16[528,256]{1,0:T(8,128)(2,1)S(1)}, bf16[136,512]{1,0:T(8,128)(2,1)S(1)}, bf16[136,512]{1,0:T(8,128)(2,1)S(1)}) custom-call(f32[520,128]{1,0:T(8,128)S(1)} %collective-permute-done.left, f32[520,128]{1,0:T(8,128)S(1)} %collective-permute-done.1.right, bf16[128,256]{1,0:T(8,128)(2,1)S(1)} %get-tuple-element.40.early_up, ...), custom_call_target="tpu_custom_call" | custom-call | flops 8589934592 | bytes 17179868 | tf_op jit(solution)/shard_map/edges/pallas_call | solution.py:538
  18.0 1.3 %collective-permute-start.7 = (bf16[528,256]{1,0:T(8,128)(2,1)S(1)}, bf16[528,256]{1,0:T(8,128)(2,1)S(1)}, u32[]{:S(2)}, u32[]{:S(2)}) collective-permute-start(bf16[528,256]{1,0:T(8,128)(2,1)S(1)} %get-tuple-element.54), channel_id=1, source_target_pairs={{0,16},{1,17},{2,18},{3,19},{4,20},{5,21},{6,22},{7,23},{8,24},{9,... | collective-permute-start | bytes 811016 | tf_op jit(solution)/shard_map/ppermute | solution.py:35
  19.3 1.3 %collective-permute-start.4 = (bf16[136,512]{1,0:T(8,128)(2,1)S(1)}, bf16[136,512]{1,0:T(8,128)(2,1)S(1)}, u32[]{:S(2)}, u32[]{:S(2)}) collective-permute-start(bf16[136,512]{1,0:T(8,128)(2,1)S(1)} %get-tuple-element.51.down_in), channel_id=1, source_target_pairs={{0,20},{1,21},{2,22},{3,23},{4,24},{5,25},{6,26},{7,27},{8,28},{9,... | collective-permute-start | bytes 417800 | tf_op jit(solution)/shard_map/ppermute | solution.py:35
  20.6 0.7 %collective-permute-start.5 = (bf16[136,512]{1,0:T(8,128)(2,1)S(1)}, bf16[136,512]{1,0:T(8,128)(2,1)S(1)}, u32[]{:S(2)}, u32[]{:S(2)}) collective-permute-start(bf16[136,512]{1,0:T(8,128)(2,1)S(1)} %get-tuple-element.52.up_in), channel_id=1, source_target_pairs={{4,16},{5,17},{6,18},{7,19},{8,20},{9,21},{10,22},{11,23},{12,24},... | collective-permute-start | bytes 417800 | tf_op jit(solution)/shard_map/ppermute | solution.py:35
  21.4 4.5 %collective-permute-start.8 = (bf16[128,512]{1,0:T(8,128)(2,1)S(1)}, bf16[128,512]{1,0:T(8,128)(2,1)S(1)}, u32[]{:S(2)}, u32[]{:S(2)}) collective-permute-start(bf16[128,512]{1,0:T(8,128)(2,1)S(1)} %get-tuple-element.57), channel_id=1, source_target_pairs={{0,4},{1,5},{2,6},{3,7},{4,8},{5,9},{6,10},{7,11},{8,12},{9,13},{1... | collective-permute-start | bytes 393224 | tf_op jit(solution)/shard_map/ppermute | solution.py:35
  25.8 0.0 collective-permute-done.6.mid
  25.8 1.3 %collective-permute-start.9 = (bf16[128,512]{1,0:T(8,128)(2,1)S(1)}, bf16[128,512]{1,0:T(8,128)(2,1)S(1)}, u32[]{:S(2)}, u32[]{:S(2)}) collective-permute-start(bf16[128,512]{1,0:T(8,128)(2,1)S(1)} %get-tuple-element.58), channel_id=1, source_target_pairs={{4,0},{5,1},{6,2},{7,3},{8,4},{9,5},{10,6},{11,7},{12,8},{13,9},{1... | collective-permute-start | bytes 393224 | tf_op jit(solution)/shard_map/ppermute | solution.py:35
  27.2 0.6 %collective-permute-done.8.got_up = bf16[128,512]{1,0:T(8,128)(2,1)S(1)} collective-permute-done((bf16[128,512]{1,0:T(8,128)(2,1)S(1)}, bf16[128,512]{1,0:T(8,128)(2,1)S(1)}, u32[]{:S(2)}, u32[]{:S(2)}) %collective-permute-start.8) | collective-permute-done | bytes 131104 | tf_op jit(solution)/shard_map/ppermute | solution.py:35
  27.8 3.8 %collective-permute-done.9.got_down = bf16[128,512]{1,0:T(8,128)(2,1)S(1)} collective-permute-done((bf16[128,512]{1,0:T(8,128)(2,1)S(1)}, bf16[128,512]{1,0:T(8,128)(2,1)S(1)}, u32[]{:S(2)}, u32[]{:S(2)}) %collective-permute-start.9) | collective-permute-done | bytes 131104 | tf_op jit(solution)/shard_map/ppermute | solution.py:35
  31.6 0.0 collective-permute-done.4.side_up
  31.6 0.0 collective-permute-done.5.side_down
  31.6 0.0 collective-permute-done.7.end
  31.6 1.1 %finish.1 = f32[512,512]{1,0:T(8,128)} custom-call(f32[512,512]{1,0:T(8,128)S(1)} %bitcast.7, bf16[512,256]{1,0:T(8,128)(2,1)S(1)} %get-tuple-element.34.after.own_mid, bf16[512,256]{1,0:T(8,128)(2,1)S(1)} %get-tuple-element.50.after.end_in.own_end, bf16[136,512]{1,0:T(8,128)(2,1)S(1)} %collective-permute-done.4.side_up, ...), custom_call_target="tpu_custom_call" | custom-call | tf_op jit(solution)/shard_map/finish/pallas_call | solution.py:564
  (3 shorter events, 0.0 us)
Async XLA Ops:
  2.0 8.6 %copy-start = (f32[1,512,512]{2,1,0:T(8,128)S(1)}, f32[1,512,512]{2,1,0:T(8,128)}, u32[]{:S(2)}) copy-start(f32[1,512,512]{2,1,0:T(8,128)} %param.9) | copy-start | bytes 3145732
  2.0 8.6 %copy-start.1 = (f32[48,128]{1,0:T(8,128)S(1)}, f32[48,128]{1,0:T(8,128)}, u32[]{:S(2)}) copy-start(f32[48,128]{1,0:T(8,128)} %get-tuple-element.32.meta) | copy-start | bytes 73732
  2.0 11.4 %collective-permute-start.3 = (f32[8,128]{1,0:T(8,128)}, f32[8,128]{1,0:T(8,128)S(1)}, u32[]{:S(2)}, u32[]{:S(2)}) collective-permute-start(f32[8,128]{1,0:T(8,128)} %get-tuple-element.37), channel_id=1, source_target_pairs={{20,0},{21,1},{22,2},{23,3},{24,4},{25,5},{26,6},{27,7},{28,8},{29... | collective-permute-start | bytes 12296 | tf_op jit(solution)/shard_map/ppermute | solution.py:35
  3.4 10.0 %collective-permute-start.2 = (f32[8,128]{1,0:T(8,128)}, f32[8,128]{1,0:T(8,128)S(1)}, u32[]{:S(2)}, u32[]{:S(2)}) collective-permute-start(f32[8,128]{1,0:T(8,128)} %get-tuple-element.37), channel_id=1, source_target_pairs={{16,4},{17,5},{18,6},{19,7},{20,8},{21,9},{22,10},{23,11},{24,12},... | collective-permute-start | bytes 12296 | tf_op jit(solution)/shard_map/ppermute | solution.py:35
  4.1 10.0 %collective-permute-start = (f32[520,128]{1,0:T(8,128)}, f32[520,128]{1,0:T(8,128)S(1)}, u32[]{:S(2)}, u32[]{:S(2)}) collective-permute-start(f32[520,128]{1,0:T(8,128)} %get-tuple-element.35), channel_id=1, source_target_pairs={{0,1},{1,2},{2,3},{4,5},{5,6},{6,7},{8,9},{9,10},{10,11},{12,13},{... | collective-permute-start | bytes 798728 | tf_op jit(solution)/shard_map/ppermute | solution.py:35
  8.6 7.9 %collective-permute-start.1 = (f32[520,128]{1,0:T(8,128)}, f32[520,128]{1,0:T(8,128)S(1)}, u32[]{:S(2)}, u32[]{:S(2)}) collective-permute-start(f32[520,128]{1,0:T(8,128)} %get-tuple-element.36), channel_id=1, source_target_pairs={{1,0},{2,1},{3,2},{5,4},{6,5},{7,6},{9,8},{10,9},{11,10},{13,12},{... | collective-permute-start | bytes 798728 | tf_op jit(solution)/shard_map/ppermute | solution.py:35
  12.1 13.8 %collective-permute-start.6 = (bf16[400,256]{1,0:T(8,128)(2,1)S(1)}, bf16[400,256]{1,0:T(8,128)(2,1)S(1)}, u32[]{:S(2)}, u32[]{:S(2)}) collective-permute-start(bf16[400,256]{1,0:T(8,128)(2,1)S(1)} %get-tuple-element.53), channel_id=1, source_target_pairs={{0,16},{1,17},{2,18},{3,19},{4,20},{5,21},{6,22},{7,23},{8,24},{9,... | collective-permute-start | bytes 614408 | tf_op jit(solution)/shard_map/ppermute | solution.py:35
  18.0 13.5 %collective-permute-start.7 = (bf16[528,256]{1,0:T(8,128)(2,1)S(1)}, bf16[528,256]{1,0:T(8,128)(2,1)S(1)}, u32[]{:S(2)}, u32[]{:S(2)}) collective-permute-start(bf16[528,256]{1,0:T(8,128)(2,1)S(1)} %get-tuple-element.54), channel_id=1, source_target_pairs={{0,16},{1,17},{2,18},{3,19},{4,20},{5,21},{6,22},{7,23},{8,24},{9,... | collective-permute-start | bytes 811016 | tf_op jit(solution)/shard_map/ppermute | solution.py:35
  19.3 12.2 %collective-permute-start.4 = (bf16[136,512]{1,0:T(8,128)(2,1)S(1)}, bf16[136,512]{1,0:T(8,128)(2,1)S(1)}, u32[]{:S(2)}, u32[]{:S(2)}) collective-permute-start(bf16[136,512]{1,0:T(8,128)(2,1)S(1)} %get-tuple-element.51.down_in), channel_id=1, source_target_pairs={{0,20},{1,21},{2,22},{3,23},{4,24},{5,25},{6,26},{7,27},{8,28},{9,... | collective-permute-start | bytes 417800 | tf_op jit(solution)/shard_map/ppermute | solution.py:35
  20.6 10.9 %collective-permute-start.5 = (bf16[136,512]{1,0:T(8,128)(2,1)S(1)}, bf16[136,512]{1,0:T(8,128)(2,1)S(1)}, u32[]{:S(2)}, u32[]{:S(2)}) collective-permute-start(bf16[136,512]{1,0:T(8,128)(2,1)S(1)} %get-tuple-element.52.up_in), channel_id=1, source_target_pairs={{4,16},{5,17},{6,18},{7,19},{8,20},{9,21},{10,22},{11,23},{12,24},... | collective-permute-start | bytes 417800 | tf_op jit(solution)/shard_map/ppermute | solution.py:35
  21.4 6.4 %collective-permute-start.8 = (bf16[128,512]{1,0:T(8,128)(2,1)S(1)}, bf16[128,512]{1,0:T(8,128)(2,1)S(1)}, u32[]{:S(2)}, u32[]{:S(2)}) collective-permute-start(bf16[128,512]{1,0:T(8,128)(2,1)S(1)} %get-tuple-element.57), channel_id=1, source_target_pairs={{0,4},{1,5},{2,6},{3,7},{4,8},{5,9},{6,10},{7,11},{8,12},{9,13},{1... | collective-permute-start | bytes 393224 | tf_op jit(solution)/shard_map/ppermute | solution.py:35
  25.8 5.7 %collective-permute-start.9 = (bf16[128,512]{1,0:T(8,128)(2,1)S(1)}, bf16[128,512]{1,0:T(8,128)(2,1)S(1)}, u32[]{:S(2)}, u32[]{:S(2)}) collective-permute-start(bf16[128,512]{1,0:T(8,128)(2,1)S(1)} %get-tuple-element.58), channel_id=1, source_target_pairs={{4,0},{5,1},{6,2},{7,3},{8,4},{9,5},{10,6},{11,7},{12,8},{13,9},{1... | collective-permute-start | bytes 393224 | tf_op jit(solution)/shard_map/ppermute | solution.py:35

commit v9 on v8

--- a/solution.py
+++ b/solution.py
@@ -264,9 +264,35 @@
             band[:, p * BLK : (p + 1) * BLK] = turned.astype(BF16)
 
 
+def row_blocks(nb):
+    for b in range(nb):
+        first, depth = (b, BLK) if b in (0, nb - 1) else (b - 1, 3 * BLK)
+        yield b, slice(b * BLK, (b + 1) * BLK), slice(first * BLK, first * BLK + depth)
+
+
+def left_kernel(nb, left, tip_hi, tip_lo, row_hi, row_lo, edge_hi, edge_lo, own, across, end_hi, end_lo):
+    side = nb * BLK
+
+    @pl.when(lax.axis_index("segment") == 0)
+    def _():
+        source = [
+            jnp.concatenate([part, tip[:, :BLK]], axis=1)
+            for part, tip in zip(split(left[:side, :]), (tip_hi, tip_lo))
+        ]
+        mat = (edge_hi[: 2 * BLK, :], edge_lo[: 2 * BLK, :])
+        end_hi[...], end_lo[...] = split(packed3(source, mat))
+        for b, rows, cols in row_blocks(nb):
+            mat = (row_hi[rows, cols], row_lo[rows, cols])
+            got = packed3(mat, (end_hi[cols, :], end_lo[cols, :]))
+            own[rows, :] = got.astype(BF16)
+            low, high = max(b * BLK, ROW0), min((b + 1) * BLK, side - ROW0)
+            across[low - ROW0 : high - ROW0, :] = got[low - b * BLK : high - b * BLK, :].astype(BF16)
+
+
 def edge_kernel(
     nb, ny,
     left, right, early_up, early_down, tip_hi, tip_lo, row_hi, row_lo, edge_hi, edge_lo, out_hi, out_lo,
+    own_low, low, low_hi, low_lo,
     own, across, side_up, side_down,
     end_hi, end_lo,
 ):
@@ -280,21 +306,22 @@
         lanes = lax.broadcasted_iota(jnp.int32, (8, BLK), 1)
         weights = taps([left[side : side + 1, :], right[side : side + 1, :]])
         shifts = [part[side + 1 : side + 2, :].astype(jnp.int32) for part in (left, right)]
-        parts = [split(left[:side, :]), split(right[:side, :])]
-        for n in range(2):
-            source = []
-            for part, tip in zip(parts[n], (tip_hi, tip_lo)):
-                inner = tip[:, n * BLK : (n + 1) * BLK]
-                source.append(jnp.concatenate([part, inner] if n == 0 else [inner, part], axis=1))
-            mat = tuple(edge[n * 2 * BLK : (n + 1) * 2 * BLK, :] for edge in (edge_hi, edge_lo))
-            hi, lo = split(packed3(source, mat))
-            end_hi[:, n * BLK : (n + 1) * BLK] = hi
-            end_lo[:, n * BLK : (n + 1) * BLK] = lo
+        source = [
+            jnp.concatenate([tip[:, BLK:], part], axis=1)
+            for part, tip in zip(split(right[:side, :]), (tip_hi, tip_lo))
+        ]
+        mat = (edge_hi[2 * BLK :, :], edge_lo[2 * BLK :, :])
+        hi, lo = split(packed3(source, mat))
+        for end, done, part in ((end_hi, low_hi, hi), (end_lo, low_lo, lo)):
+            end[:, :BLK] = done[...]
+            end[:, BLK : 2 * BLK] = part
+        own[:, :BLK] = own_low[...]
+        across[:kept, :BLK] = low[...]
         low_ok = jnp.logical_and(lanes >= BLK - HALF, j > 0)
         high_ok = jnp.logical_and(lanes < HALF, j < ny - 1)
-        low = split(banded(jnp.where(low_ok, weights[0], 0.0), shifts[0], BLK, BLK))
+        lower = split(banded(jnp.where(low_ok, weights[0], 0.0), shifts[0], BLK, BLK))
         high = split(banded(jnp.where(high_ok, weights[1], 0.0), shifts[1], BLK, -BLK))
-        mat = [jnp.concatenate(pair, axis=0) for pair in zip(low, high)]
+        mat = [jnp.concatenate(pair, axis=0) for pair in zip(lower, high)]
         hi, lo = split(packed3((tip_hi[...], tip_lo[...]), mat))
         end_hi[:, 2 * BLK :] = hi
         end_lo[:, 2 * BLK :] = lo
@@ -316,16 +343,15 @@
         across[kept + 32 : kept + 48, :] = side_down[:16, half:]
         across[kept + 48 : kept + 64, :] = side_up[BLK - 16 : BLK, half:]
         strips = []
-        for b in range(nb):
-            first, depth = (b, BLK) if b in (0, nb - 1) else (b - 1, 3 * BLK)
-            rows, cols = slice(b * BLK, (b + 1) * BLK), slice(first * BLK, first * BLK + depth)
+        for b, rows, cols in row_blocks(nb):
             mat = (row_hi[rows, cols], row_lo[rows, cols])
-            got = dot3(mat, (end_hi[cols, : 2 * BLK], end_lo[cols, : 2 * BLK]), MATMUL)
-            own[rows, :] = got.astype(BF16)
-            low = max(b * BLK, ROW0)
-            high = min((b + 1) * BLK, side - ROW0)
-            across[low - ROW0 : high - ROW0, :] = got[low - b * BLK : high - b * BLK, :].astype(BF16)
-            strips.append(packed3(mat, (end_hi[cols, 2 * BLK :], end_lo[cols, 2 * BLK :])))
+            got = dot3(mat, (end_hi[cols, BLK:], end_lo[cols, BLK:]), MATMUL)
+            own[rows, BLK:] = got[:, :BLK].astype(BF16)
+            start, stop = max(b * BLK, ROW0), min((b + 1) * BLK, side - ROW0)
+            across[start - ROW0 : stop - ROW0, BLK:] = (
+                got[start - b * BLK : stop - b * BLK, :BLK].astype(BF16)
+            )
+            strips.append(got[:, BLK:])
         strip = jnp.concatenate(strips, axis=0)
         strip = jnp.concatenate(
             [
@@ -535,17 +561,21 @@
     )(frame, meta, meta_up, meta_down, mid_hi, mid_lo, own_mid)
     mid = moved(mid, (1, 0, 0), (0,))
     tip_hi, tip_lo, edge_hi, edge_lo, out_hi, out_lo = parts
+    tip_row = (tip_hi, tip_lo, row_hi, row_lo, edge_hi, edge_lo)
+    lows = call(
+        functools.partial(left_kernel, nb), "left",
+        (shape((side, BLK), BF16), shape((kept, BLK), BF16)) + (shape((side, BLK), BF16),) * 2,
+        [VM] * 7,
+        flops=1 << 33,
+    )(left, *tip_row)
     own_end, end, to_up, to_down = call(
         functools.partial(edge_kernel, nb, ny), "edges",
         (shape((side, 2 * BLK), BF16), shape((kept + 128, side // 2), BF16))
         + (shape((BLK + 8, side), BF16),) * 2,
-        [VM] * 12,
+        [VM] * 16,
         [pltpu.VMEM((side, 3 * BLK), BF16)] * 2,
         flops=1 << 33,
-    )(
-        left, right, early_up, early_down, tip_hi, tip_lo, row_hi, row_lo, edge_hi, edge_lo,
-        out_hi, out_lo,
-    )
+    )(left, right, early_up, early_down, *tip_row, out_hi, out_lo, *lows)
     end = moved(end, (1, 0, 0), (0,))
     side_down = moved(to_up, (1, -1, 0), (0,))
     side_up = moved(to_down, (1, 1, 0), (0,))

time: 32.9 us -> 32.7 us (level)
  waiting for transfers between devices: 6.92 us -> 6.31 us
  Pallas kernels: 6.61 us -> 6.96 us
    ppermute x10, waiting for transfers between devices: 6.92 us -> 6.31 us  [moved(): return lax.ppermute(block, axes, route)]
    pallas_call x0 -> x1, Pallas kernels: none -> 0.59 us  [local(): call(functools.partial(left_kernel, nb), 'left', (shape((side, BLK), BF16...]
  transfers between devices with their start and end apart: 10 -> 10, of which waited for: 3 -> 3; matrix products, arithmetic and copies ran while one was open for 0% -> 0% of each run, Pallas kernels for 11% -> 12%
where the time goes in v9:
time: 32.7 us; the launch traced here: 32.4 us
  starting transfers between devices  18.9 us (58%)
  Pallas kernels  6.96 us (21%)
  waiting for transfers between devices  6.31 us (19%)
    ppermute x10, starting transfers between devices, moved(): return lax.ppermute(block, axes, route)  18.9 us
    ppermute x10, waiting for transfers between devices, moved(): return lax.ppermute(block, axes, route)  6.31 us
    pallas_call x1, Pallas kernels, local(): pl.pallas_call(functools.partial(gather_kernel, nb), out_shape=(shape((to...  1.96 us
    pallas_call x1, Pallas kernels, local(): call(functools.partial(center_kernel, nb), 'center', (shape((side, inner)...  1.46 us
    pallas_call x1, Pallas kernels, local(): call(functools.partial(edge_kernel, nb, ny), 'edges', (shape((side, 2 * B...  1.18 us
    pallas_call x1, Pallas kernels, local(): pl.pallas_call(functools.partial(finish_kernel, nb, nu), out_shape=shape(...  1.05 us
    pallas_call x1, Pallas kernels, local(): call(functools.partial(outer_kernel, nb, nx), 'outer', (shape((BLK, inner...  0.67 us
  transfers between devices with their start and end apart: 10, of which 3 were waited for; matrix products, arithmetic and copies ran while one was open for 0% of the time, Pallas kernels for 12%

profile of v9, /device:TPU:1, one launch (start us, length us, event | category | flops | bytes accessed | tf_op | source)
XLA Modules:
  0.0 32.4 jit_solution(10213350607968421903)
XLA Ops:
  0.0 2.0 %gather.1 = (f32[48,128]{1,0:T(8,128)}, f32[32768,128]{1,0:T(8,128)}, f32[8,128]{1,0:T(8,128)}, f32[520,128]{1,0:T(8,128)}, f32[520,128]{1,0:T(8,128)}) custom-call(f32[512,512]{1,0:T(8,128)} %bitcast.4, f32[4,128]{1,0:T(4,128)} %bitcast.8, f32[4,128]{1,0:T(4,128)} %bitcast.9, s32[4]{0:T(128)} %row_shift.1, s32[4]{0:T(128)} %col_shift.1, f32[16,32]{1,0:T(8,128)} %table.1, ...), custom_call_target="tpu_custom_call" | custom-call | tf_op jit(solution)/shard_map/gather/pallas_call | solution.py:520
  2.0 0.0 copy-start
  2.0 0.0 copy-start.1
  2.0 1.4 %collective-permute-start.3 = (f32[8,128]{1,0:T(8,128)}, f32[8,128]{1,0:T(8,128)S(1)}, u32[]{:S(2)}, u32[]{:S(2)}) collective-permute-start(f32[8,128]{1,0:T(8,128)} %get-tuple-element.41), channel_id=1, source_target_pairs={{20,0},{21,1},{22,2},{23,3},{24,4},{25,5},{26,6},{27,7},{28,8},{29... | collective-permute-start | bytes 12296 | tf_op jit(solution)/shard_map/ppermute | solution.py:35
  3.4 0.7 %collective-permute-start.2 = (f32[8,128]{1,0:T(8,128)}, f32[8,128]{1,0:T(8,128)S(1)}, u32[]{:S(2)}, u32[]{:S(2)}) collective-permute-start(f32[8,128]{1,0:T(8,128)} %get-tuple-element.41), channel_id=1, source_target_pairs={{16,4},{17,5},{18,6},{19,7},{20,8},{21,9},{22,10},{23,11},{24,12},... | collective-permute-start | bytes 12296 | tf_op jit(solution)/shard_map/ppermute | solution.py:35
  4.1 4.5 %collective-permute-start = (f32[520,128]{1,0:T(8,128)}, f32[520,128]{1,0:T(8,128)S(1)}, u32[]{:S(2)}, u32[]{:S(2)}) collective-permute-start(f32[520,128]{1,0:T(8,128)} %get-tuple-element.39), channel_id=1, source_target_pairs={{0,1},{1,2},{2,3},{4,5},{5,6},{6,7},{8,9},{9,10},{10,11},{12,13},{... | collective-permute-start | bytes 798728 | tf_op jit(solution)/shard_map/ppermute | solution.py:35
  8.6 1.9 %collective-permute-start.1 = (f32[520,128]{1,0:T(8,128)}, f32[520,128]{1,0:T(8,128)S(1)}, u32[]{:S(2)}, u32[]{:S(2)}) collective-permute-start(f32[520,128]{1,0:T(8,128)} %get-tuple-element.40), channel_id=1, source_target_pairs={{1,0},{2,1},{3,2},{5,4},{6,5},{7,6},{9,8},{10,9},{11,10},{13,12},{... | collective-permute-start | bytes 798728 | tf_op jit(solution)/shard_map/ppermute | solution.py:35
  10.6 0.0 copy-done
  10.6 0.0 copy-done.1
  10.6 1.5 %center.1 = (bf16[512,256]{1,0:T(8,128)(2,1)S(1)}, bf16[400,256]{1,0:T(8,128)(2,1)S(1)}, bf16[512,256]{1,0:T(8,128)(2,1)S(1)}, bf16[512,256]{1,0:T(8,128)(2,1)S(...) custom-call(f32[512,512]{1,0:T(8,128)S(1)} %bitcast.5, f32[48,128]{1,0:T(8,128)S(1)} %copy-done.1, ...), custom_call_target="tpu_custom_call" | custom-call | flops 8589934592 | bytes 17179868 | tf_op jit(solution)/shard_map/center/pallas_call | solution.py:544
  12.1 1.3 %collective-permute-start.6 = (bf16[400,256]{1,0:T(8,128)(2,1)S(1)}, bf16[400,256]{1,0:T(8,128)(2,1)S(1)}, u32[]{:S(2)}, u32[]{:S(2)}) collective-permute-start(bf16[400,256]{1,0:T(8,128)(2,1)S(1)} %get-tuple-element.61), channel_id=1, source_target_pairs={{0,16},{1,17},{2,18},{3,19},{4,20},{5,21},{6,22},{7,23},{8,24},{9,... | collective-permute-start | bytes 614408 | tf_op jit(solution)/shard_map/ppermute | solution.py:35
  13.4 0.0 collective-permute-done.3.meta_down
  13.4 0.0 collective-permute-done.2.meta_up
  13.4 0.7 %outer.1 = (bf16[128,256]{1,0:T(8,128)(2,1)S(1)}, bf16[128,256]{1,0:T(8,128)(2,1)S(1)}, bf16[512,256]{1,0:T(8,128)(2,1)S(1)}, bf16[512,256]{1,0:T(8,128)(2,1)S(1...) custom-call(f32[512,512]{1,0:T(8,128)S(1)} %bitcast.6, ...), custom_call_target="tpu_custom_call" | custom-call | flops 8589934592 | bytes 17179868 | tf_op jit(solution)/shard_map/outer/pallas_call | solution.py:553
  14.1 0.0 collective-permute-done.left
  14.1 0.6 %left.1 = (bf16[512,128]{1,0:T(8,128)(2,1)S(1)}, bf16[400,128]{1,0:T(8,128)(2,1)S(1)}, bf16[512,128]{1,0:T(8,128)(2,1)S(1)}, bf16[512,128]{1,0:T(8,128)(2,1)S(1)}) custom-call(f32[520,128]{1,0:T(8,128)S(1)} %collective-permute-done.left, bf16[512,256]{1,0:T(8,128)(2,1)S(1)} %get-tuple-element.46.tip_hi, bf16[512,256]{1,0:T(8,128)(2,1)S(1)} %get-tuple-element.47.tip_lo, ...), custom_call_target="tpu_custom_call" | custom-call | flops 8589934592 | bytes 17179868 | tf_op jit(solution)/shard_map/left/pallas_call | solution.py:565
  14.7 1.9 %collective-permute-done.1.right = f32[520,128]{1,0:T(8,128)S(1)} collective-permute-done((f32[520,128]{1,0:T(8,128)}, f32[520,128]{1,0:T(8,128)S(1)}, u32[]{:S(2)}, u32[]{:S(2)}) %collective-permute-start.1) | collective-permute-done | bytes 266272 | tf_op jit(solution)/shard_map/ppermute | solution.py:35
  16.6 1.2 %edges.1 = (bf16[512,256]{1,0:T(8,128)(2,1)S(1)}, bf16[528,256]{1,0:T(8,128)(2,1)S(1)}, bf16[136,512]{1,0:T(8,128)(2,1)S(1)}, bf16[136,512]{1,0:T(8,128)(2,1)S(1)}) custom-call(f32[520,128]{1,0:T(8,128)S(1)} %collective-permute-done.left, f32[520,128]{1,0:T(8,128)S(1)} %collective-permute-done.1.right, bf16[128,256]{1,0:T(8,128)(2,1)S(1)} %get-tuple-element.44.early_up, ...), custom_call_target="tpu_custom_call" | custom-call | flops 8589934592 | bytes 17179868 | tf_op jit(solution)/shard_map/edges/pallas_call | solution.py:571
  17.8 1.3 %collective-permute-start.7 = (bf16[528,256]{1,0:T(8,128)(2,1)S(1)}, bf16[528,256]{1,0:T(8,128)(2,1)S(1)}, u32[]{:S(2)}, u32[]{:S(2)}) collective-permute-start(bf16[528,256]{1,0:T(8,128)(2,1)S(1)} %get-tuple-element.62), channel_id=1, source_target_pairs={{0,16},{1,17},{2,18},{3,19},{4,20},{5,21},{6,22},{7,23},{8,24},{9,... | collective-permute-start | bytes 811016 | tf_op jit(solution)/shard_map/ppermute | solution.py:35
  19.1 1.3 %collective-permute-start.4 = (bf16[136,512]{1,0:T(8,128)(2,1)S(1)}, bf16[136,512]{1,0:T(8,128)(2,1)S(1)}, u32[]{:S(2)}, u32[]{:S(2)}) collective-permute-start(bf16[136,512]{1,0:T(8,128)(2,1)S(1)} %get-tuple-element.59.down_in), channel_id=1, source_target_pairs={{0,20},{1,21},{2,22},{3,23},{4,24},{5,25},{6,26},{7,27},{8,28},{9,... | collective-permute-start | bytes 417800 | tf_op jit(solution)/shard_map/ppermute | solution.py:35
  20.4 0.7 %collective-permute-start.5 = (bf16[136,512]{1,0:T(8,128)(2,1)S(1)}, bf16[136,512]{1,0:T(8,128)(2,1)S(1)}, u32[]{:S(2)}, u32[]{:S(2)}) collective-permute-start(bf16[136,512]{1,0:T(8,128)(2,1)S(1)} %get-tuple-element.60.up_in), channel_id=1, source_target_pairs={{4,16},{5,17},{6,18},{7,19},{8,20},{9,21},{10,22},{11,23},{12,24},... | collective-permute-start | bytes 417800 | tf_op jit(solution)/shard_map/ppermute | solution.py:35
  21.1 4.5 %collective-permute-start.8 = (bf16[128,512]{1,0:T(8,128)(2,1)S(1)}, bf16[128,512]{1,0:T(8,128)(2,1)S(1)}, u32[]{:S(2)}, u32[]{:S(2)}) collective-permute-start(bf16[128,512]{1,0:T(8,128)(2,1)S(1)} %get-tuple-element.65), channel_id=1, source_target_pairs={{0,4},{1,5},{2,6},{3,7},{4,8},{5,9},{6,10},{7,11},{8,12},{9,13},{1... | collective-permute-start | bytes 393224 | tf_op jit(solution)/shard_map/ppermute | solution.py:35
  25.6 0.0 collective-permute-done.6.mid
  25.6 1.3 %collective-permute-start.9 = (bf16[128,512]{1,0:T(8,128)(2,1)S(1)}, bf16[128,512]{1,0:T(8,128)(2,1)S(1)}, u32[]{:S(2)}, u32[]{:S(2)}) collective-permute-start(bf16[128,512]{1,0:T(8,128)(2,1)S(1)} %get-tuple-element.66), channel_id=1, source_target_pairs={{4,0},{5,1},{6,2},{7,3},{8,4},{9,5},{10,6},{11,7},{12,8},{13,9},{1... | collective-permute-start | bytes 393224 | tf_op jit(solution)/shard_map/ppermute | solution.py:35
  26.9 0.6 %collective-permute-done.8.got_up = bf16[128,512]{1,0:T(8,128)(2,1)S(1)} collective-permute-done((bf16[128,512]{1,0:T(8,128)(2,1)S(1)}, bf16[128,512]{1,0:T(8,128)(2,1)S(1)}, u32[]{:S(2)}, u32[]{:S(2)}) %collective-permute-start.8) | collective-permute-done | bytes 131104 | tf_op jit(solution)/shard_map/ppermute | solution.py:35
  27.5 3.8 %collective-permute-done.9.got_down = bf16[128,512]{1,0:T(8,128)(2,1)S(1)} collective-permute-done((bf16[128,512]{1,0:T(8,128)(2,1)S(1)}, bf16[128,512]{1,0:T(8,128)(2,1)S(1)}, u32[]{:S(2)}, u32[]{:S(2)}) %collective-permute-start.9) | collective-permute-done | bytes 131104 | tf_op jit(solution)/shard_map/ppermute | solution.py:35
  31.3 0.0 collective-permute-done.4.side_up
  31.3 0.0 collective-permute-done.5.side_down
  31.3 0.0 collective-permute-done.7.end
  31.3 1.1 %finish.1 = f32[512,512]{1,0:T(8,128)} custom-call(f32[512,512]{1,0:T(8,128)S(1)} %bitcast.7, bf16[512,256]{1,0:T(8,128)(2,1)S(1)} %get-tuple-element.38.after.own_mid, bf16[512,256]{1,0:T(8,128)(2,1)S(1)} %get-tuple-element.58.after.end_in.own_end, bf16[136,512]{1,0:T(8,128)(2,1)S(1)} %collective-permute-done.4.side_up, ...), custom_call_target="tpu_custom_call" | custom-call | tf_op jit(solution)/shard_map/finish/pallas_call | solution.py:594
  (3 shorter events, 0.0 us)
Async XLA Ops:
  2.0 8.6 %copy-start = (f32[1,512,512]{2,1,0:T(8,128)S(1)}, f32[1,512,512]{2,1,0:T(8,128)}, u32[]{:S(2)}) copy-start(f32[1,512,512]{2,1,0:T(8,128)} %param.9) | copy-start | bytes 3145732
  2.0 8.6 %copy-start.1 = (f32[48,128]{1,0:T(8,128)S(1)}, f32[48,128]{1,0:T(8,128)}, u32[]{:S(2)}) copy-start(f32[48,128]{1,0:T(8,128)} %get-tuple-element.36.meta) | copy-start | bytes 73732
  2.0 11.4 %collective-permute-start.3 = (f32[8,128]{1,0:T(8,128)}, f32[8,128]{1,0:T(8,128)S(1)}, u32[]{:S(2)}, u32[]{:S(2)}) collective-permute-start(f32[8,128]{1,0:T(8,128)} %get-tuple-element.41), channel_id=1, source_target_pairs={{20,0},{21,1},{22,2},{23,3},{24,4},{25,5},{26,6},{27,7},{28,8},{29... | collective-permute-start | bytes 12296 | tf_op jit(solution)/shard_map/ppermute | solution.py:35
  3.4 10.0 %collective-permute-start.2 = (f32[8,128]{1,0:T(8,128)}, f32[8,128]{1,0:T(8,128)S(1)}, u32[]{:S(2)}, u32[]{:S(2)}) collective-permute-start(f32[8,128]{1,0:T(8,128)} %get-tuple-element.41), channel_id=1, source_target_pairs={{16,4},{17,5},{18,6},{19,7},{20,8},{21,9},{22,10},{23,11},{24,12},... | collective-permute-start | bytes 12296 | tf_op jit(solution)/shard_map/ppermute | solution.py:35
  4.1 10.0 %collective-permute-start = (f32[520,128]{1,0:T(8,128)}, f32[520,128]{1,0:T(8,128)S(1)}, u32[]{:S(2)}, u32[]{:S(2)}) collective-permute-start(f32[520,128]{1,0:T(8,128)} %get-tuple-element.39), channel_id=1, source_target_pairs={{0,1},{1,2},{2,3},{4,5},{5,6},{6,7},{8,9},{9,10},{10,11},{12,13},{... | collective-permute-start | bytes 798728 | tf_op jit(solution)/shard_map/ppermute | solution.py:35
  8.6 7.9 %collective-permute-start.1 = (f32[520,128]{1,0:T(8,128)}, f32[520,128]{1,0:T(8,128)S(1)}, u32[]{:S(2)}, u32[]{:S(2)}) collective-permute-start(f32[520,128]{1,0:T(8,128)} %get-tuple-element.40), channel_id=1, source_target_pairs={{1,0},{2,1},{3,2},{5,4},{6,5},{7,6},{9,8},{10,9},{11,10},{13,12},{... | collective-permute-start | bytes 798728 | tf_op jit(solution)/shard_map/ppermute | solution.py:35
  12.1 13.5 %collective-permute-start.6 = (bf16[400,256]{1,0:T(8,128)(2,1)S(1)}, bf16[400,256]{1,0:T(8,128)(2,1)S(1)}, u32[]{:S(2)}, u32[]{:S(2)}) collective-permute-start(bf16[400,256]{1,0:T(8,128)(2,1)S(1)} %get-tuple-element.61), channel_id=1, source_target_pairs={{0,16},{1,17},{2,18},{3,19},{4,20},{5,21},{6,22},{7,23},{8,24},{9,... | collective-permute-start | bytes 614408 | tf_op jit(solution)/shard_map/ppermute | solution.py:35
  17.8 13.5 %collective-permute-start.7 = (bf16[528,256]{1,0:T(8,128)(2,1)S(1)}, bf16[528,256]{1,0:T(8,128)(2,1)S(1)}, u32[]{:S(2)}, u32[]{:S(2)}) collective-permute-start(bf16[528,256]{1,0:T(8,128)(2,1)S(1)} %get-tuple-element.62), channel_id=1, source_target_pairs={{0,16},{1,17},{2,18},{3,19},{4,20},{5,21},{6,22},{7,23},{8,24},{9,... | collective-permute-start | bytes 811016 | tf_op jit(solution)/shard_map/ppermute | solution.py:35
  19.1 12.2 %collective-permute-start.4 = (bf16[136,512]{1,0:T(8,128)(2,1)S(1)}, bf16[136,512]{1,0:T(8,128)(2,1)S(1)}, u32[]{:S(2)}, u32[]{:S(2)}) collective-permute-start(bf16[136,512]{1,0:T(8,128)(2,1)S(1)} %get-tuple-element.59.down_in), channel_id=1, source_target_pairs={{0,20},{1,21},{2,22},{3,23},{4,24},{5,25},{6,26},{7,27},{8,28},{9,... | collective-permute-start | bytes 417800 | tf_op jit(solution)/shard_map/ppermute | solution.py:35
  20.4 10.9 %collective-permute-start.5 = (bf16[136,512]{1,0:T(8,128)(2,1)S(1)}, bf16[136,512]{1,0:T(8,128)(2,1)S(1)}, u32[]{:S(2)}, u32[]{:S(2)}) collective-permute-start(bf16[136,512]{1,0:T(8,128)(2,1)S(1)} %get-tuple-element.60.up_in), channel_id=1, source_target_pairs={{4,16},{5,17},{6,18},{7,19},{8,20},{9,21},{10,22},{11,23},{12,24},... | collective-permute-start | bytes 417800 | tf_op jit(solution)/shard_map/ppermute | solution.py:35
  21.1 6.4 %collective-permute-start.8 = (bf16[128,512]{1,0:T(8,128)(2,1)S(1)}, bf16[128,512]{1,0:T(8,128)(2,1)S(1)}, u32[]{:S(2)}, u32[]{:S(2)}) collective-permute-start(bf16[128,512]{1,0:T(8,128)(2,1)S(1)} %get-tuple-element.65), channel_id=1, source_target_pairs={{0,4},{1,5},{2,6},{3,7},{4,8},{5,9},{6,10},{7,11},{8,12},{9,13},{1... | collective-permute-start | bytes 393224 | tf_op jit(solution)/shard_map/ppermute | solution.py:35
  25.6 5.7 %collective-permute-start.9 = (bf16[128,512]{1,0:T(8,128)(2,1)S(1)}, bf16[128,512]{1,0:T(8,128)(2,1)S(1)}, u32[]{:S(2)}, u32[]{:S(2)}) collective-permute-start(bf16[128,512]{1,0:T(8,128)(2,1)S(1)} %get-tuple-element.66), channel_id=1, source_target_pairs={{4,0},{5,1},{6,2},{7,3},{8,4},{9,5},{10,6},{11,7},{12,8},{13,9},{1... | collective-permute-start | bytes 393224 | tf_op jit(solution)/shard_map/ppermute | solution.py:35

commit v10 on v9

--- a/solution.py
+++ b/solution.py
@@ -270,11 +270,19 @@
         yield b, slice(b * BLK, (b + 1) * BLK), slice(first * BLK, first * BLK + depth)
 
 
-def left_kernel(nb, left, tip_hi, tip_lo, row_hi, row_lo, edge_hi, edge_lo, own, across, end_hi, end_lo):
+def left_kernel(
+    nb, left, tip_hi, tip_lo, row_hi, row_lo, edge_hi, edge_lo, own, across, end_hi, end_lo, halo
+):
     side = nb * BLK
+    j = lax.axis_index("skyy")
 
     @pl.when(lax.axis_index("segment") == 0)
     def _():
+        lanes = lax.broadcasted_iota(jnp.int32, (8, BLK), 1)
+        kept = jnp.logical_and(lanes >= BLK - HALF, j > 0)
+        weight = jnp.where(kept, taps([left[side : side + 1, :]])[0], 0.0)
+        mat = split(banded(weight, left[side + 1 : side + 2, :].astype(jnp.int32), BLK, BLK))
+        halo[...] = packed3((tip_hi[:, :BLK], tip_lo[:, :BLK]), mat)
         source = [
             jnp.concatenate([part, tip[:, :BLK]], axis=1)
             for part, tip in zip(split(left[:side, :]), (tip_hi, tip_lo))
@@ -292,7 +300,7 @@
 def edge_kernel(
     nb, ny,
     left, right, early_up, early_down, tip_hi, tip_lo, row_hi, row_lo, edge_hi, edge_lo, out_hi, out_lo,
-    own_low, low, low_hi, low_lo,
+    own_low, low, low_hi, low_lo, halo,
     own, across, side_up, side_down,
     end_hi, end_lo,
 ):
@@ -304,8 +312,8 @@
     @pl.when(lax.axis_index("segment") == 0)
     def _():
         lanes = lax.broadcasted_iota(jnp.int32, (8, BLK), 1)
-        weights = taps([left[side : side + 1, :], right[side : side + 1, :]])
-        shifts = [part[side + 1 : side + 2, :].astype(jnp.int32) for part in (left, right)]
+        weight = taps([right[side : side + 1, :]])[0]
+        shift = right[side + 1 : side + 2, :].astype(jnp.int32)
         source = [
             jnp.concatenate([tip[:, BLK:], part], axis=1)
             for part, tip in zip(split(right[:side, :]), (tip_hi, tip_lo))
@@ -317,12 +325,9 @@
             end[:, BLK : 2 * BLK] = part
         own[:, :BLK] = own_low[...]
         across[:kept, :BLK] = low[...]
-        low_ok = jnp.logical_and(lanes >= BLK - HALF, j > 0)
         high_ok = jnp.logical_and(lanes < HALF, j < ny - 1)
-        lower = split(banded(jnp.where(low_ok, weights[0], 0.0), shifts[0], BLK, BLK))
-        high = split(banded(jnp.where(high_ok, weights[1], 0.0), shifts[1], BLK, -BLK))
-        mat = [jnp.concatenate(pair, axis=0) for pair in zip(lower, high)]
-        hi, lo = split(packed3((tip_hi[...], tip_lo[...]), mat))
+        mat = split(banded(jnp.where(high_ok, weight, 0.0), shift, BLK, -BLK))
+        hi, lo = split(packed3((tip_hi[:, BLK:], tip_lo[:, BLK:]), mat) + halo[...])
         end_hi[:, 2 * BLK :] = hi
         end_lo[:, 2 * BLK :] = lo
         outer = []
@@ -564,7 +569,8 @@
     tip_row = (tip_hi, tip_lo, row_hi, row_lo, edge_hi, edge_lo)
     lows = call(
         functools.partial(left_kernel, nb), "left",
-        (shape((side, BLK), BF16), shape((kept, BLK), BF16)) + (shape((side, BLK), BF16),) * 2,
+        (shape((side, BLK), BF16), shape((kept, BLK), BF16)) + (shape((side, BLK), BF16),) * 2
+        + (shape((side, BLK), F32),),
         [VM] * 7,
         flops=1 << 33,
     )(left, *tip_row)
@@ -572,7 +578,7 @@
         functools.partial(edge_kernel, nb, ny), "edges",
         (shape((side, 2 * BLK), BF16), shape((kept + 128, side // 2), BF16))
         + (shape((BLK + 8, side), BF16),) * 2,
-        [VM] * 16,
+        [ANY] + [VM] * 16,
         [pltpu.VMEM((side, 3 * BLK), BF16)] * 2,
         flops=1 << 33,
     )(left, right, early_up, early_down, *tip_row, out_hi, out_lo, *lows)

time: 32.7 us -> 32.6 us (level)
  transfers between devices with their start and end apart: 10 -> 10, of which waited for: 3 -> 3; matrix products, arithmetic and copies ran while one was open for 0% -> 0% of each run, Pallas kernels for 12% -> 13%
where the time goes in v10:
time: 32.6 us; the launch traced here: 32.3 us
  starting transfers between devices  18.9 us (58%)
  Pallas kernels  7.13 us (22%)
  waiting for transfers between devices  6.11 us (19%)
    ppermute x10, starting transfers between devices, moved(): return lax.ppermute(block, axes, route)  18.9 us
    ppermute x10, waiting for transfers between devices, moved(): return lax.ppermute(block, axes, route)  6.11 us
    pallas_call x1, Pallas kernels, local(): pl.pallas_call(functools.partial(gather_kernel, nb), out_shape=(shape((to...  1.96 us
    pallas_call x1, Pallas kernels, local(): call(functools.partial(center_kernel, nb), 'center', (shape((side, inner)...  1.47 us
    pallas_call x1, Pallas kernels, local(): call(functools.partial(edge_kernel, nb, ny), 'edges', (shape((side, 2 * B...  1.14 us
    pallas_call x1, Pallas kernels, local(): pl.pallas_call(functools.partial(finish_kernel, nb, nu), out_shape=shape(...  1.05 us
    pallas_call x1, Pallas kernels, local(): call(functools.partial(left_kernel, nb), 'left', (shape((side, BLK), BF16...  0.78 us
    pallas_call x1, Pallas kernels, local(): call(functools.partial(outer_kernel, nb, nx), 'outer', (shape((BLK, inner...  0.67 us
  transfers between devices with their start and end apart: 10, of which 3 were waited for; matrix products, arithmetic and copies ran while one was open for 0% of the time, Pallas kernels for 13%

profile of v10, /device:TPU:1, one launch (start us, length us, event | category | flops | bytes accessed | tf_op | source)
XLA Modules:
  0.0 32.3 jit_solution(9509799646074169459)
XLA Ops:
  0.0 2.0 %gather.1 = (f32[48,128]{1,0:T(8,128)}, f32[32768,128]{1,0:T(8,128)}, f32[8,128]{1,0:T(8,128)}, f32[520,128]{1,0:T(8,128)}, f32[520,128]{1,0:T(8,128)}) custom-call(f32[512,512]{1,0:T(8,128)} %bitcast.4, f32[4,128]{1,0:T(4,128)} %bitcast.8, f32[4,128]{1,0:T(4,128)} %bitcast.9, s32[4]{0:T(128)} %row_shift.1, s32[4]{0:T(128)} %col_shift.1, f32[16,32]{1,0:T(8,128)} %table.1, ...), custom_call_target="tpu_custom_call" | custom-call | tf_op jit(solution)/shard_map/gather/pallas_call | solution.py:525
  2.0 0.0 copy-start
  2.0 0.0 copy-start.1
  2.0 1.4 %collective-permute-start.3 = (f32[8,128]{1,0:T(8,128)}, f32[8,128]{1,0:T(8,128)S(1)}, u32[]{:S(2)}, u32[]{:S(2)}) collective-permute-start(f32[8,128]{1,0:T(8,128)} %get-tuple-element.42), channel_id=1, source_target_pairs={{20,0},{21,1},{22,2},{23,3},{24,4},{25,5},{26,6},{27,7},{28,8},{29... | collective-permute-start | bytes 12296 | tf_op jit(solution)/shard_map/ppermute | solution.py:35
  3.4 0.7 %collective-permute-start.2 = (f32[8,128]{1,0:T(8,128)}, f32[8,128]{1,0:T(8,128)S(1)}, u32[]{:S(2)}, u32[]{:S(2)}) collective-permute-start(f32[8,128]{1,0:T(8,128)} %get-tuple-element.42), channel_id=1, source_target_pairs={{16,4},{17,5},{18,6},{19,7},{20,8},{21,9},{22,10},{23,11},{24,12},... | collective-permute-start | bytes 12296 | tf_op jit(solution)/shard_map/ppermute | solution.py:35
  4.1 4.5 %collective-permute-start = (f32[520,128]{1,0:T(8,128)}, f32[520,128]{1,0:T(8,128)S(1)}, u32[]{:S(2)}, u32[]{:S(2)}) collective-permute-start(f32[520,128]{1,0:T(8,128)} %get-tuple-element.40), channel_id=1, source_target_pairs={{0,1},{1,2},{2,3},{4,5},{5,6},{6,7},{8,9},{9,10},{10,11},{12,13},{... | collective-permute-start | bytes 798728 | tf_op jit(solution)/shard_map/ppermute | solution.py:35
  8.6 1.9 %collective-permute-start.1 = (f32[520,128]{1,0:T(8,128)}, f32[520,128]{1,0:T(8,128)S(1)}, u32[]{:S(2)}, u32[]{:S(2)}) collective-permute-start(f32[520,128]{1,0:T(8,128)} %get-tuple-element.41), channel_id=1, source_target_pairs={{1,0},{2,1},{3,2},{5,4},{6,5},{7,6},{9,8},{10,9},{11,10},{13,12},{... | collective-permute-start | bytes 798728 | tf_op jit(solution)/shard_map/ppermute | solution.py:35
  10.6 0.0 copy-done
  10.6 0.0 copy-done.1
  10.6 1.5 %center.1 = (bf16[512,256]{1,0:T(8,128)(2,1)S(1)}, bf16[400,256]{1,0:T(8,128)(2,1)S(1)}, bf16[512,256]{1,0:T(8,128)(2,1)S(1)}, bf16[512,256]{1,0:T(8,128)(2,1)S(...) custom-call(f32[512,512]{1,0:T(8,128)S(1)} %bitcast.5, f32[48,128]{1,0:T(8,128)S(1)} %copy-done.1, ...), custom_call_target="tpu_custom_call" | custom-call | flops 8589934592 | bytes 17179868 | tf_op jit(solution)/shard_map/center/pallas_call | solution.py:549
  12.1 1.3 %collective-permute-start.6 = (bf16[400,256]{1,0:T(8,128)(2,1)S(1)}, bf16[400,256]{1,0:T(8,128)(2,1)S(1)}, u32[]{:S(2)}, u32[]{:S(2)}) collective-permute-start(bf16[400,256]{1,0:T(8,128)(2,1)S(1)} %get-tuple-element.63), channel_id=1, source_target_pairs={{0,16},{1,17},{2,18},{3,19},{4,20},{5,21},{6,22},{7,23},{8,24},{9,... | collective-permute-start | bytes 614408 | tf_op jit(solution)/shard_map/ppermute | solution.py:35
  13.4 0.0 collective-permute-done.3.meta_down
  13.4 0.0 collective-permute-done.2.meta_up
  13.4 0.7 %outer.1 = (bf16[128,256]{1,0:T(8,128)(2,1)S(1)}, bf16[128,256]{1,0:T(8,128)(2,1)S(1)}, bf16[512,256]{1,0:T(8,128)(2,1)S(1)}, bf16[512,256]{1,0:T(8,128)(2,1)S(1...) custom-call(f32[512,512]{1,0:T(8,128)S(1)} %bitcast.6, ...), custom_call_target="tpu_custom_call" | custom-call | flops 8589934592 | bytes 17179868 | tf_op jit(solution)/shard_map/outer/pallas_call | solution.py:558
  14.1 0.0 collective-permute-done.left
  14.1 0.8 %left.1 = (bf16[512,128]{1,0:T(8,128)(2,1)S(1)}, bf16[400,128]{1,0:T(8,128)(2,1)S(1)}, bf16[512,128]{1,0:T(8,128)(2,1)S(1)}, bf16[512,128]{1,0:T(8,128)(2,1)S(1)}, f32[512,128]{1,0:T(8,128)S(1)}) custom-call(f32[520,128]{1,0:T(8,128)S(1)} %collective-permute-done.left, bf16[512,256]{1,0:T(8,128)(2,1)S(1)} %get-tuple-element.47.tip_hi, ...), custom_call_target="tpu_custom_call" | custom-call | flops 8589934592 | bytes 17179868 | tf_op jit(solution)/shard_map/left/pallas_call | solution.py:570
  14.9 1.7 %collective-permute-done.1.right = f32[520,128]{1,0:T(8,128)S(1)} collective-permute-done((f32[520,128]{1,0:T(8,128)}, f32[520,128]{1,0:T(8,128)S(1)}, u32[]{:S(2)}, u32[]{:S(2)}) %collective-permute-start.1) | collective-permute-done | bytes 266272 | tf_op jit(solution)/shard_map/ppermute | solution.py:35
  16.6 1.1 %edges.1 = (bf16[512,256]{1,0:T(8,128)(2,1)S(1)}, bf16[528,256]{1,0:T(8,128)(2,1)S(1)}, bf16[136,512]{1,0:T(8,128)(2,1)S(1)}, bf16[136,512]{1,0:T(8,128)(2,1)S(1)}) custom-call(f32[520,128]{1,0:T(8,128)S(1)} %collective-permute-done.left, f32[520,128]{1,0:T(8,128)S(1)} %collective-permute-done.1.right, bf16[128,256]{1,0:T(8,128)(2,1)S(1)} %get-tuple-element.45.early_up, ...), custom_call_target="tpu_custom_call" | custom-call | flops 8589934592 | bytes 17179868 | tf_op jit(solution)/shard_map/edges/pallas_call | solution.py:577
  17.7 1.3 %collective-permute-start.7 = (bf16[528,256]{1,0:T(8,128)(2,1)S(1)}, bf16[528,256]{1,0:T(8,128)(2,1)S(1)}, u32[]{:S(2)}, u32[]{:S(2)}) collective-permute-start(bf16[528,256]{1,0:T(8,128)(2,1)S(1)} %get-tuple-element.64), channel_id=1, source_target_pairs={{0,16},{1,17},{2,18},{3,19},{4,20},{5,21},{6,22},{7,23},{8,24},{9,... | collective-permute-start | bytes 811016 | tf_op jit(solution)/shard_map/ppermute | solution.py:35
  19.1 1.3 %collective-permute-start.4 = (bf16[136,512]{1,0:T(8,128)(2,1)S(1)}, bf16[136,512]{1,0:T(8,128)(2,1)S(1)}, u32[]{:S(2)}, u32[]{:S(2)}) collective-permute-start(bf16[136,512]{1,0:T(8,128)(2,1)S(1)} %get-tuple-element.61.down_in), channel_id=1, source_target_pairs={{0,20},{1,21},{2,22},{3,23},{4,24},{5,25},{6,26},{7,27},{8,28},{9,... | collective-permute-start | bytes 417800 | tf_op jit(solution)/shard_map/ppermute | solution.py:35
  20.4 0.7 %collective-permute-start.5 = (bf16[136,512]{1,0:T(8,128)(2,1)S(1)}, bf16[136,512]{1,0:T(8,128)(2,1)S(1)}, u32[]{:S(2)}, u32[]{:S(2)}) collective-permute-start(bf16[136,512]{1,0:T(8,128)(2,1)S(1)} %get-tuple-element.62.up_in), channel_id=1, source_target_pairs={{4,16},{5,17},{6,18},{7,19},{8,20},{9,21},{10,22},{11,23},{12,24},... | collective-permute-start | bytes 417800 | tf_op jit(solution)/shard_map/ppermute | solution.py:35
  21.1 4.5 %collective-permute-start.8 = (bf16[128,512]{1,0:T(8,128)(2,1)S(1)}, bf16[128,512]{1,0:T(8,128)(2,1)S(1)}, u32[]{:S(2)}, u32[]{:S(2)}) collective-permute-start(bf16[128,512]{1,0:T(8,128)(2,1)S(1)} %get-tuple-element.67), channel_id=1, source_target_pairs={{0,4},{1,5},{2,6},{3,7},{4,8},{5,9},{6,10},{7,11},{8,12},{9,13},{1... | collective-permute-start | bytes 393224 | tf_op jit(solution)/shard_map/ppermute | solution.py:35
  25.5 0.0 collective-permute-done.6.mid
  25.6 1.3 %collective-permute-start.9 = (bf16[128,512]{1,0:T(8,128)(2,1)S(1)}, bf16[128,512]{1,0:T(8,128)(2,1)S(1)}, u32[]{:S(2)}, u32[]{:S(2)}) collective-permute-start(bf16[128,512]{1,0:T(8,128)(2,1)S(1)} %get-tuple-element.68), channel_id=1, source_target_pairs={{4,0},{5,1},{6,2},{7,3},{8,4},{9,5},{10,6},{11,7},{12,8},{13,9},{1... | collective-permute-start | bytes 393224 | tf_op jit(solution)/shard_map/ppermute | solution.py:35
  26.9 0.6 %collective-permute-done.8.got_up = bf16[128,512]{1,0:T(8,128)(2,1)S(1)} collective-permute-done((bf16[128,512]{1,0:T(8,128)(2,1)S(1)}, bf16[128,512]{1,0:T(8,128)(2,1)S(1)}, u32[]{:S(2)}, u32[]{:S(2)}) %collective-permute-start.8) | collective-permute-done | bytes 131104 | tf_op jit(solution)/shard_map/ppermute | solution.py:35
  27.5 3.8 %collective-permute-done.9.got_down = bf16[128,512]{1,0:T(8,128)(2,1)S(1)} collective-permute-done((bf16[128,512]{1,0:T(8,128)(2,1)S(1)}, bf16[128,512]{1,0:T(8,128)(2,1)S(1)}, u32[]{:S(2)}, u32[]{:S(2)}) %collective-permute-start.9) | collective-permute-done | bytes 131104 | tf_op jit(solution)/shard_map/ppermute | solution.py:35
  31.3 0.0 collective-permute-done.4.side_up
  31.3 0.0 collective-permute-done.5.side_down
  31.3 0.0 collective-permute-done.7.end
  31.3 1.1 %finish.1 = f32[512,512]{1,0:T(8,128)} custom-call(f32[512,512]{1,0:T(8,128)S(1)} %bitcast.7, bf16[512,256]{1,0:T(8,128)(2,1)S(1)} %get-tuple-element.39.after.own_mid, bf16[512,256]{1,0:T(8,128)(2,1)S(1)} %get-tuple-element.60.after.end_in.own_end, bf16[136,512]{1,0:T(8,128)(2,1)S(1)} %collective-permute-done.4.side_up, ...), custom_call_target="tpu_custom_call" | custom-call | tf_op jit(solution)/shard_map/finish/pallas_call | solution.py:600
  (3 shorter events, 0.0 us)
Async XLA Ops:
  2.0 8.6 %copy-start = (f32[1,512,512]{2,1,0:T(8,128)S(1)}, f32[1,512,512]{2,1,0:T(8,128)}, u32[]{:S(2)}) copy-start(f32[1,512,512]{2,1,0:T(8,128)} %param.9) | copy-start | bytes 3145732
  2.0 8.6 %copy-start.1 = (f32[48,128]{1,0:T(8,128)S(1)}, f32[48,128]{1,0:T(8,128)}, u32[]{:S(2)}) copy-start(f32[48,128]{1,0:T(8,128)} %get-tuple-element.37.meta) | copy-start | bytes 73732
  2.0 11.4 %collective-permute-start.3 = (f32[8,128]{1,0:T(8,128)}, f32[8,128]{1,0:T(8,128)S(1)}, u32[]{:S(2)}, u32[]{:S(2)}) collective-permute-start(f32[8,128]{1,0:T(8,128)} %get-tuple-element.42), channel_id=1, source_target_pairs={{20,0},{21,1},{22,2},{23,3},{24,4},{25,5},{26,6},{27,7},{28,8},{29... | collective-permute-start | bytes 12296 | tf_op jit(solution)/shard_map/ppermute | solution.py:35
  3.4 10.0 %collective-permute-start.2 = (f32[8,128]{1,0:T(8,128)}, f32[8,128]{1,0:T(8,128)S(1)}, u32[]{:S(2)}, u32[]{:S(2)}) collective-permute-start(f32[8,128]{1,0:T(8,128)} %get-tuple-element.42), channel_id=1, source_target_pairs={{16,4},{17,5},{18,6},{19,7},{20,8},{21,9},{22,10},{23,11},{24,12},... | collective-permute-start | bytes 12296 | tf_op jit(solution)/shard_map/ppermute | solution.py:35
  4.1 10.0 %collective-permute-start = (f32[520,128]{1,0:T(8,128)}, f32[520,128]{1,0:T(8,128)S(1)}, u32[]{:S(2)}, u32[]{:S(2)}) collective-permute-start(f32[520,128]{1,0:T(8,128)} %get-tuple-element.40), channel_id=1, source_target_pairs={{0,1},{1,2},{2,3},{4,5},{5,6},{6,7},{8,9},{9,10},{10,11},{12,13},{... | collective-permute-start | bytes 798728 | tf_op jit(solution)/shard_map/ppermute | solution.py:35
  8.6 7.9 %collective-permute-start.1 = (f32[520,128]{1,0:T(8,128)}, f32[520,128]{1,0:T(8,128)S(1)}, u32[]{:S(2)}, u32[]{:S(2)}) collective-permute-start(f32[520,128]{1,0:T(8,128)} %get-tuple-element.41), channel_id=1, source_target_pairs={{1,0},{2,1},{3,2},{5,4},{6,5},{7,6},{9,8},{10,9},{11,10},{13,12},{... | collective-permute-start | bytes 798728 | tf_op jit(solution)/shard_map/ppermute | solution.py:35
  12.1 13.5 %collective-permute-start.6 = (bf16[400,256]{1,0:T(8,128)(2,1)S(1)}, bf16[400,256]{1,0:T(8,128)(2,1)S(1)}, u32[]{:S(2)}, u32[]{:S(2)}) collective-permute-start(bf16[400,256]{1,0:T(8,128)(2,1)S(1)} %get-tuple-element.63), channel_id=1, source_target_pairs={{0,16},{1,17},{2,18},{3,19},{4,20},{5,21},{6,22},{7,23},{8,24},{9,... | collective-permute-start | bytes 614408 | tf_op jit(solution)/shard_map/ppermute | solution.py:35
  17.7 13.5 %collective-permute-start.7 = (bf16[528,256]{1,0:T(8,128)(2,1)S(1)}, bf16[528,256]{1,0:T(8,128)(2,1)S(1)}, u32[]{:S(2)}, u32[]{:S(2)}) collective-permute-start(bf16[528,256]{1,0:T(8,128)(2,1)S(1)} %get-tuple-element.64), channel_id=1, source_target_pairs={{0,16},{1,17},{2,18},{3,19},{4,20},{5,21},{6,22},{7,23},{8,24},{9,... | collective-permute-start | bytes 811016 | tf_op jit(solution)/shard_map/ppermute | solution.py:35
  19.1 12.2 %collective-permute-start.4 = (bf16[136,512]{1,0:T(8,128)(2,1)S(1)}, bf16[136,512]{1,0:T(8,128)(2,1)S(1)}, u32[]{:S(2)}, u32[]{:S(2)}) collective-permute-start(bf16[136,512]{1,0:T(8,128)(2,1)S(1)} %get-tuple-element.61.down_in), channel_id=1, source_target_pairs={{0,20},{1,21},{2,22},{3,23},{4,24},{5,25},{6,26},{7,27},{8,28},{9,... | collective-permute-start | bytes 417800 | tf_op jit(solution)/shard_map/ppermute | solution.py:35
  20.4 10.9 %collective-permute-start.5 = (bf16[136,512]{1,0:T(8,128)(2,1)S(1)}, bf16[136,512]{1,0:T(8,128)(2,1)S(1)}, u32[]{:S(2)}, u32[]{:S(2)}) collective-permute-start(bf16[136,512]{1,0:T(8,128)(2,1)S(1)} %get-tuple-element.62.up_in), channel_id=1, source_target_pairs={{4,16},{5,17},{6,18},{7,19},{8,20},{9,21},{10,22},{11,23},{12,24},... | collective-permute-start | bytes 417800 | tf_op jit(solution)/shard_map/ppermute | solution.py:35
  21.1 6.4 %collective-permute-start.8 = (bf16[128,512]{1,0:T(8,128)(2,1)S(1)}, bf16[128,512]{1,0:T(8,128)(2,1)S(1)}, u32[]{:S(2)}, u32[]{:S(2)}) collective-permute-start(bf16[128,512]{1,0:T(8,128)(2,1)S(1)} %get-tuple-element.67), channel_id=1, source_target_pairs={{0,4},{1,5},{2,6},{3,7},{4,8},{5,9},{6,10},{7,11},{8,12},{9,13},{1... | collective-permute-start | bytes 393224 | tf_op jit(solution)/shard_map/ppermute | solution.py:35
  25.6 5.7 %collective-permute-start.9 = (bf16[128,512]{1,0:T(8,128)(2,1)S(1)}, bf16[128,512]{1,0:T(8,128)(2,1)S(1)}, u32[]{:S(2)}, u32[]{:S(2)}) collective-permute-start(bf16[128,512]{1,0:T(8,128)(2,1)S(1)} %get-tuple-element.68), channel_id=1, source_target_pairs={{4,0},{5,1},{6,2},{7,3},{8,4},{9,5},{10,6},{11,7},{12,8},{13,9},{1... | collective-permute-start | bytes 393224 | tf_op jit(solution)/shard_map/ppermute | solution.py:35
